TPU v7x, 32 devices: a whole 2x2x4 slice. The times are simulated.
32 devices in a mesh: rep: 16 (over z, x, core), shard: 2 (over y).
Axes of the slice: x: 2, y: 2, z: 4, core: 2. Of those that a mesh axis runs over, the one named last changes fastest.
Arguments:
- clips: bfloat16 [64, 1568, 1536], P(('rep', 'shard')), may hold values from -6 to 6
- visible_idx: int32 [64, 157], P(('rep', 'shard')), may hold values from 0 to 1567, as said below
- masked_idx: int32 [64, 1411], P(('rep', 'shard')), may hold values from 0 to 1567
- loss_counts: int32 [64], P(('rep', 'shard')), may hold values from 705 to 1411, as said below
- enc_rows: float32 [768, 6528], P('shard'), may hold values from -0.21875 to 0.21875
- enc_cols: float32 [4608, 768], P('shard'), may hold values from -0.109375 to 0.109375
- dec_rows: float32 [384, 4608], P('shard'), may hold values from -0.3125 to 0.3125
- dec_fc2: float32 [1536, 384], P('shard'), may hold values from -0.15625 to 0.15625
- vectors: float32 [14592], P('shard'), may hold values from 0.25 to 1.75
- m_enc_rows: float32 [768, 6528], P('shard'), may hold values from -1.9073486e-06 to 1.9073486e-06
- m_enc_cols: float32 [4608, 768], P('shard'), may hold values from -1.9073486e-06 to 1.9073486e-06
- m_dec_rows: float32 [384, 4608], P('shard'), may hold values from -1.9073486e-06 to 1.9073486e-06
- m_dec_fc2: float32 [1536, 384], P('shard'), may hold values from -1.9073486e-06 to 1.9073486e-06
- m_vectors: float32 [14592], P('shard'), may hold values from -1.9073486e-06 to 1.9073486e-06
- v_enc_rows: float32 [768, 6528], P('shard'), may hold values from 2.0269753e-14 to 2.0269753e-13
- v_enc_cols: float32 [4608, 768], P('shard'), may hold values from 2.0269753e-14 to 2.0269753e-13
- v_dec_rows: float32 [384, 4608], P('shard'), may hold values from 2.0269753e-14 to 2.0269753e-13
- v_dec_fc2: float32 [1536, 384], P('shard'), may hold values from 2.0269753e-14 to 2.0269753e-13
- v_vectors: float32 [14592], P('shard'), may hold values from 2.0269753e-14 to 2.0269753e-13
Outputs:
- loss: float32 [], replicated
- grad_norm: float32 [], replicated
- next_enc_rows: float32 [768, 6528], P('shard')
- next_enc_cols: float32 [4608, 768], P('shard')
- next_dec_rows: float32 [384, 4608], P('shard')
- next_dec_fc2: float32 [1536, 384], P('shard')
- next_vectors: float32 [14592], P('shard')
- next_m_enc_rows: float32 [768, 6528], P('shard')
- next_m_enc_cols: float32 [4608, 768], P('shard')
- next_m_dec_rows: float32 [384, 4608], P('shard')
- next_m_dec_fc2: float32 [1536, 384], P('shard')
- next_m_vectors: float32 [14592], P('shard')
- next_v_enc_rows: float32 [768, 6528], P('shard')
- next_v_enc_cols: float32 [4608, 768], P('shard')
- next_v_dec_rows: float32 [384, 4608], P('shard')
- next_v_dec_fc2: float32 [1536, 384], P('shard')
- next_v_vectors: float32 [14592], P('shard')
- low_enc_rows: bfloat16 [768, 6528], P('shard')
- low_enc_cols: bfloat16 [4608, 768], P('shard')
- low_dec_rows: bfloat16 [384, 4608], P('shard')
- low_dec_fc2: bfloat16 [1536, 384], P('shard')
- low_vectors: bfloat16 [14592], P('shard')
Inputs may be any that keep to these rules, and one draw needn't show every extreme that they name: In each clip, visible_idx and masked_idx are disjoint and together name each of its 1568 tubes once. The loss counts the first loss_counts[c] entries of masked_idx[c].
All inputs are finite; a program needn't handle non-finite values.
Results may differ from a plain program's by a relative error of at most 0.0006.
The roundings to bfloat16 on the way count: a program that leaves them out, or rounds other values in their place, can miss the bound.
Values may be sent and summed in bfloat16 or wider, within the bound.
No kernel may reach another device: no remote copies, remote signals or barrier semaphores. Data moves between devices by JAX's collectives and lax.ppermute only.
A program may use at most 384 MiB of HBM per device.

v0:
```python
import jax
import jax.numpy as jnp
from jax import lax
from jax.sharding import PartitionSpec as P

D = 768
HEADS = 12
FF = 3072
DD = 384
DHEADS = 6
DFF = 1536
PATCH = 1536


beta_one = 0.9
beta_two = 0.95
bias_fix_one = 1.0 - 0.9**10
bias_fix_two = 1.0 - 0.95**10
learn_rate = 0.02
decay_rate = 0.05
adam_eps = 1e-12
norm_eps = 1e-06


def product_of(left, right):
    return jnp.dot(left, right, preferred_element_type=jnp.float32)


def product_tn(left, right):
    return jnp.dot(left.T, right, preferred_element_type=jnp.float32)


def product_nt(left, right):
    return jnp.dot(left, right.T, preferred_element_type=jnp.float32)


def sinusoid(positions, feat_width):
    places = jnp.arange(positions).astype(jnp.float32)[:, None]
    column = jnp.arange(feat_width)
    expo = (2 * (column // 2)).astype(jnp.float32) / feat_width
    angles = places / jnp.power(jnp.float32(10000.0), expo)[None, :]
    return jnp.where(column[None, :] % 2 == 0, jnp.sin(angles), jnp.cos(angles))


def unpack(vector):
    widths = [D] * 6 + [FF, D, DD] + [DD] * 6 + [DFF, DD, PATCH]
    pieces = []
    offset = 0
    for piece_width in widths:
        pieces.append(vector[offset : offset + piece_width])
        offset = offset + piece_width
    return pieces


def norm_forward(values, norm_gain, norm_bias):
    centred = values - jnp.mean(values, axis=-1, keepdims=True)
    inverse = lax.rsqrt(jnp.mean(centred * centred, axis=-1, keepdims=True) + norm_eps)
    scaled = centred * inverse
    return (scaled * norm_gain + norm_bias, scaled, inverse)


def norm_backward(upstream, scaled, inverse, norm_gain):
    gain_grad = jnp.sum(upstream * scaled, axis=0)
    bias_grad = jnp.sum(upstream, axis=0)
    weighted = upstream * norm_gain
    inner = (
        weighted
        - jnp.mean(weighted, axis=-1, keepdims=True)
        - scaled * jnp.mean(weighted * scaled, axis=-1, keepdims=True)
    )
    return (inverse * inner, gain_grad, bias_grad)


def gelu_slope(inner):
    return (
        0.5 * (1.0 + lax.erf(inner * 0.7071067811865476))
        + inner * jnp.exp(-0.5 * inner * inner) * 0.3989422804014327
    )


def row_block(length):
    return length // 2 if length >= 1024 and length % 2 == 0 else length


def split_heads(qkv_seq, head_count):
    length = qkv_seq.shape[0]
    feat_width = qkv_seq.shape[1] // 3
    head_dim = feat_width // head_count
    queries = qkv_seq[:, :feat_width].reshape(length, head_count, head_dim)
    keys_all = qkv_seq[:, feat_width : 2 * feat_width].reshape(length, head_count, head_dim)
    values_all = qkv_seq[:, 2 * feat_width :].reshape(length, head_count, head_dim)
    return (queries, keys_all, values_all, head_dim ** (-0.5))


def attend_forward(qkv_seq, head_count):
    length = qkv_seq.shape[0]
    feat_width = qkv_seq.shape[1] // 3
    queries, keys_all, values_all, scale_fac = split_heads(qkv_seq, head_count)
    span = row_block(length)
    outputs = []
    sums = []
    for row_start in range(0, length, span):
        scores = (
            jnp.einsum(
                "qhd,khd->hqk",
                queries[row_start : row_start + span],
                keys_all,
                preferred_element_type=jnp.float32,
            )
            * scale_fac
        )
        peak = jnp.max(scores, axis=-1, keepdims=True)
        raised = jnp.exp(scores - peak)
        totals = jnp.sum(raised, axis=-1, keepdims=True)
        probs_low = (raised / totals).astype(jnp.bfloat16)
        mixed = jnp.einsum(
            "hqk,khd->qhd", probs_low, values_all, preferred_element_type=jnp.float32
        )
        outputs.append(mixed.reshape(span, feat_width))
        sums.append(peak[..., 0] + jnp.log(totals[..., 0]))
    return (jnp.concatenate(outputs, axis=0), jnp.concatenate(sums, axis=1))


def attend_backward(qkv_seq, log_sums, grad_mixed, head_count):
    length = qkv_seq.shape[0]
    feat_width = qkv_seq.shape[1] // 3
    queries, keys_all, values_all, scale_fac = split_heads(qkv_seq, head_count)
    head_dim = feat_width // head_count
    span = row_block(length)
    key_grad = jnp.zeros((length, head_count, head_dim), jnp.float32)
    value_grad = jnp.zeros((length, head_count, head_dim), jnp.float32)
    query_grads = []
    for row_start in range(0, length, span):
        query_block = queries[row_start : row_start + span]
        grad_block = grad_mixed[row_start : row_start + span].reshape(span, head_count, head_dim)
        scores = (
            jnp.einsum("qhd,khd->hqk", query_block, keys_all, preferred_element_type=jnp.float32)
            * scale_fac
        )
        probs = jnp.exp(scores - log_sums[:, row_start : row_start + span, None])
        probs_low = probs.astype(jnp.bfloat16)
        prob_grad = jnp.einsum(
            "qhd,khd->hqk", grad_block, values_all, preferred_element_type=jnp.float32
        )
        score_grad = (
            probs * (prob_grad - jnp.sum(prob_grad * probs, axis=-1, keepdims=True)) * scale_fac
        ).astype(jnp.bfloat16)
        query_grads.append(
            jnp.einsum(
                "hqk,khd->qhd", score_grad, keys_all, preferred_element_type=jnp.float32
            ).reshape(span, feat_width)
        )
        key_grad = key_grad + jnp.einsum(
            "hqk,qhd->khd", score_grad, query_block, preferred_element_type=jnp.float32
        )
        value_grad = value_grad + jnp.einsum(
            "hqk,qhd->khd", probs_low, grad_block, preferred_element_type=jnp.float32
        )
    return jnp.concatenate(
        [
            jnp.concatenate(query_grads, axis=0),
            key_grad.reshape(length, feat_width),
            value_grad.reshape(length, feat_width),
        ],
        axis=1,
    )


def layer_forward(hidden, mats, vecs, head_count, seq_count):
    w_qkv, w_out, w_up, w_down = mats
    gain_one, bias_one, gain_two, bias_two, bias_up, bias_down = vecs
    normed, scaled_one, inverse_one = norm_forward(hidden, gain_one, bias_one)
    normed_low = normed.astype(jnp.bfloat16)
    qkv_low = product_of(normed_low, w_qkv).astype(jnp.bfloat16)
    length = hidden.shape[0] // seq_count
    mixed_list = []
    sums_list = []
    for seq_index in range(seq_count):
        mixed, log_sums = attend_forward(
            qkv_low[seq_index * length : (seq_index + 1) * length], head_count
        )
        mixed_list.append(mixed)
        sums_list.append(log_sums)
    mixed_low = jnp.concatenate(mixed_list, axis=0).astype(jnp.bfloat16)
    middle = hidden + product_of(mixed_low, w_out)
    normed_two, scaled_two, inverse_two = norm_forward(middle, gain_two, bias_two)
    normed_two_low = normed_two.astype(jnp.bfloat16)
    inner = product_of(normed_two_low, w_up) + bias_up
    activ_low = jax.nn.gelu(inner, approximate=False).astype(jnp.bfloat16)
    result = middle + (product_of(activ_low, w_down) + bias_down)
    kept = (
        scaled_one,
        inverse_one,
        normed_low,
        qkv_low,
        sums_list,
        mixed_low,
        scaled_two,
        inverse_two,
        normed_two_low,
        inner,
        activ_low,
    )
    return (result, kept)


def layer_backward(upstream, kept, mats, vecs, head_count, seq_count):
    w_qkv, w_out, w_up, w_down = mats
    gain_one, bias_one, gain_two, bias_two, bias_up, bias_down = vecs
    (
        scaled_one,
        inverse_one,
        normed_low,
        qkv_low,
        sums_list,
        mixed_low,
        scaled_two,
        inverse_two,
        normed_two_low,
        inner,
        activ_low,
    ) = kept
    down_low = upstream.astype(jnp.bfloat16)
    grad_down = product_tn(activ_low, down_low)
    bias_down_grad = jnp.sum(down_low.astype(jnp.float32), axis=0)
    inner_grad = (product_nt(down_low, w_down) * gelu_slope(inner)).astype(jnp.bfloat16)
    grad_up = product_tn(normed_two_low, inner_grad)
    bias_up_grad = jnp.sum(inner_grad.astype(jnp.float32), axis=0)
    middle_part, gain_two_grad, bias_two_grad = norm_backward(
        product_nt(inner_grad, w_up), scaled_two, inverse_two, gain_two
    )
    middle_grad = upstream + middle_part
    branch_low = middle_grad.astype(jnp.bfloat16)
    grad_out = product_tn(mixed_low, branch_low)
    mixed_grad = product_nt(branch_low, w_out).astype(jnp.bfloat16)
    length = upstream.shape[0] // seq_count
    qkv_parts = []
    for seq_index in range(seq_count):
        rows_here = slice(seq_index * length, (seq_index + 1) * length)
        qkv_parts.append(
            attend_backward(
                qkv_low[rows_here], sums_list[seq_index], mixed_grad[rows_here], head_count
            )
        )
    qkv_grad = jnp.concatenate(qkv_parts, axis=0).astype(jnp.bfloat16)
    grad_qkv = product_tn(normed_low, qkv_grad)
    hidden_part, gain_one_grad, bias_one_grad = norm_backward(
        product_nt(qkv_grad, w_qkv), scaled_one, inverse_one, gain_one
    )
    return (
        middle_grad + hidden_part,
        (grad_qkv, grad_out, grad_up, grad_down),
        (gain_one_grad, bias_one_grad, gain_two_grad, bias_two_grad, bias_up_grad, bias_down_grad),
    )


def enc_parts(enc_low_rows, enc_low_cols):
    mats = (
        enc_low_rows[:, : 3 * D],
        enc_low_rows[:, 3 * D : 4 * D],
        enc_low_rows[:, 4 * D : 4 * D + FF],
        enc_low_cols[PATCH:],
    )
    return (mats, enc_low_cols[:PATCH], enc_low_rows[:, 4 * D + FF :])


def dec_parts(dec_low_rows, dec_low_fc2):
    mats = (
        dec_low_rows[:, : 3 * DD],
        dec_low_rows[:, 3 * DD : 4 * DD],
        dec_low_rows[:, 4 * DD : 4 * DD + DFF],
        dec_low_fc2,
    )
    return (mats, dec_low_rows[:, 4 * DD + DFF :])


def adam_update(master, moment_one, moment_two, gradient):
    new_one = beta_one * moment_one + (1.0 - beta_one) * gradient
    new_two = beta_two * moment_two + (1.0 - beta_two) * gradient * gradient
    stepped = new_one / bias_fix_one / (jnp.sqrt(new_two / bias_fix_two) + adam_eps)
    return (master - learn_rate * (stepped + decay_rate * master), new_one, new_two)


def local(
    clips,
    visible_idx,
    masked_idx,
    loss_counts,
    enc_rows,
    enc_cols,
    dec_rows,
    dec_fc2,
    vectors,
    m_enc_rows,
    m_enc_cols,
    m_dec_rows,
    m_dec_fc2,
    m_vectors,
    v_enc_rows,
    v_enc_cols,
    v_dec_rows,
    v_dec_fc2,
    v_vectors,
):
    seq_count = clips.shape[0]
    tube_count = clips.shape[1]
    seen_count = visible_idx.shape[1]
    hidden_count = masked_idx.shape[1]
    masters = (enc_rows, enc_cols, dec_rows, dec_fc2, vectors)
    enc_low_rows, enc_low_cols, vec_low = (
        lax.all_gather(enc_rows.astype(jnp.bfloat16), "shard", axis=0, tiled=True),
        lax.all_gather(enc_cols.astype(jnp.bfloat16), "shard", axis=0, tiled=True),
        lax.all_gather(vectors.astype(jnp.bfloat16), "shard", axis=0, tiled=True),
    )
    pieces = [piece.astype(jnp.float32) for piece in unpack(vec_low)]
    enc_mats, w_embed, w_proj = enc_parts(enc_low_rows, enc_low_cols)
    enc_vecs = (pieces[0], pieces[1], pieces[2], pieces[3], pieces[6], pieces[7])
    dec_vecs = (pieces[9], pieces[10], pieces[11], pieces[12], pieces[15], pieces[16])
    pos_enc = sinusoid(tube_count, D)
    pos_dec = sinusoid(tube_count, DD)
    seen_pixels = jnp.take_along_axis(clips, visible_idx[:, :, None], axis=1).reshape(
        seq_count * seen_count, PATCH
    )
    embedded = product_of(seen_pixels, w_embed) + pos_enc[visible_idx].reshape(
        seq_count * seen_count, D
    )
    encoded, enc_kept = layer_forward(embedded, enc_mats, enc_vecs, HEADS, seq_count)
    latent, latent_scaled, latent_inverse = norm_forward(encoded, pieces[4], pieces[5])
    latent_low = latent.astype(jnp.bfloat16)
    projected = product_of(latent_low, w_proj)
    dec_low_rows, dec_low_fc2 = (
        lax.all_gather(dec_rows.astype(jnp.bfloat16), "shard", axis=0, tiled=True),
        lax.all_gather(dec_fc2.astype(jnp.bfloat16), "shard", axis=0, tiled=True),
    )
    dec_mats, w_head = dec_parts(dec_low_rows, dec_low_fc2)
    seen_rows = projected.reshape(seq_count, seen_count, DD) + pos_dec[visible_idx]
    hidden_rows = pieces[8][None, None, :] + pos_dec[masked_idx]
    dec_input = jnp.concatenate([seen_rows, hidden_rows], axis=1).reshape(
        seq_count * tube_count, DD
    )
    decoded, dec_kept = layer_forward(dec_input, dec_mats, dec_vecs, DHEADS, seq_count)
    final_rows = decoded.reshape(seq_count, tube_count, DD)[:, seen_count:].reshape(
        seq_count * hidden_count, DD
    )
    final, final_scaled, final_inverse = norm_forward(final_rows, pieces[13], pieces[14])
    final_low = final.astype(jnp.bfloat16)
    pred = product_of(final_low, w_head) + pieces[17]
    target = (
        jnp.take_along_axis(clips, masked_idx[:, :, None], axis=1)
        .reshape(seq_count * hidden_count, PATCH)
        .astype(jnp.float32)
    )
    centred = target - jnp.mean(target, axis=-1, keepdims=True)
    target = centred * lax.rsqrt(jnp.mean(centred * centred, axis=-1, keepdims=True) + norm_eps)
    live = (
        (jnp.arange(hidden_count)[None, :] < loss_counts[:, None]).astype(jnp.float32).reshape(-1)
    )
    errors = jnp.mean((pred - target) * (pred - target), axis=-1)
    loss_sum, count_sum = lax.psum(
        (jnp.sum(live * errors), jnp.sum(loss_counts).astype(jnp.float32)), ("rep", "shard")
    )
    loss = loss_sum / count_sum
    pred_grad = (live[:, None] * 2.0 * (pred - target) / (PATCH * count_sum)).astype(jnp.bfloat16)
    back_rows, back_fc2 = (
        lax.all_gather(dec_rows.astype(jnp.bfloat16), "shard", axis=0, tiled=True),
        lax.all_gather(dec_fc2.astype(jnp.bfloat16), "shard", axis=0, tiled=True),
    )
    dec_mats, w_head = dec_parts(back_rows, back_fc2)
    grad_head = product_tn(final_low, pred_grad)
    bias_head_grad = jnp.sum(pred_grad.astype(jnp.float32), axis=0)
    final_grad, final_gain_grad, final_bias_grad = norm_backward(
        product_nt(pred_grad, w_head), final_scaled, final_inverse, pieces[13]
    )
    decoded_grad = jnp.concatenate(
        [
            jnp.zeros((seq_count, seen_count, DD), jnp.float32),
            final_grad.reshape(seq_count, hidden_count, DD),
        ],
        axis=1,
    ).reshape(seq_count * tube_count, DD)
    input_grad, dec_mat_grads, dec_vec_grads = layer_backward(
        decoded_grad, dec_kept, dec_mats, dec_vecs, DHEADS, seq_count
    )
    input_grad = input_grad.reshape(seq_count, tube_count, DD)
    token_grad = jnp.sum(input_grad[:, seen_count:], axis=(0, 1))
    grad_dec_rows = jnp.concatenate(
        [dec_mat_grads[0], dec_mat_grads[1], dec_mat_grads[2], grad_head], axis=1
    )
    grad_dec_fc2 = dec_mat_grads[3]
    dec_reduced = (
        lax.psum_scatter(grad_dec_rows, "shard", scatter_dimension=0, tiled=True),
        lax.psum_scatter(grad_dec_fc2, "shard", scatter_dimension=0, tiled=True),
    )
    back_enc_rows, back_enc_cols = (
        lax.all_gather(enc_rows.astype(jnp.bfloat16), "shard", axis=0, tiled=True),
        lax.all_gather(enc_cols.astype(jnp.bfloat16), "shard", axis=0, tiled=True),
    )
    enc_mats, w_embed, w_proj = enc_parts(back_enc_rows, back_enc_cols)
    proj_grad = input_grad[:, :seen_count].reshape(seq_count * seen_count, DD).astype(jnp.bfloat16)
    grad_proj = product_tn(latent_low, proj_grad)
    encoded_grad, latent_gain_grad, latent_bias_grad = norm_backward(
        product_nt(proj_grad, w_proj), latent_scaled, latent_inverse, pieces[4]
    )
    embedded_grad, enc_mat_grads, enc_vec_grads = layer_backward(
        encoded_grad, enc_kept, enc_mats, enc_vecs, HEADS, seq_count
    )
    grad_embed = product_tn(seen_pixels, embedded_grad.astype(jnp.bfloat16))
    grad_enc_rows = jnp.concatenate(
        [enc_mat_grads[0], enc_mat_grads[1], enc_mat_grads[2], grad_proj], axis=1
    )
    grad_enc_cols = jnp.concatenate([grad_embed, enc_mat_grads[3]], axis=0)
    grad_vectors = jnp.concatenate(
        [
            enc_vec_grads[0],
            enc_vec_grads[1],
            enc_vec_grads[2],
            enc_vec_grads[3],
            latent_gain_grad,
            latent_bias_grad,
            enc_vec_grads[4],
            enc_vec_grads[5],
            token_grad,
            dec_vec_grads[0],
            dec_vec_grads[1],
            dec_vec_grads[2],
            dec_vec_grads[3],
            final_gain_grad,
            final_bias_grad,
            dec_vec_grads[4],
            dec_vec_grads[5],
            bias_head_grad,
        ]
    )
    enc_reduced = (
        lax.psum_scatter(grad_enc_rows, "shard", scatter_dimension=0, tiled=True),
        lax.psum_scatter(grad_enc_cols, "shard", scatter_dimension=0, tiled=True),
        lax.psum_scatter(grad_vectors, "shard", scatter_dimension=0, tiled=True),
    )
    summed = lax.psum(
        (enc_reduced[0], enc_reduced[1], dec_reduced[0], dec_reduced[1], enc_reduced[2]), "rep"
    )
    grads = (summed[0], summed[1], summed[2], summed[3], summed[4])
    squares = jnp.float32(0.0)
    for gradient in grads:
        squares = squares + jnp.sum(gradient * gradient)
    grad_norm = jnp.sqrt(lax.psum(squares, "shard"))
    factor = jnp.minimum(jnp.float32(1.0), lax.rsqrt(count_sum) / grad_norm)
    firsts = (m_enc_rows, m_enc_cols, m_dec_rows, m_dec_fc2, m_vectors)
    seconds = (v_enc_rows, v_enc_cols, v_dec_rows, v_dec_fc2, v_vectors)
    new_w = []
    new_m = []
    new_v = []
    for index in range(5):
        updated = adam_update(masters[index], firsts[index], seconds[index], grads[index] * factor)
        new_w.append(updated[0])
        new_m.append(updated[1])
        new_v.append(updated[2])
    return (
        loss,
        grad_norm,
        new_w[0],
        new_w[1],
        new_w[2],
        new_w[3],
        new_w[4],
        new_m[0],
        new_m[1],
        new_m[2],
        new_m[3],
        new_m[4],
        new_v[0],
        new_v[1],
        new_v[2],
        new_v[3],
        new_v[4],
        new_w[0].astype(jnp.bfloat16),
        new_w[1].astype(jnp.bfloat16),
        new_w[2].astype(jnp.bfloat16),
        new_w[3].astype(jnp.bfloat16),
        new_w[4].astype(jnp.bfloat16),
    )


def solution(mesh):
    in_specs = (
        P(("rep", "shard"), None, None),
        P(("rep", "shard"), None),
        P(("rep", "shard"), None),
        P(("rep", "shard")),
        P("shard", None),
        P("shard", None),
        P("shard", None),
        P("shard", None),
        P("shard"),
        P("shard", None),
        P("shard", None),
        P("shard", None),
        P("shard", None),
        P("shard"),
        P("shard", None),
        P("shard", None),
        P("shard", None),
        P("shard", None),
        P("shard"),
    )
    out_specs = (
        P(),
        P(),
        P("shard", None),
        P("shard", None),
        P("shard", None),
        P("shard", None),
        P("shard"),
        P("shard", None),
        P("shard", None),
        P("shard", None),
        P("shard", None),
        P("shard"),
        P("shard", None),
        P("shard", None),
        P("shard", None),
        P("shard", None),
        P("shard"),
        P("shard", None),
        P("shard", None),
        P("shard", None),
        P("shard", None),
        P("shard"),
    )
    return jax.shard_map(local, mesh=mesh, in_specs=in_specs, out_specs=out_specs, check_vma=False)
```

profile of v0, /device:TPU:0, one launch (start us, length us, event | category | flops | bytes accessed | tf_op | source)
XLA Modules:
  0.0 2225.1 jit_solution(6105228312388666965)
XLA Ops:
  12.5 6.6 convert_element_type.279
  26.0 6.7 all-gather
  35.0 65.6 %gather_fusion.4 = bf16[2822,1536]{1,0:T(8,128)(2,1)} fusion(bf16[2,1568,1536]{2,1,0:T(8,128)(2,1)} %param.19, s32[2822]{0:T(1024)S(1)} %reshape.685), kind=kCustom, calls=%fused_computation.4 | custom fusion | bytes 17360944 | tf_op jit(solution)/shard_map/jit(take_along_axis)/gather | solution.py:349
  100.6 8.6 reshape.688
  123.4 14.6 gather_fusion.3
  138.0 8.5 cosine_select_fusion.1
  148.7 8.3 gather_fusion.2
  161.7 18.7 cosine_select_fusion
  193.6 38.2 %all-gather.8.cloned.1.call-done = bf16[768,6528]{1,0:T(8,128)(2,1)} async-done(((bf16[384,6528]{1,0:T(8,128)(2,1)}), bf16[768,6528]{1,0:T(8,128)(2,1)}) %all-gather.8.cloned.1.call-update) | async-done | bytes 10027024 | tf_op jit(solution)/shard_map/all_gather | solution.py:311
  246.6 11.5 fusion.111
  273.0 10.3 all-gather.10.cloned.1.call-done
  308.7 12.4 multiply_reduce_fusion.6
  321.1 12.5 multiply_reduce_fusion.7
  333.6 12.6 fusion.11
  346.3 14.0 fusion.187
  360.3 12.9 fusion.10
  373.3 14.1 fusion.188
  387.3 12.4 multiply_reduce_fusion.5
  399.7 12.3 multiply_reduce_fusion.4
  412.0 12.6 fusion.12
  424.7 14.2 fusion.186
  438.9 12.5 fusion.13
  451.5 14.1 fusion.185
  476.2 49.4 %fusion.28 = (bf16[3136,1536]{1,0:T(8,128)(2,1)}, f32[3136,1536]{1,0:T(8,128)}) fusion(f32[1536]{0:T(1024)S(1)} %copy-done.150, bf16[384,4608]{1,0:T(8,128)(2,1)} %all-gather.10.cloned.1.call-done, f32[3136,384]{1,0:T(8,128)S(1)} %get-tuple-element.142, f32[384]{0:T(512)S(1)} %copy-done.160, f32[384]{0:T(512)S(1)} %copy-done.147, ...), kind=kOutput, calls=%fused_computation.54 | convolution fusion | flops 4023312384 | bytes 34932224 | tf_op jit(solution)/shard_map/dot_general | solution.py:26
  527.5 9.0 fusion.71
  544.6 15.6 multiply_reduce_fusion.8
  560.8 39.9 %all-reduce.2 = (f32[]{:T(128)}, f32[]{:T(128)}) all-reduce(f32[]{:T(128)} %get-tuple-element.120, f32[]{:T(128)S(6)} %convert_element_type.316), channel_id=1, replica_groups=mesh['rep'=16,'shard'=2] {'rep','shard'}, use_global_device_ids=true, to_apply=%region_28.29 | all-reduce | flops 2 | bytes 16 | tf_op jit(solution)/shard_map/psum | solution.py:359
  601.4 8.1 convert_reduce_fusion.2
  609.6 8.9 multiply_reduce_fusion.18
  634.2 9.1 fusion.354
  643.3 15.4 convert_reduce_fusion.1
  658.7 8.8 multiply_reduce_fusion.11
  674.8 12.3 fusion.349
  687.1 56.1 %fusion.176 = bf16[6,64,784]{2,1,0:T(8,128)(2,1)} fusion(bf16[1568,6,64]{0,2,1:T(8,128)(2,1)S(1)} %bitcast.180, f32[6,784,1568]{2,1,0:T(8,128)} %fusion.349, f32[6,784,1568]{2,1,0:T(8,128)} %get-tuple-element.138, f32[6,784]{1,0:T(8,128)S(1)} %log_add_fusion.1), kind=kOutput, calls=%fused_computation.237 | convolution fusion | flops 1010801792 | bytes 60832128 | tf_op jit(solution)/shard_map/hqk,khd->qhd/dot_general | solution.py:149
  743.3 48.9 %fusion.85 = f32[6,64,1568]{2,1,0:T(8,128)} fusion(bf16[784,6,64]{0,2,1:T(8,128)(2,1)} %bitcast.214, f32[6,784,1568]{2,1,0:T(8,128)} %fusion.349, f32[6,784,1568]{2,1,0:T(8,128)} %get-tuple-element.138, f32[6,784]{1,0:T(8,128)S(1)} %log_add_fusion.1), kind=kOutput, calls=%fused_computation.146 | convolution fusion | flops 1010500736 | bytes 62036352 | tf_op jit(solution)/shard_map/hqk,qhd->khd/dot_general | solution.py:153
  792.5 16.0 fusion.347
  808.5 55.8 %fusion.182 = bf16[6,64,784]{2,1,0:T(8,128)(2,1)} fusion(bf16[1568,6,64]{0,2,1:T(8,128)(2,1)S(1)} %bitcast.184, f32[6,784,1568]{2,1,0:T(8,128)} %fusion.347, f32[6,784,1568]{2,1,0:T(8,128)} %get-tuple-element.134, f32[6,784]{1,0:T(8,128)S(1)} %copy-done.72), kind=kOutput, calls=%fused_computation.239 | convolution fusion | flops 1010801792 | bytes 60832128 | tf_op jit(solution)/shard_map/hqk,khd->qhd/dot_general | solution.py:149
  864.3 48.5 %fusion.73 = f32[6,64,1568]{2,1,0:T(8,128)} fusion(bf16[784,6,64]{0,2,1:T(8,128)(2,1)} %bitcast.212, f32[6,784,1568]{2,1,0:T(8,128)} %fusion.347, f32[6,784,1568]{2,1,0:T(8,128)} %get-tuple-element.134, f32[6,784]{1,0:T(8,128)S(1)} %copy-done.72), kind=kOutput, calls=%fused_computation.142 | convolution fusion | flops 1010500736 | bytes 62036352 | tf_op jit(solution)/shard_map/hqk,qhd->khd/dot_general | solution.py:153
  917.3 14.1 fusion.348
  931.4 12.2 fusion.56
  943.6 14.0 fusion.142
  957.5 12.4 fusion.350
  970.0 12.1 fusion.52
  982.1 13.1 fusion.139
  995.2 55.6 %fusion.173 = bf16[6,64,784]{2,1,0:T(8,128)(2,1)} fusion(bf16[1568,6,64]{0,2,1:T(8,128)(2,1)S(1)} %bitcast.181, f32[6,784,1568]{2,1,0:T(8,128)} %fusion.350, f32[6,784,1568]{2,1,0:T(8,128)} %get-tuple-element.140, f32[6,784]{1,0:T(8,128)S(1)} %copy-done.71), kind=kOutput, calls=%fused_computation.236 | convolution fusion | flops 1010801792 | bytes 60832128 | tf_op jit(solution)/shard_map/hqk,khd->qhd/dot_general | solution.py:149
  1050.9 58.0 %fusion.148 = bf16[6,64,1568]{2,1,0:T(8,128)(2,1)} fusion(f32[6,64,1568]{2,1,0:T(8,128)} %fusion.85, bf16[784,6,64]{0,2,1:T(8,128)(2,1)S(1)} %bitcast.211, f32[6,784,1568]{2,1,0:T(8,128)} %fusion.350, f32[6,784,1568]{2,1,0:T(8,128)} %get-tuple-element.140, f32[6,784]{1,0:T(8,128)S(1)} %copy-done.71), kind=kOutput, calls=%fused_computation.209 | convolution fusion | flops 1011704960 | bytes 63240576 | tf_op jit(solution)/shard_map/hqk,qhd->khd/dot_general | solution.py:153
  1108.8 54.8 %fusion.179 = bf16[6,64,784]{2,1,0:T(8,128)(2,1)} fusion(bf16[1568,6,64]{0,2,1:T(8,128)(2,1)S(1)} %bitcast.185, f32[6,784,1568]{2,1,0:T(8,128)} %fusion.348, f32[6,784,1568]{2,1,0:T(8,128)} %get-tuple-element.136, f32[6,784]{1,0:T(8,128)S(1)} %copy-done.70), kind=kOutput, calls=%fused_computation.238 | convolution fusion | flops 1010801792 | bytes 60832128 | tf_op jit(solution)/shard_map/hqk,khd->qhd/dot_general | solution.py:149
  1163.7 57.1 %fusion.145 = bf16[6,64,1568]{2,1,0:T(8,128)(2,1)} fusion(f32[6,64,1568]{2,1,0:T(8,128)} %fusion.73, bf16[784,6,64]{0,2,1:T(8,128)(2,1)S(1)} %bitcast.209, f32[6,784,1568]{2,1,0:T(8,128)} %fusion.348, f32[6,784,1568]{2,1,0:T(8,128)} %get-tuple-element.136, f32[6,784]{1,0:T(8,128)S(1)} %copy-done.70), kind=kOutput, calls=%fused_computation.208 | convolution fusion | flops 1011704960 | bytes 63240576 | tf_op jit(solution)/shard_map/hqk,qhd->khd/dot_general | solution.py:153
  1220.8 24.7 %fusion.67 = bf16[3136,1152]{0,1:T(8,128)(2,1)S(1)} fusion(bf16[784,384]{0,1:T(8,128)(2,1)} %bitcast.240, bf16[784,384]{0,1:T(8,128)(2,1)} %bitcast.238, bf16[784,384]{0,1:T(8,128)(2,1)} %bitcast.241, bf16[784,384]{0,1:T(8,128)(2,1)} %bitcast.239, bf16[1568,384]{0,1:T(8,128)(2,1)S(1)} %bitcast.205, bf16[1568,384]{0,1:T(8,128)(2,1)} %bitcast.232, ...), kind=kLoop, calls=%fused_computation.111 | loop fusion | flops 57802752 | bytes 14450688 | tf_op jit(solution)/shard_map/concatenate | solution.py:245
  1245.6 6.5 fusion.210
  1255.9 8.4 fusion.326
  1272.6 14.6 multiply_reduce_fusion.12
  1297.4 5.8 convert_reduce_fusion.4
  1310.6 5.7 fusion.198
  1360.6 8.1 pad_maximum_fusion
  1368.8 153.7 %reduce-scatter.7.cloned.1.call-done = f32[2304,768]{1,0:T(8,128)} async-done(((f32[4608,768]{1,0:T(8,128)}), f32[2304,768]{1,0:T(8,128)}) %reduce-scatter.7.cloned.1.call-update) | async-done | bytes 7077904 | tf_op jit(solution)/shard_map/reduce_scatter | solution.py:436
  1522.5 226.7 %reduce-scatter.5.cloned.1.call-done = f32[384,6528]{1,0:T(8,128)} async-done(((f32[768,6528]{1,0:T(8,128)}), f32[384,6528]{1,0:T(8,128)}) %reduce-scatter.5.cloned.1.call-update) | async-done | bytes 10027024 | tf_op jit(solution)/shard_map/reduce_scatter | solution.py:435
  1754.9 7.7 all-reduce.1
  1762.7 63.0 %psum.62 = f32[7296]{0:T(1024)S(1)} all-reduce(f32[7296]{0:T(1024)S(1)} %dynamic-slice.1), channel_id=1, replica_groups=mesh['rep'=16,'shard'=2] {'rep'}, use_global_device_ids=true, to_apply=%region_80.81 | all-reduce | flops 7296 | bytes 58368 | tf_op jit(solution)/shard_map/psum | solution.py:439
  1826.4 302.7 %all-reduce.6.cloned.1.call-done = (f32[384,6528]{1,0:T(8,128)}, f32[2304,768]{1,0:T(8,128)}, f32[192,4608]{1,0:T(8,128)}, f32[768,384]{1,0:T(8,128)}) async-done(((f32[384,6528]{1,0:T(8,128)}, f32[2304,768]{1,0:T(8,128)}, f32[192,4608]{1,0:T(8,128)}, f32[768,384]{1,0:T(8,128)}), (f32[384,6528]{1,0:T(8,128)}, f32[2304,768]{1,0:T(8,128)}, f32[192,4608]{1,0:T(8,128)}, ...) | async-done | bytes 21823504 | tf_op jit(solution)/shard_map/psum | solution.py:439
  2134.9 5.7 multiply_reduce_fusion.10
  2161.3 7.6 fusion.331
  2169.0 20.0 fusion.333
  2189.0 26.9 %fusion.335 = (bf16[384,6528]{1,0:T(8,128)(2,1)}, f32[384,6528]{1,0:T(8,128)}, f32[384,6528]{1,0:T(8,128)}, f32[384,6528]{1,0:T(8,128)}) fusion(f32[384,6528]{1,0:T(8,128)} %param.23, f32[384,6528]{1,0:T(8,128)} %get-tuple-element.48, f32[]{:T(128)S(6)} %min.3, f32[384,6528]{1,0:T(8,128)} %param.28, f32[384,6528]{1,0:T(8,128)} %param.33), kind=kLoop, calls=%fused_computation.490 | loop fusion | flops 42614784 | bytes 75202560 | tf_op jit(solution)/shard_map/convert_element_type | solution.py:476
  (611 shorter events, 250.3 us)
Async XLA Ops:
  7.2 183.3 %all-gather.6.cloned.1.call-start = ((), (), s32[]{:S(2)}) async-start(), calls=%async_computation.4 | async-start | bytes 10616832 | tf_op jit(solution)/shard_map/all_gather | solution.py:312
  12.4 219.3 %all-gather.8.cloned.1.call-start = ((), (), s32[]{:S(2)}) async-start(), calls=%async_computation.5 | async-start | bytes 15040512 | tf_op jit(solution)/shard_map/all_gather | solution.py:311
  19.1 264.1 %all-gather.10.cloned.1.call-start = ((), (), s32[]{:S(2)}) async-start(), calls=%async_computation.6 | async-start | bytes 5308416 | tf_op jit(solution)/shard_map/all_gather | solution.py:332
  22.5 505.0 %all-gather.12.cloned.1.call-start = ((), (), s32[]{:S(2)}) async-start(), calls=%async_computation.7 | async-start | bytes 1769472 | tf_op jit(solution)/shard_map/all_gather | solution.py:333
  25.0 1343.8 %reduce-scatter.11.cloned.1.call-start = ((), (), s32[]{:S(2)}) async-start(), calls=%async_computation.11 | async-start | bytes 3538944 | tf_op jit(solution)/shard_map/reduce_scatter | solution.py:392
  33.6 236.0 %copy-start.135 = (f32[384]{0:T(512)}, f32[384]{0:T(512)S(1)}, u32[]{:S(2)}) copy-start(f32[384]{0:T(512)S(1)} %get-tuple-element.108) | copy-start | bytes 4612
  34.2 197.6 %copy-start.140 = (f32[768]{0:T(1024)}, f32[768]{0:T(1024)S(1)}, u32[]{:S(2)}) copy-start(f32[768]{0:T(1024)S(1)} %get-tuple-element.118) | copy-start | bytes 9220
  34.2 197.6 %copy-start.155 = (f32[768]{0:T(1024)}, f32[768]{0:T(1024)S(1)}, u32[]{:S(2)}) copy-start(f32[768]{0:T(1024)S(1)} %get-tuple-element.117) | copy-start | bytes 9220
  34.2 212.4 %copy-start.81 = (f32[768]{0:T(1024)}, f32[768]{0:T(1024)S(1)}, u32[]{:S(2)}) copy-start(f32[768]{0:T(1024)S(1)} %get-tuple-element.116) | copy-start | bytes 9220
  34.2 212.4 %copy-start.91 = (f32[768]{0:T(1024)}, f32[768]{0:T(1024)S(1)}, u32[]{:S(2)}) copy-start(f32[768]{0:T(1024)S(1)} %get-tuple-element.115) | copy-start | bytes 9220
  34.2 226.0 %copy-start.114 = (f32[768]{0:T(1024)}, f32[768]{0:T(1024)S(1)}, u32[]{:S(2)}) copy-start(f32[768]{0:T(1024)S(1)} %get-tuple-element.112) | copy-start | bytes 9220
  34.2 226.0 %copy-start.130 = (f32[768]{0:T(1024)}, f32[768]{0:T(1024)S(1)}, u32[]{:S(2)}) copy-start(f32[768]{0:T(1024)S(1)} %get-tuple-element.113) | copy-start | bytes 9220
  122.4 68.1 %copy-start.167 = (pred[314]{0:T(512)(128)(4,1)}, pred[314]{0:T(512)(128)(4,1)S(1)}, u32[]{:S(2)}) copy-start(pred[314]{0:T(512)(128)(4,1)S(1)} %broadcast_in_dim.42) | copy-start | bytes 946
  138.0 52.6 %copy-start.42 = (bf16[314,1536]{1,0:T(8,128)(2,1)}, bf16[314,1536]{1,0:T(8,128)(2,1)S(1)}, u32[]{:S(2)}) copy-start(bf16[314,1536]{1,0:T(8,128)(2,1)S(1)} %gather_fusion.3) | copy-start | bytes 2893828
  193.3 48.6 %copy-start.44 = (f32[314,768]{1,0:T(8,128)}, f32[314,768]{1,0:T(8,128)S(1)}, u32[]{:S(2)}) copy-start(f32[314,768]{1,0:T(8,128)S(1)} %get-tuple-element.122) | copy-start | bytes 2893828
  193.3 41.9 %copy-start.138 = (f32[314]{0:T(512)}, f32[314]{0:T(512)S(1)}, u32[]{:S(2)}) copy-start(f32[314]{0:T(512)S(1)} %broadcast_multiply_fusion.18) | copy-start | bytes 3772
  193.6 42.5 %copy-start.153 = (f32[314]{0:T(512)}, f32[314]{0:T(512)S(1)}, u32[]{:S(2)}) copy-start(f32[314]{0:T(512)S(1)} %add_rsqrt_fusion.6) | copy-start | bytes 3772
  241.9 16.2 copy-start.79
  269.5 19.2 copy-start.99
  273.0 15.8 copy-start.55
  294.0 105.7 %copy-start.13 = (bf16[1568,384]{0,1:T(8,128)(2,1)}, bf16[1568,384]{0,1:T(8,128)(2,1)S(1)}, u32[]{:S(2)}) copy-start(bf16[1568,384]{0,1:T(8,128)(2,1)S(1)} %copy.145) | copy-start | bytes 3612676
  299.3 21.9 copy-start.47
  305.7 15.4 copy-start.16
  321.1 25.1 %copy-start.83 = (f32[6,784]{1,0:T(8,128)}, f32[6,784]{1,0:T(8,128)S(1)}, u32[]{:S(2)}) copy-start(f32[6,784]{1,0:T(8,128)S(1)} %get-tuple-element.135) | copy-start | bytes 56452
  333.6 39.6 %copy-start.85 = (f32[6,784]{1,0:T(8,128)}, f32[6,784]{1,0:T(8,128)S(1)}, u32[]{:S(2)}) copy-start(f32[6,784]{1,0:T(8,128)S(1)} %get-tuple-element.133) | copy-start | bytes 56452
  373.2 14.1 copy-start.105
  399.7 25.0 %copy-start.87 = (f32[6,784]{1,0:T(8,128)}, f32[6,784]{1,0:T(8,128)S(1)}, u32[]{:S(2)}) copy-start(f32[6,784]{1,0:T(8,128)S(1)} %get-tuple-element.137) | copy-start | bytes 56452
  412.0 39.4 %copy-start.89 = (f32[6,784]{1,0:T(8,128)}, f32[6,784]{1,0:T(8,128)S(1)}, u32[]{:S(2)}) copy-start(f32[6,784]{1,0:T(8,128)S(1)} %get-tuple-element.139) | copy-start | bytes 56452
  424.7 14.2 copy-start.107
  451.4 14.1 copy-start.109
  451.5 14.1 copy-start.73
  475.0 50.6 %copy-start.2 = (f32[3136,384]{1,0:T(8,128)}, f32[3136,384]{1,0:T(8,128)S(1)}, u32[]{:S(2)}) copy-start(f32[3136,384]{1,0:T(8,128)S(1)} %get-tuple-element.142) | copy-start | bytes 14450692
  475.0 192.5 %copy-start.101 = (f32[3136]{0:T(1024)}, f32[3136]{0:T(1024)S(1)}, u32[]{:S(2)}) copy-start(f32[3136]{0:T(1024)S(1)} %broadcast_multiply_fusion.4) | copy-start | bytes 37636
  476.1 191.4 %copy-start.120 = (f32[3136]{0:T(1024)}, f32[3136]{0:T(1024)S(1)}, u32[]{:S(2)}) copy-start(f32[3136]{0:T(1024)S(1)} %add_rsqrt_fusion) | copy-start | bytes 37636
  476.1 49.5 %copy-start.84 = (f32[6,784]{1,0:T(8,128)S(1)}, f32[6,784]{1,0:T(8,128)}, u32[]{:S(2)}) copy-start(f32[6,784]{1,0:T(8,128)} %copy-done.83) | copy-start | bytes 56452
  476.1 49.5 %copy-start.104 = (f32[6,784]{1,0:T(8,128)S(1)}, f32[6,784]{1,0:T(8,128)}, u32[]{:S(2)}) copy-start(f32[6,784]{1,0:T(8,128)} %copy-done.103) | copy-start | bytes 56452
  476.1 50.1 %copy-start.86 = (f32[6,784]{1,0:T(8,128)S(1)}, f32[6,784]{1,0:T(8,128)}, u32[]{:S(2)}) copy-start(f32[6,784]{1,0:T(8,128)} %copy-done.85) | copy-start | bytes 56452
  476.1 50.1 %copy-start.106 = (f32[6,784]{1,0:T(8,128)S(1)}, f32[6,784]{1,0:T(8,128)}, u32[]{:S(2)}) copy-start(f32[6,784]{1,0:T(8,128)} %copy-done.105) | copy-start | bytes 56452
  476.1 50.7 %copy-start.88 = (f32[6,784]{1,0:T(8,128)S(1)}, f32[6,784]{1,0:T(8,128)}, u32[]{:S(2)}) copy-start(f32[6,784]{1,0:T(8,128)} %copy-done.87) | copy-start | bytes 56452
  476.2 50.7 %copy-start.108 = (f32[6,784]{1,0:T(8,128)S(1)}, f32[6,784]{1,0:T(8,128)}, u32[]{:S(2)}) copy-start(f32[6,784]{1,0:T(8,128)} %copy-done.107) | copy-start | bytes 56452
  476.2 50.7 %copy-start.90 = (f32[6,784]{1,0:T(8,128)S(1)}, f32[6,784]{1,0:T(8,128)}, u32[]{:S(2)}) copy-start(f32[6,784]{1,0:T(8,128)} %copy-done.89) | copy-start | bytes 56452
  476.2 50.7 %copy-start.110 = (f32[6,784]{1,0:T(8,128)S(1)}, f32[6,784]{1,0:T(8,128)}, u32[]{:S(2)}) copy-start(f32[6,784]{1,0:T(8,128)} %copy-done.109) | copy-start | bytes 56452
  476.2 51.3 %copy-start.162 = (f32[384]{0:T(512)S(1)}, f32[384]{0:T(512)}, u32[]{:S(2)}) copy-start(f32[384]{0:T(512)} %get-tuple-element.104) | copy-start | bytes 4612
  539.8 78.7 %copy-start.126 = (f32[2822]{0:T(1024)}, f32[2822]{0:T(1024)S(1)}, u32[]{:S(2)}) copy-start(f32[2822]{0:T(1024)S(1)} %div.319) | copy-start | bytes 33868
  539.9 78.6 %copy-start.128 = (f32[2822]{0:T(1024)}, f32[2822]{0:T(1024)S(1)}, u32[]{:S(2)}) copy-start(f32[2822]{0:T(1024)S(1)} %rsqrt.75) | copy-start | bytes 33868
  544.6 15.6 copy-start.144
  634.2 24.5 %slice-start = ((s8[4816896]{0:T(1024)(128)(4,1)}), s8[622592]{0:T(1024)(128)(4,1)S(1)}, s32[]{:S(2)}) async-start(s8[4816896]{0:T(1024)(128)(4,1)} %bitcast.170), calls=%async_computation.13 | async-start | bytes 1245184
  643.3 15.4 slice-start.1
  743.3 48.9 %copy-start.57 = (bf16[784,384]{1,0:T(8,128)(2,1)S(1)}, bf16[784,384]{1,0:T(8,128)(2,1)}, u32[]{:S(2)}) copy-start(bf16[784,384]{1,0:T(8,128)(2,1)} %get-tuple-element.90) | copy-start | bytes 1806340
  792.5 16.0 copy-start.17
  792.5 16.0 copy-start.72
  912.8 456.0 %reduce-scatter.9.cloned.1.call-start = ((), (), s32[]{:S(2)}) async-start(), calls=%async_computation.10 | async-start | bytes 10616832 | tf_op jit(solution)/shard_map/reduce_scatter | solution.py:391
  917.3 14.1 copy-start.33
  917.3 14.1 copy-start.70
  995.2 55.6 %copy-start.50 = (bf16[784,384]{0,1:T(8,128)(2,1)S(1)}, bf16[784,384]{0,1:T(8,128)(2,1)}, u32[]{:S(2)}) copy-start(bf16[784,384]{0,1:T(8,128)(2,1)} %copy.146) | copy-start | bytes 1806340
  1050.8 58.0 %copy-start.18 = (bf16[1568,384]{0,1:T(8,128)(2,1)S(1)}, bf16[1568,384]{0,1:T(8,128)(2,1)}, u32[]{:S(2)}) copy-start(bf16[1568,384]{0,1:T(8,128)(2,1)} %copy-done.16) | copy-start | bytes 3612676
  1108.8 54.8 %copy-start.48 = (bf16[784,384]{0,1:T(8,128)(2,1)S(1)}, bf16[784,384]{0,1:T(8,128)(2,1)}, u32[]{:S(2)}) copy-start(bf16[784,384]{0,1:T(8,128)(2,1)} %copy-done.47) | copy-start | bytes 1806340
  1163.7 57.1 %copy-start.34 = (bf16[6,64,1568]{2,1,0:T(8,128)(2,1)S(1)}, bf16[6,64,1568]{2,1,0:T(8,128)(2,1)}, u32[]{:S(2)}) copy-start(bf16[6,64,1568]{2,1,0:T(8,128)(2,1)} %fusion.142) | copy-start | bytes 3612676
  1220.8 24.7 %copy-start.7 = (bf16[3136,384]{0,1:T(8,128)(2,1)S(1)}, bf16[3136,384]{0,1:T(8,128)(2,1)}, u32[]{:S(2)}) copy-start(bf16[3136,384]{0,1:T(8,128)(2,1)} %copy-done.6) | copy-start | bytes 7225348
  1271.9 250.7 %reduce-scatter.7.cloned.1.call-start = ((), (), s32[]{:S(2)}) async-start(), calls=%async_computation.9 | async-start | bytes 21233664 | tf_op jit(solution)/shard_map/reduce_scatter | solution.py:436
  1351.6 397.7 %reduce-scatter.5.cloned.1.call-start = ((), (), s32[]{:S(2)}) async-start(), calls=%async_computation.8 | async-start | bytes 30081024 | tf_op jit(solution)/shard_map/reduce_scatter | solution.py:435
  1368.7 760.3 %all-reduce.6.cloned.1.call-start = ((), (), s32[]{:S(2)}) async-start(), calls=%async_computation.12 | async-start | bytes 43646976 | tf_op jit(solution)/shard_map/psum | solution.py:439
  1825.7 314.8 %copy-start.80 = (f32[7296]{0:T(1024)}, f32[7296]{0:T(1024)S(1)}, u32[]{:S(2)}) copy-start(f32[7296]{0:T(1024)S(1)} %psum.62) | copy-start | bytes 87556
  2143.8 17.6 copy-start.28
  (142 other events, 812.4 us)
Sparse Core Ops, SparseCore 0:
  12.5 92.5 all-gather.5
  107.3 124.4 all-gather.7
  233.9 49.3 all-gather.9
  285.2 22.7 all-gather.11
  912.9 35.6 reduce-scatter.10
  1272.0 86.6 reduce-scatter.8
  1361.0 161.4 reduce-scatter.6
  1524.8 224.3 reduce-scatter.4
  1753.9 375.1 all-reduce.5
where the time goes:
time: 2240 us; the launch traced here: 2230 us
  matrix products  891 us (40%)
  waiting for transfers between devices  732 us (33%)
  other arithmetic  276 us (12%)
  local copies, waits for them, and re-layouts  175 us (8%)
  blocking collectives  123 us (5%)
  between operations  27.7 us (1%)
    psum x1, waiting for transfers between devices, local(): lax.psum((enc_reduced[0], enc_reduced[1], dec_reduced[0], dec_reduced[1],...  303 us
    dot_general x6, matrix products, attend_backward(): jnp.einsum('hqk,khd->qhd', score_grad, keys_all, preferred_element_type=j...  232 us
    reduce_scatter x1, waiting for transfers between devices, local(): lax.psum_scatter(grad_enc_rows, 'shard', scatter_dimension=0, tiled=True)  227 us
    dot_general x6, matrix products, attend_backward(): jnp.einsum('hqk,qhd->khd', score_grad, query_block, preferred_element_typ...  222 us
    reduce_scatter x1, waiting for transfers between devices, local(): lax.psum_scatter(grad_enc_cols, 'shard', scatter_dimension=0, tiled=True)  154 us
    dot_general x11, matrix products, product_of(): return jnp.dot(left, right, preferred_element_type=jnp.float32)  105 us
    gather x3, local copies, waits for them, and re-layouts, local(): jnp.take_along_axis(clips, masked_idx[:, :, None], axis=1)  74.3 us
    dot_general x10, matrix products, product_nt(): return jnp.dot(left, right.T, preferred_element_type=jnp.float32)  65.2 us
  transfers between devices with their start and end apart: 9, of which 5 were waited for; matrix products, arithmetic and copies ran while one was open for 41% of the time, Pallas kernels for 0%

commit v1 on v0

v1 whole, which is shorter than its diff:
```python
import functools
import jax
import jax.numpy as jnp
from jax import lax
from jax.experimental import pallas as pl
from jax.experimental.pallas import tpu as pltpu
from jax.sharding import PartitionSpec as P

D = 768
HEADS = 12
FF = 3072
DD = 384
DHEADS = 6
DFF = 1536
PATCH = 1536


beta_one = 0.9
beta_two = 0.95
bias_fix_one = 1.0 - 0.9**10
bias_fix_two = 1.0 - 0.95**10
learn_rate = 0.02
decay_rate = 0.05
adam_eps = 1e-12
norm_eps = 1e-06


def product_of(left, right):
    return jnp.dot(left, right, preferred_element_type=jnp.float32)


def product_tn(left, right):
    return jnp.dot(left.T, right, preferred_element_type=jnp.float32)


f32, bf16 = jnp.float32, jnp.bfloat16
LOG2E = 1.4426950408889634
NT = (((1,), (1,)), ((), ()))
NN = (((1,), (0,)), ((), ()))
TN = (((0,), (0,)), ((), ()))
def dot(a, b, dims): return lax.dot_general(a, b, dims, preferred_element_type=f32)

def cost(micros, moved=0):
    return pl.CostEstimate(flops=int(micros * 1.1e9), transcendentals=0, bytes_accessed=moved)

def fwd_body(scale, q_ref, k_ref, v_ref, o_ref, lse_ref):
    q = q_ref[0]; k = k_ref[0]; v = v_ref[0]
    lane = lax.broadcasted_iota(jnp.int32, (1, 128), 1)
    outs = []
    for h in range(2):
        own = (lane < 64) if h == 0 else (lane >= 64)
        qh = jnp.where(own, q, jnp.zeros_like(q))
        s = dot(qh, k, NT)
        peak = jnp.max(s, axis=1, keepdims=True)
        e = jnp.exp2((s - peak) * (scale * LOG2E))
        tot = jnp.sum(e, axis=1, keepdims=True)
        p = (e * (1.0 / tot)).astype(bf16)
        outs.append(dot(p, v, NN))
        lse_ref[0, 0, h:h+1, :] = (peak * (scale * LOG2E) + jnp.log2(tot)).T
    o_ref[0] = jnp.where(lane < 64, outs[0], outs[1]).astype(bf16)

def attn_fwd(qkv, heads, rows, bq):
    clips, keys, w3 = qkv.shape
    pairs = heads // 2
    nb = rows // bq
    body = functools.partial(fwd_body, 64 ** -0.5)
    return pl.pallas_call(
        body, grid=(clips, pairs, nb),
        in_specs=[pl.BlockSpec((1, bq, 128), lambda c, p, i: (c, i, p)),
                  pl.BlockSpec((1, keys, 128), lambda c, p, i: (c, 0, pairs + p)),
                  pl.BlockSpec((1, keys, 128), lambda c, p, i: (c, 0, 2 * pairs + p))],
        out_specs=[pl.BlockSpec((1, bq, 128), lambda c, p, i: (c, i, p)),
                   pl.BlockSpec((1, 1, 2, bq), lambda c, p, i: (c * pairs + p, i, 0, 0))],
        out_shape=[jax.ShapeDtypeStruct((clips, rows, w3 // 3), bf16),
                   jax.ShapeDtypeStruct((clips * pairs, nb, 2, bq), f32)],
        compiler_params=pltpu.CompilerParams(vmem_limit_bytes=60 << 20), name="dec_attend_forward", cost_estimate=cost(70),
    )(qkv, qkv, qkv)

def bwd_body(scale, nb, mode, q_ref, k_ref, v_ref, do_ref, lse_ref, dq_ref, dk_ref, dv_ref, dk_acc, dv_acc, kt_ref):
    i = pl.program_id(2)
    q = q_ref[0]; k = k_ref[0]; v = v_ref[0]; do = do_ref[0]
    lane = lax.broadcasted_iota(jnp.int32, (1, 128), 1)
    if mode == 1:
        @pl.when(i == 0)
        def _(): kt_ref[...] = k.T
    dk = dv = None
    dqs = []
    for h in range(2):
        own = (lane < 64) if h == 0 else (lane >= 64)
        qh = jnp.where(own, q, jnp.zeros_like(q))
        doh = jnp.where(own, do, jnp.zeros_like(do))
        s = dot(k, qh, NT)
        dp = dot(v, doh, NT)
        p = jnp.exp2(s * (scale * LOG2E) - lse_ref[0, 0, h:h+1, :])
        pd = p * dp
        delta = jnp.sum(pd, axis=0, keepdims=True)
        ds = (p * (dp - delta)).astype(bf16)
        a = dot(p.astype(bf16), doh, NN)
        b = dot(ds, qh, NN)
        dv = a if dv is None else dv + a
        dk = b if dk is None else dk + b
        if mode == 0:
            dqs.append(dot(ds, k, TN))
        else:
            dqs.append(dot(kt_ref[h*64:(h+1)*64, :], ds, NN))
    if mode == 0:
        dq = jnp.where(lane < 64, dqs[0], dqs[1])
    else:
        dq = jnp.concatenate(dqs, axis=0).T
    bq = q.shape[0]
    dq_ref[0, pl.ds(pl.multiple_of(i * bq, bq), bq), :] = (dq * scale).astype(bf16)
    @pl.when(i == nb - 1)
    def _():
        keys = k.shape[0]
        if nb * bq < keys:
            dq_ref[0, nb * bq:keys, :] = jnp.zeros((keys - nb * bq, 128), bf16)
    @pl.when(i == 0)
    def _():
        dk_acc[...] = dk; dv_acc[...] = dv
    @pl.when(i > 0)
    def _():
        dk_acc[...] += dk; dv_acc[...] += dv
    @pl.when(i == nb - 1)
    def _():
        dk_ref[0] = (dk_acc[...] * scale).astype(bf16)
        dv_ref[0] = dv_acc[...].astype(bf16)

def attn_bwd(qkv, do, lse, heads, rows, bq, clip, pair):
    clips, keys, w3 = qkv.shape
    pairs = heads // 2
    nb = rows // bq
    return pl.pallas_call(
        functools.partial(bwd_body, 64 ** -0.5, nb, 0), grid=(1, 1, nb),
        in_specs=[pl.BlockSpec((1, bq, 128), lambda c, p, i: (clip, i, pair)),
                  pl.BlockSpec((1, keys, 128), lambda c, p, i: (clip, 0, pairs + pair)),
                  pl.BlockSpec((1, keys, 128), lambda c, p, i: (clip, 0, 2 * pairs + pair)),
                  pl.BlockSpec((1, bq, 128), lambda c, p, i: (clip, i, pair)),
                  pl.BlockSpec((1, 1, 2, bq), lambda c, p, i: (clip * pairs + pair, i, 0, 0))],
        out_specs=[pl.BlockSpec((1, keys, 128), lambda c, p, i: (0, 0, 0))] * 3,
        out_shape=[jax.ShapeDtypeStruct((1, keys, 128), bf16)] * 3,
        scratch_shapes=[pltpu.VMEM((keys, 128), f32), pltpu.VMEM((keys, 128), f32), pltpu.VMEM((128, keys), bf16)],
        compiler_params=pltpu.CompilerParams(vmem_limit_bytes=60 << 20), name=f"dec_attend_backward_{clip}_{pair}",
        cost_estimate=cost(17),
    )(qkv, qkv, qkv, do, lse)
DEC_VEC = 6 * D + FF + D + DD

def ln(x):
    c = x - jnp.mean(x, axis=1, keepdims=True)
    inv = lax.rsqrt(jnp.mean(c * c, axis=1, keepdims=True) + norm_eps)
    return c * inv, inv

def ln_back(up, scaled, inv, gain):
    w = up * gain
    return inv * (w - jnp.mean(w, axis=1, keepdims=True) - scaled * jnp.mean(w * scaled, axis=1, keepdims=True))

def col(x): return jnp.sum(x, axis=0, keepdims=True)

def gelu_parts(x):
    cdf = 0.5 * (1.0 + lax.erf(x * 0.7071067811865476))
    return x * cdf, cdf + x * jnp.exp(-0.5 * x * x) * 0.3989422804014327

def post_body(nb, rows, keys, cnt_ref, inv_ref, h_ref, o_ref, t_ref, wout_ref, wup_ref, wdown_ref, whead_ref,
              v_ref, dmid_ref, do_ref, grow_ref, gdown_ref, s384_ref, s1536_ref, loss_ref, gdown_acc):
    c = pl.program_id(0); i = pl.program_id(1)
    first = jnp.logical_and(c == 0, i == 0)
    @pl.when(first)
    def _():
        for r in (grow_ref, gdown_acc, s384_ref, s1536_ref, loss_ref):
            r[...] = jnp.zeros_like(r)
    R = rows
    h = h_ref[0]; o = o_ref[0]
    w, ff = h.shape[1], wup_ref.shape[1]
    gain2, bias2, gainf, biasf = (v_ref[:, DEC_VEC + j * DD:DEC_VEC + (j + 1) * DD] for j in range(2, 6))
    bup = v_ref[:, DEC_VEC + 6 * DD:DEC_VEC + 6 * DD + DFF]
    bdown = v_ref[:, DEC_VEC + 6 * DD + DFF:DEC_VEC + 7 * DD + DFF]
    bhead = v_ref[:, DEC_VEC + 7 * DD + DFF:]
    h1 = h + dot(o, wout_ref[...], NN)
    sc2, inv2 = ln(h1)
    m = (sc2 * gain2 + bias2).astype(bf16)
    inner = dot(m, wup_ref[...], NN) + bup
    act, slope = gelu_parts(inner)
    act = act.astype(bf16)
    out = h1 + (dot(act, wdown_ref[...], NN) + bdown)
    scf, invf = ln(out)
    fin = (scf * gainf + biasf).astype(bf16)
    pred = dot(fin, whead_ref[...], NN) + bhead
    t = t_ref[0].astype(f32)
    tc = t - jnp.mean(t, axis=1, keepdims=True)
    err = pred - tc * lax.rsqrt(jnp.mean(tc * tc, axis=1, keepdims=True) + norm_eps)
    row = lax.broadcasted_iota(jnp.int32, (R, 1), 0) + i * R
    live = (row < cnt_ref[c]).astype(f32)
    rl = jnp.mean(err * err, axis=1, keepdims=True) * live
    loss_ref[...] += jnp.sum(rl).reshape(1, 1)
    pg32 = err * (live * inv_ref[0])
    pg = pg32.astype(bf16)
    grow_ref[:, w + ff:] += dot(fin, pg, TN)
    dfin = dot(pg, whead_ref[...], NT)
    s1536_ref[1:2, :] += col(pg.astype(f32))
    s384_ref[2:3, :] += col(dfin * scf)
    s384_ref[3:4, :] += col(dfin)
    dout = ln_back(dfin, scf, invf, gainf)
    dl = dout.astype(bf16)
    gdown_acc[...] += dot(dl, act, TN)
    s384_ref[4:5, :] += col(dl.astype(f32))
    din = (dot(dl, wdown_ref[...], NT) * slope).astype(bf16)
    grow_ref[:, w:w + ff] += dot(m, din, TN)
    s1536_ref[0:1, :] += col(din.astype(f32))
    dm = dot(din, wup_ref[...], NT)
    s384_ref[0:1, :] += col(dm * sc2)
    s384_ref[1:2, :] += col(dm)
    dmid = dout + ln_back(dm, sc2, inv2, gain2)
    bl = dmid.astype(bf16)
    grow_ref[:, :w] += dot(o, bl, TN)
    do_ref[0] = dot(bl, wout_ref[...], NT).astype(bf16)
    dmid_ref[0, pl.ds(pl.multiple_of(i * R, R), R), :] = dmid
    @pl.when(i == nb - 1)
    def _():
        dmid_ref[0, nb * R:keys, :] = jnp.zeros((keys - nb * R, dmid.shape[1]), f32)
    @pl.when(jnp.logical_and(c == pl.num_programs(0) - 1, i == nb - 1))
    def _():
        gdown_ref[...] = gdown_acc[...].T

def dec_post(counts, inv, h, o, t, wout, wup, wdown, whead, vec, R):
    clips, keys, w = h.shape
    rows = o.shape[1]; nb = rows // R
    ff, px = wup.shape[1], whead.shape[1]
    full = lambda a: pl.BlockSpec(a.shape, lambda c, i: (0,) * len(a.shape))
    sm = pl.BlockSpec(memory_space=pltpu.SMEM)
    outs = [jax.ShapeDtypeStruct((clips, keys, w), f32), jax.ShapeDtypeStruct((clips, rows, w), bf16),
            jax.ShapeDtypeStruct((w, w + ff + px), f32), jax.ShapeDtypeStruct((ff, w), f32), jax.ShapeDtypeStruct((8, w), f32), jax.ShapeDtypeStruct((8, ff), f32),
            jax.ShapeDtypeStruct((1, 1), f32)]
    blk = lambda n: pl.BlockSpec((1, R, n), lambda c, i: (c, i, 0))
    return pl.pallas_call(
        functools.partial(post_body, nb, R, keys), grid=(clips, nb),
        in_specs=[sm, sm, blk(w), blk(w), blk(px), full(wout), full(wup), full(wdown), full(whead), full(vec)],
        out_specs=[pl.BlockSpec((1, keys, w), lambda c, i: (c, 0, 0)), blk(w)] + [full(x) for x in outs[2:]],
        out_shape=outs, compiler_params=pltpu.CompilerParams(vmem_limit_bytes=62 << 20), name="dec_post",
        scratch_shapes=[pltpu.VMEM((w, ff), f32)], cost_estimate=cost(67),
    )(counts, inv, h, o, t, wout, wup, wdown, whead, vec)

def qkv_body(h_ref, w_ref, v_ref, o_ref):
    s, _ = ln(h_ref[0])
    a = (s * v_ref[:, DEC_VEC:DEC_VEC + DD] + v_ref[:, DEC_VEC + DD:DEC_VEC + 2 * DD]).astype(bf16)
    o_ref[0] = dot(a, w_ref[...], NN).astype(bf16)

def dec_qkv(h, w, v, R):
    clips, keys, d = h.shape
    full = lambda a: pl.BlockSpec(a.shape, lambda c, i: (0,) * len(a.shape))
    return pl.pallas_call(qkv_body, grid=(clips, keys // R),
        in_specs=[pl.BlockSpec((1, R, d), lambda c, i: (c, i, 0)), full(w), full(v)],
        out_specs=pl.BlockSpec((1, R, w.shape[1]), lambda c, i: (c, i, 0)),
        out_shape=jax.ShapeDtypeStruct((clips, keys, w.shape[1]), bf16),
        compiler_params=pltpu.CompilerParams(vmem_limit_bytes=60 << 20), name="dec_qkv", cost_estimate=cost(9))(h, w, v)

def qkvb_body(R, masked, h_ref, dmid_ref, w_ref, v_ref, gi_ref, si_ref, *refs):
    parts, (dh_ref, g_ref, s_ref) = refs[:9], refs[9:]
    i = pl.program_id(0)
    @pl.when(i == 0)
    def _():
        g_ref[...] = gi_ref[...]; s_ref[...] = si_ref[...]
    d = h_ref.shape[2]
    s, inv = ln(h_ref[0])
    gain = v_ref[:, DEC_VEC:DEC_VEC + DD]
    a = (s * gain + v_ref[:, DEC_VEC + DD:DEC_VEC + 2 * DD]).astype(bf16)
    da = None
    for j in range(3):
        x = jnp.concatenate([parts[3 * p + j][0] for p in range(3)], axis=1)
        g_ref[:, j * d:(j + 1) * d] += dot(a, x, TN)
        y = dot(x, w_ref[:, j * d:(j + 1) * d], NT)
        da = y if da is None else da + y
    s_ref[0:1, :] += col(da * s)
    s_ref[1:2, :] += col(da)
    dh = dmid_ref[0] + ln_back(da, s, inv, gain)
    row = lax.broadcasted_iota(jnp.int32, (R, 1), 0) + i * R
    s_ref[2:3, :] += col(jnp.where(row < masked, dh, 0.0))
    dh_ref[0] = dh.astype(bf16)

def dec_qkv_back(h, parts, dmid, w, v, masked, R, clip, before):
    clips, keys, d = h.shape
    full = lambda a: pl.BlockSpec(a.shape, lambda i: (0,) * len(a.shape))
    blk = pl.BlockSpec((1, R, d), lambda i: (clip, i, 0))
    part = pl.BlockSpec((1, R, 128), lambda i: (0, i, 0))
    outs = [jax.ShapeDtypeStruct((1, keys, d), bf16), jax.ShapeDtypeStruct((d, 3 * d), f32), jax.ShapeDtypeStruct((8, d), f32)]
    return pl.pallas_call(functools.partial(qkvb_body, R, masked), grid=(keys // R,),
        in_specs=[blk, blk, full(w), full(v), full(outs[1]), full(outs[2])] + [part] * 9,
        out_specs=[pl.BlockSpec((1, R, d), lambda i: (0, i, 0)), full(outs[1]), full(outs[2])], out_shape=outs,
        compiler_params=pltpu.CompilerParams(vmem_limit_bytes=60 << 20), name=f"dec_qkv_back_{clip}",
        cost_estimate=cost(10))(h, dmid, w, v, *before, *parts)

def pick_body(idx_ref, x_ref, *refs):
    n = x_ref.shape[1]
    hot = (idx_ref[0] == lax.broadcasted_iota(jnp.int32, (1, n), 1)).astype(f32).astype(bf16)
    refs[-1][0] = dot(hot, x_ref[0], NN).astype(bf16)

def pick_rows(x, idx, R, clip, name, into=None):
    clips, n, w = x.shape
    m = idx.shape[1]
    more = [] if into is None else [into]
    return pl.pallas_call(pick_body, grid=(m // R,),
        in_specs=[pl.BlockSpec((1, R, 1), lambda i: (clip, i, 0)), pl.BlockSpec((1, n, w), lambda i: (clip, 0, 0))]
        + [pl.BlockSpec(memory_space=pl.ANY)] * len(more),
        out_specs=pl.BlockSpec((1, R, w), lambda i: (clip, i, 0)),
        out_shape=jax.ShapeDtypeStruct((clips, m, w), bf16), cost_estimate=cost(m / 140),
        input_output_aliases={2: 0} if more else {},
        compiler_params=pltpu.CompilerParams(vmem_limit_bytes=60 << 20), name=f"{name}_{clip}")(idx[:, :, None], x, *more)

QKV, OUT, UP, PROJ = slice(0, 3 * D), slice(3 * D, 4 * D), slice(4 * D, 4 * D + FF), slice(4 * D + FF, 4 * D + FF + DD)

def enc_vec(v_ref, at):
    starts = [0, D, 2 * D, 3 * D, 4 * D, 5 * D, 6 * D, 6 * D + FF]
    return v_ref[:, starts[at]:starts[at] + (FF if at == 6 else D)]

def most(x):
    x = x.astype(f32)
    return jnp.max(jnp.sum(x * x, axis=0, keepdims=True))

def enc_scores(qkv_ref, rows, p, h, seen):
    lane = lax.broadcasted_iota(jnp.int32, (1, 128), 1)
    own = (lane < 64) if h == 0 else (lane >= 64)
    q = qkv_ref[rows, p * 128:(p + 1) * 128]
    k = qkv_ref[rows, D + p * 128:D + (p + 1) * 128]
    v = qkv_ref[rows, 2 * D + p * 128:2 * D + (p + 1) * 128]
    qh = jnp.where(own, q, jnp.zeros_like(q))
    s = dot(qh, k, NT)
    s = jnp.where(lax.broadcasted_iota(jnp.int32, (1, s.shape[1]), 1) < seen, s, -3e38)
    peak = jnp.max(s, axis=1, keepdims=True)
    e = jnp.exp2((s - peak) * (0.125 * LOG2E))
    return q, k, v, qh, own, e * (1.0 / jnp.sum(e, axis=1, keepdims=True))

def enc_fwd_body(clips, seen, x_ref, pos_ref, wr_ref, wc_ref, v_ref,
                 h_ref, qkv_ref, h1_ref, inner_ref, enc_ref, proj_ref, tall_ref, pair_ref, m_ref, lat_ref, most_ref):
    x = x_ref[...]
    h = dot(x, wc_ref[:PATCH], NN) + pos_ref[...]
    h_ref[...] = h
    s1, _ = ln(h)
    a = (s1 * enc_vec(v_ref, 0) + enc_vec(v_ref, 1)).astype(bf16)
    pair_ref[0] = a
    qkv_ref[...] = dot(a, wr_ref[:, QKV], NN).astype(bf16)
    n = h.shape[0] // clips
    for c in range(clips):
        rows = slice(c * n, (c + 1) * n)
        for p in range(HEADS // 2):
            outs = []
            for hd in range(2):
                q, k, v, qh, own, prob = enc_scores(qkv_ref, rows, p, hd, seen)
                outs.append(dot(prob.astype(bf16), v, NN))
            lane = lax.broadcasted_iota(jnp.int32, (1, 128), 1)
            pair_ref[1, rows, p * 128:(p + 1) * 128] = jnp.where(lane < 64, outs[0], outs[1]).astype(bf16)
    o = pair_ref[1]
    h1 = h + dot(o, wr_ref[:, OUT], NN)
    h1_ref[...] = h1
    s2, _ = ln(h1)
    m = (s2 * enc_vec(v_ref, 2) + enc_vec(v_ref, 3)).astype(bf16)
    m_ref[...] = m
    inner = dot(m, wr_ref[:, UP], NN) + enc_vec(v_ref, 6)
    inner_ref[...] = inner
    act = gelu_parts(inner)[0].astype(bf16)
    out = h1 + (dot(act, wc_ref[PATCH:], NN) + enc_vec(v_ref, 7))
    enc_ref[...] = out
    sf, _ = ln(out)
    lat = (sf * enc_vec(v_ref, 4) + enc_vec(v_ref, 5)).astype(bf16)
    lat_ref[...] = lat
    proj_ref[...] = dot(lat, wr_ref[:, PROJ], NN)
    tall_ref[:, :PATCH] = x
    tall_ref[:, PATCH:] = act
    for at, y in enumerate((x, act, a, o, m)):
        most_ref[at:at + 1, :] = jnp.broadcast_to(most(y).reshape(1, 1), (1, 128))

def whole(shape): return pl.BlockSpec(shape, lambda: (0,) * len(shape))

def enc_fwd(x, pos, wr, wc, vec, clips, seen):
    n = x.shape[0]
    shapes = [((n, D), f32), ((n, 3 * D), bf16), ((n, D), f32), ((n, FF), f32), ((n, D), f32), ((n, DD), f32),
              ((n, PATCH + FF), bf16), ((2, n, D), bf16), ((n, D), bf16), ((n, D), bf16), ((8, 128), f32)]
    return pl.pallas_call(functools.partial(enc_fwd_body, clips, seen),
        in_specs=[whole(a.shape) for a in (x, pos, wr, wc, vec)],
        out_specs=[whole(s) for s, _ in shapes], out_shape=[jax.ShapeDtypeStruct(s, d) for s, d in shapes],
        compiler_params=pltpu.CompilerParams(vmem_limit_bytes=62 << 20), name="enc_forward",
        cost_estimate=pl.CostEstimate(flops=2 * n * 8552448, transcendentals=n * FF, bytes_accessed=26 << 20),
    )(x, pos, wr, wc, vec)

def enc_bwd_body(clips, seen, dp_ref, h_ref, qkv_ref, h1_ref, inner_ref, enc_ref, wr_ref, wc_ref, v_ref,
                 gdown_ref, gup_ref, gwide_ref, gin_ref, s_ref, sup_ref, most_ref):
    sf, invf = ln(enc_ref[...])
    up = dot(dp_ref[...], wr_ref[:, PROJ], NT)
    s_ref[4:5, :] = col(up * sf); s_ref[5:6, :] = col(up)
    dout = ln_back(up, sf, invf, enc_vec(v_ref, 4))
    dl = dout.astype(bf16)
    gdown_ref[...] = dl
    s_ref[6:7, :] = col(dl.astype(f32))
    din = (dot(dl, wc_ref[PATCH:], NT) * gelu_parts(inner_ref[...])[1]).astype(bf16)
    gup_ref[...] = din
    sup_ref[...] = col(din.astype(f32))
    dm = dot(din, wr_ref[:, UP], NT)
    s2, inv2 = ln(h1_ref[...])
    s_ref[2:3, :] = col(dm * s2); s_ref[3:4, :] = col(dm)
    dmid = dout + ln_back(dm, s2, inv2, enc_vec(v_ref, 2))
    bl = dmid.astype(bf16)
    gwide_ref[:, 3 * D:] = bl
    do = dot(bl, wr_ref[:, OUT], NT).astype(bf16)
    n = do.shape[0] // clips
    for c in range(clips):
        rows = slice(c * n, (c + 1) * n)
        for p in range(HEADS // 2):
            dop = do[rows, p * 128:(p + 1) * 128]
            dqs, dk, dv = [], None, None
            for hd in range(2):
                q, k, v, qh, own, prob = enc_scores(qkv_ref, rows, p, hd, seen)
                doh = jnp.where(own, dop, jnp.zeros_like(dop))
                dpr = dot(doh, v, NT)
                ds = (prob * (dpr - jnp.sum(dpr * prob, axis=1, keepdims=True))).astype(bf16)
                dqs.append(dot(ds, k, NN))
                x, y = dot(ds, qh, TN), dot(prob.astype(bf16), doh, TN)
                dk = x if dk is None else dk + x
                dv = y if dv is None else dv + y
            lane = lax.broadcasted_iota(jnp.int32, (1, 128), 1)
            dq = jnp.where(lane < 64, dqs[0], dqs[1])
            gwide_ref[rows, p * 128:(p + 1) * 128] = (dq * 0.125).astype(bf16)
            gwide_ref[rows, D + p * 128:D + (p + 1) * 128] = (dk * 0.125).astype(bf16)
            gwide_ref[rows, 2 * D + p * 128:2 * D + (p + 1) * 128] = dv.astype(bf16)
    da = dot(gwide_ref[:, :3 * D], wr_ref[:, QKV], NT)
    s1, inv1 = ln(h_ref[...])
    s_ref[0:1, :] = col(da * s1); s_ref[1:2, :] = col(da)
    s_ref[7:8, :] = jnp.zeros_like(s_ref[7:8, :])
    gin = (dmid + ln_back(da, s1, inv1, enc_vec(v_ref, 0))).astype(bf16)
    gin_ref[...] = gin
    for at, y in enumerate((gin, dl, gwide_ref[:, :3 * D], bl, din)):
        most_ref[at:at + 1, :] = jnp.broadcast_to(most(y).reshape(1, 1), (1, 128))

def enc_bwd(dp, h, qkv, h1, inner, enc, wr, wc, vec, clips, seen):
    n = h.shape[0]
    shapes = [((n, D), bf16), ((n, FF), bf16), ((n, 4 * D), bf16), ((n, D), bf16), ((8, D), f32), ((1, FF), f32), ((8, 128), f32)]
    ins = (dp, h, qkv, h1, inner, enc, wr, wc, vec)
    return pl.pallas_call(functools.partial(enc_bwd_body, clips, seen),
        in_specs=[whole(a.shape) for a in ins],
        out_specs=[whole(s) for s, _ in shapes], out_shape=[jax.ShapeDtypeStruct(s, d) for s, d in shapes],
        compiler_params=pltpu.CompilerParams(vmem_limit_bytes=62 << 20), name="enc_backward",
        cost_estimate=pl.CostEstimate(flops=2 * n * 8552448, transcendentals=n * FF, bytes_accessed=28 << 20),
    )(*ins)

def pair_body(al_ref, bl_ref, ar_ref, br_ref, o_ref):
    o_ref[...] = dot(al_ref[0], ar_ref[0], TN) + dot(bl_ref[0], br_ref[0], TN)

def pair_product(lefts, rights, rows, cols, bm, bn, left_at, right_at, name):
    n = lefts[0].shape[1]
    ls = pl.BlockSpec((1, n, bm), lambda i, j: left_at(i, j))
    rs = pl.BlockSpec((1, n, bn), lambda i, j: right_at(i, j))
    return pl.pallas_call(pair_body, grid=(rows // bm, cols // bn), in_specs=[ls, ls, rs, rs],
        out_specs=pl.BlockSpec((bm, bn), lambda i, j: (i, j)), out_shape=jax.ShapeDtypeStruct((rows, cols), f32),
        compiler_params=pltpu.CompilerParams(vmem_limit_bytes=60 << 20), name=name,
        cost_estimate=pl.CostEstimate(flops=4 * n * rows * cols, transcendentals=0, bytes_accessed=4 * rows * cols),
    )(lefts[0], lefts[1], rights[0], rights[1])
def dec_parts(dec_low_rows, dec_low_fc2):
    mats = (
        dec_low_rows[:, : 3 * DD],
        dec_low_rows[:, 3 * DD : 4 * DD],
        dec_low_rows[:, 4 * DD : 4 * DD + DFF],
        dec_low_fc2,
    )
    return (mats, dec_low_rows[:, 4 * DD + DFF :])


def adam_update(master, moment_one, moment_two, gradient):
    new_one = beta_one * moment_one + (1.0 - beta_one) * gradient
    new_two = beta_two * moment_two + (1.0 - beta_two) * gradient * gradient
    stepped = new_one / bias_fix_one / (jnp.sqrt(new_two / bias_fix_two) + adam_eps)
    return (master - learn_rate * (stepped + decay_rate * master), new_one, new_two)


BLOCK = 480


def sinusoid_at(places, feat_width):
    column = jnp.arange(feat_width)
    expo = (2 * (column // 2)).astype(jnp.float32) / feat_width
    angles = places.astype(jnp.float32)[..., None] / jnp.power(jnp.float32(10000.0), expo)
    return jnp.where(column % 2 == 0, jnp.sin(angles), jnp.cos(angles))


def bit_of(name, hop):
    return (lax.axis_index(name) // hop) % 2


def swap(value, name, size, hop):
    return lax.ppermute(value, name, [(i, i ^ hop) for i in range(size)])


def total_everywhere(value, sizes, combine=jnp.add):
    for name, size in sizes:
        hop = 1
        while hop < size:
            value = combine(value, swap(value, name, size, hop))
            hop *= 2
    return value


def keep_and_send(value, dim, bit):
    half = value.shape[dim] // 2
    kept = lax.dynamic_slice_in_dim(value, bit * half, half, dim)
    sent = lax.dynamic_slice_in_dim(value, (1 - bit) * half, half, dim)
    return kept, sent


def join(mine, other, dim, bit):
    return jnp.where(
        bit == 0, jnp.concatenate([mine, other], axis=dim), jnp.concatenate([other, mine], axis=dim)
    )


def split_view(value, shard, ways):
    rows = value.shape[0] // shard
    return value.reshape((shard,) + (2,) * ways + (rows >> ways, value.shape[1]))


class Links:
    def __init__(self, rep, shard):
        self.rep, self.shard = rep, shard
        self.ways = min(3, rep.bit_length() - 1)
        self.inner = [("rep", 1 << k) for k in range(self.ways)]
        self.outer = [("rep", 1 << k) for k in range(self.ways, rep.bit_length() - 1)]
        self.owners = [("shard", 1 << k) for k in reversed(range(shard.bit_length() - 1))]
        self.sizes = (("rep", rep), ("shard", shard))

    def size(self, name):
        return self.rep if name == "rep" else self.shard

    def swap(self, value, hop):
        return swap(value, hop[0], self.size(hop[0]), hop[1])

    def dim(self, hop, core):
        return 0 if hop[0] == "shard" else hop[1].bit_length() - (not core)

    def reduce(self, parts, scales, turns, core):
        parts = list(parts)
        first = self.inner[:1] if core else []
        rest = self.inner[1:] + self.owners[:1]
        orders = []
        for turn in turns:
            turn = turn % len(rest)
            orders.append(first + rest[turn:] + rest[:turn] + self.owners[1:])
        for step in range(len(orders[0])):
            held, moving = [], []
            for part, scale, order in zip(parts, scales, orders):
                hop = order[step]
                kept, sent = keep_and_send(part, self.dim(hop, core), bit_of(*hop))
                if scale is not None:
                    sent = (sent * scale).astype(jnp.float16)
                held.append(kept)
                moving.append(self.swap(sent, hop))
            moving = yield moving
            for at, (kept, came) in enumerate(zip(held, moving)):
                if scales[at] is not None:
                    came = came.astype(jnp.float32) * (1.0 / scales[at])
                parts[at] = kept + came
        for hop in self.outer:
            mine = [
                part if scale is None else lax.optimization_barrier((part * scale).astype(jnp.float16))
                for part, scale in zip(parts, scales)
            ]
            other = yield [self.swap(part, hop) for part in mine]
            for at, scale in enumerate(scales):
                if scale is None:
                    parts[at] = mine[at] + other[at]
                else:
                    both = mine[at].astype(jnp.float32) + other[at].astype(jnp.float32)
                    parts[at] = both * (1.0 / scale)
        return parts

    def spread(self, pieces, turns, core):
        pieces = list(pieces)
        rest = self.inner[1:]
        orders = []
        for turn in turns:
            turn = turn % len(rest) if rest else 0
            orders.append(rest[turn:] + rest[:turn] + (self.inner[:1] if core else []))
        for step in range(len(orders[0])):
            moving = yield [self.swap(piece, order[step]) for piece, order in zip(pieces, orders)]
            pieces = [
                join(piece, came, self.dim(order[step], core), bit_of(*order[step]))
                for piece, came, order in zip(pieces, moving, orders)
            ]
        return pieces

    def own_block(self, view):
        for hop in self.inner:
            view, _ = keep_and_send(view, self.dim(hop, True), bit_of(*hop))
        return view


class Steps:
    def __init__(self, generator):
        self.generator, self.flight, self.result = generator, None, None
        self.step()

    def step(self):
        if self.result is None:
            try:
                self.flight = self.generator.send(self.flight)
            except StopIteration as end:
                self.flight, self.result = None, end.value


def arrive(steps, value=()):
    steps = [each for each in steps if each.result is None]
    value, flights = lax.optimization_barrier((value, [each.flight for each in steps]))
    for each, flight in zip(steps, flights):
        each.flight = flight
        each.step()
    return value


def complete(*steps):
    while any(each.result is None for each in steps):
        arrive(steps)
    return [each.result for each in steps]


def one_hop(links, values, hop):
    return (yield [links.swap(value, hop) for value in values])


def over_all(links, value, combine, skip=()):
    for name, size in links.sizes:
        for k in range(size.bit_length() - 1):
            if (name, 1 << k) not in skip:
                other = yield links.swap(value, (name, 1 << k))
                value = combine(value, other)
    return value


def from_owners(links, owned, fars):
    size = links.shard
    return (
        yield [
            [lax.ppermute(own, "shard", [(i, (i + far) % size) for i in range(size)]) for own in owned] for far in fars
        ]
    )


def assembled(own, parts, me):
    parts = [part.reshape(own.shape) for part in parts]
    if len(parts) == 1:
        return join(own, parts[0], 0, me)
    whole = jnp.zeros((len(parts) + 1,) + own.shape, own.dtype)
    for far, part in enumerate([own] + parts):
        whole = lax.dynamic_update_slice_in_dim(whole, part[None], (me - far) % (len(parts) + 1), 0)
    return whole.reshape((-1,) + own.shape[1:])


def half_of(value, bit):
    size = value.shape[-1] // 2
    return lax.dynamic_slice_in_dim(value, bit * size, size, value.ndim - 1)


def local(mesh_shape, clips, visible_idx, masked_idx, loss_counts, *state):
    masters, firsts, seconds = state[:5], state[5:10], state[10:]
    seq_count, tube_count, _ = clips.shape
    seen_count = visible_idx.shape[1]
    hidden_count = masked_idx.shape[1]
    query_rows = -(-hidden_count // BLOCK) * BLOCK
    seen_rows = -(-seen_count // 16) * 16
    rep, shard = mesh_shape["rep"], mesh_shape["shard"]
    links = Links(rep, shard)
    me = lax.axis_index("shard")

    views = [split_view(master, 1, links.ways) for master in masters[:4]]
    blocks = [links.own_block(view).astype(jnp.bfloat16) for view in views]
    vec_own = masters[4].astype(jnp.bfloat16).reshape(1, -1)
    fars = range(1, shard)
    first = Steps(from_owners(links, blocks[:2] + [vec_own], fars))
    counts = Steps(over_all(links, jnp.sum(loss_counts).astype(jnp.float32).reshape(1), jnp.add))

    seen_idx = jnp.pad(visible_idx, ((0, 0), (0, seen_rows - seen_count)), constant_values=-1)
    hidden_idx = jnp.pad(masked_idx, ((0, 0), (0, query_rows - hidden_count)), constant_values=-1)
    seen_pixels = None
    for clip in range(seq_count):
        seen_pixels = pick_rows(clips, seen_idx, seen_rows, clip, "pick_seen", seen_pixels)
    lows = [master.astype(jnp.bfloat16) for master in masters[:4]]
    seen_pixels, lows, hidden_idx, dec_blocks = arrive([first, counts], (seen_pixels, lows, hidden_idx, blocks[2:]))
    enc_came = [came[:2] for came in first.result]
    vec_parts = [came[2] for came in first.result]
    share = Steps(links.spread([block for came in enc_came for block in came], (0, 1) * len(fars), True))
    second = Steps(from_owners(links, dec_blocks, fars))

    pixels = None
    for clip in range(seq_count):
        pixels = pick_rows(clips, hidden_idx, BLOCK, clip, "pick_hidden", pixels)
        if clip == 0:
            pixels, hidden_idx, visible_idx, masked_idx, vec_own, vec_parts = arrive(
                [share, counts, second], (pixels, hidden_idx, visible_idx, masked_idx, vec_own, vec_parts)
            )
    dec_share = Steps(links.spread([block for came in second.result for block in came], (0, 1) * len(fars), True))
    vec = assembled(vec_own, vec_parts, me).reshape(1, -1).astype(jnp.float32)
    token = vec[:, DEC_VEC - DD : DEC_VEC]
    place = (
        jnp.pad(sinusoid_at(visible_idx, D), ((0, 0), (0, seen_rows - seen_count), (0, 0))),
        jnp.concatenate([sinusoid_at(masked_idx, DD) + token, sinusoid_at(visible_idx, DD)], axis=1),
    )
    pixels, place = arrive([share, counts, dec_share], (pixels, place))
    place = arrive([share, counts, dec_share], place)
    flat = lambda whole: whole.reshape(-1, whole.shape[-1])
    enc_low_rows, enc_low_cols = [
        flat(assembled(lows[at], share.result[at :: 2], me)) for at in (0, 1)
    ]
    (enc_h, enc_qkv, enc_mid, enc_inner, encoded, projected, tall, pair, normed_two, latent, left_most) = enc_fwd(
        seen_pixels.reshape(-1, PATCH), place[0].reshape(-1, D), enc_low_rows, enc_low_cols, vec, seq_count, seen_count
    )
    core = links.inner[0]
    left_swap = Steps(one_hop(links, (tall, pair, normed_two), core))
    complete(dec_share)
    projected = arrive([counts], projected)
    count_sum = complete(counts)[0][0]
    dec_low_rows, u_down = [flat(assembled(lows[2 + at], dec_share.result[at::2], me)) for at in (0, 1)]
    (u_qkv, u_out, u_up, _), w_head = dec_parts(dec_low_rows, u_down)

    projected = projected.reshape(seq_count, seen_rows, DD)[:, :seen_count]
    hidden = place[1].at[:, hidden_count:].add(projected)
    qkv = dec_qkv(hidden, u_qkv, vec, tube_count // 2)
    mixed, log_sums = attn_fwd(qkv, DHEADS, query_rows, BLOCK)
    log_sums = arrive([left_swap], log_sums)
    far_lefts = left_swap.result
    (middle_grad, mixed_grad, grad_row_part, grad_dec_fc2, narrow_grads, wide_grads, loss_part) = dec_post(
        loss_counts, (2.0 / (PATCH * count_sum)).reshape(1), hidden, mixed, pixels,
        u_out, u_up, u_down, w_head, vec, BLOCK,
    )
    view = functools.partial(split_view, shard=shard, ways=links.ways)
    dec_flight = Steps(links.reduce([view(grad_row_part), view(grad_dec_fc2)], (None, None), (0, 1), True))
    input_grads, before = [], [jnp.zeros((DD, 3 * DD), jnp.float32), jnp.zeros((8, DD), jnp.float32)]
    parts = [[], []]
    for clip in range(seq_count):
        for pair_at in range(DHEADS // 2):
            parts[clip] += attn_bwd(qkv, mixed_grad, log_sums, DHEADS, query_rows, BLOCK, clip, pair_at)
            log_sums = arrive([dec_flight], log_sums)
        back = dec_qkv_back(
            hidden, parts[clip], middle_grad, u_qkv, vec, hidden_count, tube_count // 2, clip, before
        )
        input_grads.append(back[0])
        before = back[1:]
    grad_qkv, one_grads = before
    dec_sums = complete(dec_flight)[0]

    proj_grad = jnp.concatenate([grad[:, hidden_count:] for grad in input_grads], axis=0)
    proj_grad = jnp.pad(proj_grad, ((0, 0), (0, seen_rows - seen_count), (0, 0))).reshape(-1, DD)
    grad_proj = product_tn(latent, proj_grad)
    late = Steps(links.reduce([view(grad_qkv), view(grad_proj)], (None, None), (0, 1), True))
    proj_grad = arrive([late], proj_grad)
    dec_spread = Steps(links.spread(dec_sums, (0, 1), True))
    grad_down, grad_up, grad_wide, grad_in, enc_sums, up_sums, right_most = enc_bwd(
        proj_grad, enc_h, enc_qkv, enc_mid, enc_inner, encoded, enc_low_rows, enc_low_cols, vec, seq_count, seen_count
    )
    grad_vectors = jnp.concatenate(
        [enc_sums[at] for at in range(6)] + [up_sums[0], enc_sums[6], one_grads[2], one_grads[0], one_grads[1]]
        + [narrow_grads[0], narrow_grads[1], narrow_grads[2], narrow_grads[3], wide_grads[0], narrow_grads[4], wide_grads[1]]
    )

    bit = bit_of(*core)
    grad_up, grad_wide, grad_in, grad_down, right_most, grad_vectors = arrive(
        [late, dec_spread], (grad_up, grad_wide, grad_in, grad_down, right_most, grad_vectors)
    )
    shape_right = lambda b: (
        half_of(grad_up, b)[None],
        jnp.concatenate([half_of(grad_wide[:, : 3 * D], b), half_of(grad_wide[:, 3 * D :], b)], axis=1)[None],
        jnp.stack([half_of(grad_in, b), half_of(grad_down, b)]),
    )
    right_swap = Steps(one_hop(links, shape_right(1 - bit), core))
    rights = shape_right(bit)
    norms = jnp.sqrt(left_most[:5, 0] * right_most[:5, 0])
    bounds = jnp.stack([norms[4], jnp.maximum(norms[2], norms[3]), jnp.maximum(norms[0], norms[1])])
    size = grad_vectors.shape[0]
    is_sum = lax.broadcasted_iota(jnp.int32, (1, size + 128), 1) < size + 1
    message = jnp.concatenate([grad_vectors, loss_part[0], bounds, jnp.zeros(124, jnp.float32)]).reshape(1, -1)
    vector_flight = Steps(over_all(links, message, lambda x, y: jnp.where(is_sum, x + y, jnp.maximum(x, y))))
    rights = arrive([right_swap, vector_flight, late, dec_spread], rights)
    far_rights = right_swap.result
    wide_cols, tall_rows = 2 * D, PATCH + FF
    zero = lambda i, j: (0, 0, i)
    hops = [vector_flight, late, dec_spread]
    sum_up = pair_product(
        (normed_two[None], far_lefts[2][None]), (rights[0], far_rights[0]), D, wide_cols, D, D // 2,
        zero, lambda i, j: (0, 0, j), "grad_up",
    )
    sum_up, rights = arrive(hops, (sum_up, rights))
    sum_wide = pair_product(
        (pair, far_lefts[1]), (rights[1], far_rights[1]), D, wide_cols, D, D // 2,
        lambda i, j: (j // 3, 0, i), lambda i, j: (0, 0, j), "grad_wide",
    )
    sum_wide, rights = arrive(hops, (sum_wide, rights))
    sum_tall = pair_product(
        (tall[None], far_lefts[0][None]), (rights[2], far_rights[2]), tall_rows, D // 2, D, D // 2,
        zero, lambda i, j: (jnp.minimum(i // 2, 1), 0, j), "grad_tall",
    )
    sum_up, sum_wide, sum_tall = arrive(hops, (sum_up, sum_wide, sum_tall))
    totals = complete(*hops)[0]
    vector_sum, loss_sum = totals[0, :size], totals[0, size]
    bounds = totals[0, size + 1 : size + 4] * (2.0 * rep * shard)
    scales = list(jnp.exp2(jnp.floor(15.0 - jnp.log2(jnp.maximum(bounds, 1e-30)))))
    slim = functools.partial(split_view, shard=shard, ways=links.ways - 1)
    enc_flight = Steps(links.reduce([slim(sum_up), slim(sum_wide), slim(sum_tall)], scales, (0, 1, 2), False))
    late_sums = late.result
    late_spread = Steps(links.spread(late_sums, (0, 1), True))
    while enc_flight.result is None:
        arrive([enc_flight, late_spread])
    complete(late_spread)
    enc_parts_sum = enc_flight.result

    lowered = [(part * scale).astype(jnp.float16) for part, scale in zip(enc_parts_sum, scales)]
    enc_spread = Steps(links.spread(lowered, (0, 0, 1), False))
    squares = jnp.float32(0.0)
    for part in enc_parts_sum + dec_sums + late_sums:
        squares = squares + jnp.sum(part * part)
    norm = Steps(over_all(links, squares.reshape(1), jnp.add, links.outer))
    while enc_spread.result is None:
        arrive([norm])
        arrive([norm, enc_spread])
    everyone = complete(norm)[0]
    loss = loss_sum / count_sum
    grad_norm = jnp.sqrt(everyone[0] + jnp.sum(vector_sum * vector_sum))
    factor = jnp.minimum(jnp.float32(1.0), lax.rsqrt(count_sum) / grad_norm)

    flat_piece = lambda piece: piece.reshape(-1, piece.shape[-1])
    dec_rows_sum, dec_fc2_sum, dec_qkv_sum, proj_sum = [
        flat_piece(piece) for piece in dec_spread.result + late_spread.result
    ]
    halves = [flat_piece(piece) for piece in enc_spread.result]
    other = [links.swap(half, core) for half in halves]

    def sided(mine, yours):
        return jnp.where(bit == 0, jnp.concatenate([mine, yours], 1), jnp.concatenate([yours, mine], 1))

    wide_parts = []
    for at, (lo, hi) in enumerate(((0, 3 * D // 2), (3 * D // 2, 2 * D))):
        wide_parts.append(sided(halves[1][:, lo:hi], other[1][:, lo:hi]).astype(jnp.float32) * (1.0 / scales[1]))
    grads = [
        jnp.concatenate(
            wide_parts + [sided(halves[0], other[0]).astype(jnp.float32) * (1.0 / scales[0]), proj_sum], axis=1
        ),
        sided(halves[2], other[2]).astype(jnp.float32) * (1.0 / scales[2]),
        jnp.concatenate([dec_qkv_sum, dec_rows_sum], axis=1),
        dec_fc2_sum,
        lax.dynamic_slice_in_dim(vector_sum, me * masters[4].shape[0], masters[4].shape[0]),
    ]
    new_w, new_m, new_v = [], [], []
    for index in range(5):
        updated = adam_update(masters[index], firsts[index], seconds[index], grads[index] * factor)
        new_w.append(updated[0])
        new_m.append(updated[1])
        new_v.append(updated[2])
    return (loss, grad_norm, *new_w, *new_m, *new_v, *[w.astype(jnp.bfloat16) for w in new_w])


def solution(mesh):
    both, one = ("rep", "shard"), "shard"
    held = (P(one, None), P(one, None), P(one, None), P(one, None), P(one))
    in_specs = (P(both, None, None), P(both, None), P(both, None), P(both)) + held * 3
    out_specs = (P(), P()) + held * 4
    return jax.shard_map(
        functools.partial(local, dict(mesh.shape)),
        mesh=mesh, in_specs=in_specs, out_specs=out_specs, check_vma=False,
    )
```

time: 2240 us -> 969 us (0.43)
  matrix products: 891 us -> 0.5 us
  waiting for transfers between devices: 732 us -> 141 us
  Pallas kernels: 0 us -> 389 us
  starting transfers between devices: 0.37 us -> 129 us
  blocking collectives: 123 us -> 0 us
  local copies, waits for them, and re-layouts: 175 us -> 54.5 us
  other arithmetic: 276 us -> 223 us
    dot_general x57 -> x0, matrix products: 847 us -> none  [the longest x6 232 us: attend_backward(): jnp.einsum('hqk,khd->qhd', score_grad, keys_all, preferred_element_type=j...]
    pallas_call x0 -> x20, Pallas kernels: none -> 389 us  [the longest x6 116 us: attn_bwd(): pl.pallas_call(functools.partial(bwd_body, 64 ** (-0.5), nb, 0), grid=(1,...]
    reduce_scatter x4 -> x0, waiting for transfers between devices: 380 us -> none  [the longest x1 227 us: local(): lax.psum_scatter(grad_enc_rows, 'shard', scatter_dimension=0, tiled=True)]
    psum x1 -> x0, waiting for transfers between devices: 303 us -> none  [local(): lax.psum((enc_reduced[0], enc_reduced[1], dec_reduced[0], dec_reduced[1],...]
    ppermute x0 -> x90, waiting for transfers between devices: none -> 141 us  [the longest x85 141 us: swap(): return lax.ppermute(value, name, [(i, i ^ hop) for i in range(size)])]
    ppermute x0 -> x90, starting transfers between devices: none -> 129 us  [the longest x85 122 us: swap(): return lax.ppermute(value, name, [(i, i ^ hop) for i in range(size)])]
    gather x9 -> x0, local copies, waits for them, and re-layouts: 109 us -> none  [the longest x3 74.3 us: local(): jnp.take_along_axis(clips, masked_idx[:, :, None], axis=1)]
    psum x3 -> x0, blocking collectives: 108 us -> none  [the longest x1 63 us: local(): lax.psum((enc_reduced[0], enc_reduced[1], dec_reduced[0], dec_reduced[1],...]
  transfers between devices with their start and end apart: 9 -> 90, of which waited for: 5 -> 22; matrix products, arithmetic and copies ran while one was open for 41% -> 21% of each run, Pallas kernels for 0% -> 35%
where the time goes in v1:
time: 969 us; the launch traced here: 959 us
  Pallas kernels  389 us (40%)
  other arithmetic  223 us (23%)
  waiting for transfers between devices  141 us (15%)
  starting transfers between devices  129 us (13%)
  local copies, waits for them, and re-layouts  54.5 us (6%)
  between operations  22.3 us (2%)
    ppermute x85, waiting for transfers between devices, swap(): return lax.ppermute(value, name, [(i, i ^ hop) for i in range(size)])  141 us
    ppermute x85, starting transfers between devices, swap(): return lax.ppermute(value, name, [(i, i ^ hop) for i in range(size)])  122 us
    pallas_call x6, Pallas kernels, attn_bwd(): pl.pallas_call(functools.partial(bwd_body, 64 ** (-0.5), nb, 0), grid=(1,...  116 us
    pallas_call x1, Pallas kernels, attn_fwd(): pl.pallas_call(body, grid=(clips, pairs, nb), in_specs=[pl.BlockSpec((1,...  70.5 us
    pallas_call x1, Pallas kernels, dec_post(): pl.pallas_call(functools.partial(post_body, nb, R, keys), grid=(clips, nb...  66.5 us
    convert_element_type x5, other arithmetic, local(): w.astype(jnp.bfloat16)  57.1 us
    select_n x33, other arithmetic, join(): jnp.where(bit == 0, jnp.concatenate([mine, other], axis=dim), jnp.concate...  52 us
    pallas_call x4, Pallas kernels, pick_rows(): pl.pallas_call(pick_body, grid=(m // R,), in_specs=[pl.BlockSpec((1, R, 1...  33.6 us
  transfers between devices with their start and end apart: 90, of which 22 were waited for; matrix products, arithmetic and copies ran while one was open for 21% of the time, Pallas kernels for 35%

profile of v1, /device:TPU:0, one launch (start us, length us, event | category | flops | bytes accessed | tf_op | source)
XLA Modules:
  0.0 959.5 jit_solution(5315160085512629361)
XLA Ops:
  0.8 2.3 dynamic-slice_convert_fusion
  3.1 3.0 collective-permute-start
  18.2 4.3 pick_seen_0.1.refs_0_
  22.5 4.5 pick_seen_1.1
  27.5 6.8 convert_element_type.180
  46.6 12.3 %pick_hidden_0.1.refs_0_ = bf16[2,1440,1536]{2,1,0:T(8,128)(2,1)} custom-call(s32[2,1440,1]{2,1,0:T(8,128)} %copy.80.idx_ref, bf16[2,1568,1536]{2,1,0:T(8,128)(2,1)} %x_ref.7), custom_call_target="tpu_custom_call" | custom-call | flops 11314285568 | tf_op jit(solution)/shard_map/pick_hidden_0/pallas_call | solution.py:299
  70.5 22.4 %collective-permute-start.11 = (f32[1]{0:T(128)}, f32[1]{0:T(128)}, u32[]{:S(2)}, u32[]{:S(2)}) collective-permute-start(f32[1]{0:T(128)} %add.533), channel_id=1, source_target_pairs={{0,8},{2,10},{4,12},{6,14},{8,0},{10,2},{12,4},{14,6},{16,24},{18,... | collective-permute-start | bytes 20 | tf_op jit(solution)/shard_map/ppermute | solution.py:485
  95.1 12.5 %pick_hidden_1.1.t_ref = bf16[2,1440,1536]{2,1,0:T(8,128)(2,1)} custom-call(s32[2,1440,1]{2,1,0:T(8,128)} %copy.81.idx_ref, bf16[2,1568,1536]{2,1,0:T(8,128)(2,1)} %x_ref.7, bf16[2,1440,1536]{2,1,0:T(8,128)(2,1)} %pick_hidden_0.1.refs_0_), custom_call_target="tpu_custom_call", output_to_operand_aliasing={{}: (2, {})} | custom-call | flops 11314285568 | tf_op jit(solution)/shard_map/pick_hidden_1/pallas_call | solution.py:299
  109.4 26.4 %select_add_fusion = f32[2,1411,384]{2,1,0:T(8,128)S(1)} fusion(f32[384]{0:T(512)S(1)} %slice_reduce_fusion.9, f32[384]{0:T(512)S(1)} %copy-done.58, f32[2,1411]{1,0:T(2,128)S(1)} %convert_element_type.192, pred[384]{0:T(512)(128)(4,1)S(1)} %copy-done.71), kind=kLoop, calls=%fused_computation.16 | loop fusion | flops 3250944 | bytes 4349336 | tf_op jit(solution)/shard_map/add | solution.py:697
  135.8 2.5 pad_maximum_fusion
  139.9 3.5 cosine_select_fusion
  148.0 3.0 maximum_select_fusion.9
  152.1 4.0 collective-permute-start.16
  158.4 3.1 collective-permute-done.18
  161.5 6.0 collective-permute-done.17
  167.5 3.5 maximum_select_fusion.2
  171.0 3.8 maximum_select_fusion.3
  178.1 11.3 %maximum_select_fusion.wr_ref = bf16[768,6528]{1,0:T(8,128)(2,1)} fusion(bf16[384,6528]{1,0:T(8,128)(2,1)S(1)} %bitcast.131, bf16[384,6528]{1,0:T(8,128)(2,1)S(1)} %bitcast.130, pred[]{:T(512)S(6)} %eq.133), kind=kLoop, calls=%fused_computation.3 | loop fusion | flops 45121536 | bytes 20054016 | tf_op jit(solution)/shard_map/jit(_where)/select_n | solution.py:505
  189.5 4.5 maximum_select_fusion.1.wc_ref
  194.0 19.0 %enc_forward.1 = (f32[320,768]{1,0:T(8,128)}, bf16[320,2304]{1,0:T(8,128)(2,1)}, f32[320,768]{1,0:T(8,128)}, f32[320,3072]{1,0:T(8,128)}, f32[320,768]{1,0:T(8,1...) custom-call(bf16[320,1536]{1,0:T(8,128)(2,1)} %bitcast.149, ...), custom_call_target="tpu_custom_call" | custom-call | flops 5473566720 | bytes 27262976 | tf_op jit(solution)/shard_map/enc_forward/pallas_call | solution.py:375
  223.5 9.4 dec_qkv.1.q_ref.k_ref.v_ref
  232.9 70.5 %dec_attend_forward.1 = (bf16[2,1440,384]{2,1,0:T(8,128)(2,1)}, f32[6,3,2,480]{3,2,1,0:T(2,128)}) custom-call(bf16[2,1568,1152]{2,1,0:T(8,128)(2,1)} %dec_qkv.1.q_ref.k_ref.v_ref, bf16[2,1568,1152]{2,1,0:T(8,128)(2,1)} %dec_qkv.1.q_ref.k_ref.v_ref, bf16[2,1568,1152]{2,1,0:T(8,128)(2,1)} %dec_qkv.1.q_ref.k_ref.v_ref), custom_call_target="tpu_custom_call" | custom-call | flops 76999999488 | tf_op jit(solution)/shard_map/dec_attend_forward/pallas_call | solution.py:67
  306.1 66.5 %dec_post.1 = (f32[2,1568,384]{2,1,0:T(8,128)}, bf16[2,1440,384]{2,1,0:T(8,128)(2,1)}, f32[384,3456]{1,0:T(8,128)}, f32[1536,384]{1,0:T(8,128)}, f32[8,384]{1,0:...) custom-call(s32[2]{0:T(128)} %cnt_ref.1, f32[1]{0:T(128)} %bitcast.20.inv_ref, f32[2,1568,384]{2,1,0:T(8,128)} %scatter-add.4.h_ref, ...), custom_call_target="tpu_custom_call" | custom-call | flops 73699999744 | tf_op jit(solution)/shard_map/dec_post/pallas_call | solution.py:233
  376.3 2.4 constant_dynamic-slice_fusion.18
  380.8 19.4 %dec_attend_backward_0_0.1 = (bf16[1,1568,128]{2,1,0:T(8,128)(2,1)}, bf16[1,1568,128]{2,1,0:T(8,128)(2,1)}, bf16[1,1568,128]{2,1,0:T(8,128)(2,1)}) custom-call(bf16[2,1568,1152]{2,1,0:T(8,128)(2,1)} %dec_qkv.1.q_ref.k_ref.v_ref, bf16[2,1568,1152]{2,1,0:T(8,128)(2,1)} %dec_qkv.1.q_ref.k_ref.v_ref, bf16[2,1568,1152]{2,1,0:T(8,128)(2,1)} %dec_qkv.1.q_ref.k_ref.v_ref, ...), custom_call_target="tpu_custom_call" | custom-call | flops 18699999232 | tf_op jit(solution)/shard_map/dec_attend_backward_0_0/pallas_call | solution.py:132
  400.2 2.8 dynamic-slice_add_fusion
  408.5 19.2 %dec_attend_backward_0_1.1 = (bf16[1,1568,128]{2,1,0:T(8,128)(2,1)}, bf16[1,1568,128]{2,1,0:T(8,128)(2,1)}, bf16[1,1568,128]{2,1,0:T(8,128)(2,1)}) custom-call(bf16[2,1568,1152]{2,1,0:T(8,128)(2,1)} %dec_qkv.1.q_ref.k_ref.v_ref, bf16[2,1568,1152]{2,1,0:T(8,128)(2,1)} %dec_qkv.1.q_ref.k_ref.v_ref, bf16[2,1568,1152]{2,1,0:T(8,128)(2,1)} %dec_qkv.1.q_ref.k_ref.v_ref, ...), custom_call_target="tpu_custom_call" | custom-call | flops 18699999232 | tf_op jit(solution)/shard_map/dec_attend_backward_0_1/pallas_call | solution.py:132
  427.7 7.1 collective-permute-done.27
  434.8 19.5 %dec_attend_backward_0_2.1 = (bf16[1,1568,128]{2,1,0:T(8,128)(2,1)}, bf16[1,1568,128]{2,1,0:T(8,128)(2,1)}, bf16[1,1568,128]{2,1,0:T(8,128)(2,1)}) custom-call(bf16[2,1568,1152]{2,1,0:T(8,128)(2,1)} %dec_qkv.1.q_ref.k_ref.v_ref, bf16[2,1568,1152]{2,1,0:T(8,128)(2,1)} %dec_qkv.1.q_ref.k_ref.v_ref, bf16[2,1568,1152]{2,1,0:T(8,128)(2,1)} %dec_qkv.1.q_ref.k_ref.v_ref, ...), custom_call_target="tpu_custom_call" | custom-call | flops 18699999232 | tf_op jit(solution)/shard_map/dec_attend_backward_0_2/pallas_call | solution.py:132
  461.7 11.7 %dec_qkv_back_0.1 = (bf16[1,1568,384]{2,1,0:T(8,128)(2,1)}, f32[384,1152]{1,0:T(8,128)}, f32[8,384]{1,0:T(8,128)}) custom-call(f32[2,1568,384]{2,1,0:T(8,128)} %scatter-add.4.h_ref, f32[2,1568,384]{2,1,0:T(8,128)} %get-tuple-element.257.dmid_ref, bf16[384,1152]{1,0:T(8,128)(2,1)} %slice.204.w_ref, f32[1,14592]{1,0:T(1,128)} %bitcast.177, ...), custom_call_target="tpu_custom_call" | custom-call | flops 11000000512 | tf_op jit(solution)/shard_map/dec_qkv_back_0/pallas_call | solution.py:284
  478.5 19.3 %dec_attend_backward_1_0.1 = (bf16[1,1568,128]{2,1,0:T(8,128)(2,1)}, bf16[1,1568,128]{2,1,0:T(8,128)(2,1)}, bf16[1,1568,128]{2,1,0:T(8,128)(2,1)}) custom-call(bf16[2,1568,1152]{2,1,0:T(8,128)(2,1)} %dec_qkv.1.q_ref.k_ref.v_ref, bf16[2,1568,1152]{2,1,0:T(8,128)(2,1)} %dec_qkv.1.q_ref.k_ref.v_ref, bf16[2,1568,1152]{2,1,0:T(8,128)(2,1)} %dec_qkv.1.q_ref.k_ref.v_ref, ...), custom_call_target="tpu_custom_call" | custom-call | flops 18699999232 | tf_op jit(solution)/shard_map/dec_attend_backward_1_0/pallas_call | solution.py:132
  498.3 2.7 collective-permute-start.34
  501.0 19.2 %dec_attend_backward_1_1.1 = (bf16[1,1568,128]{2,1,0:T(8,128)(2,1)}, bf16[1,1568,128]{2,1,0:T(8,128)(2,1)}, bf16[1,1568,128]{2,1,0:T(8,128)(2,1)}) custom-call(bf16[2,1568,1152]{2,1,0:T(8,128)(2,1)} %dec_qkv.1.q_ref.k_ref.v_ref, bf16[2,1568,1152]{2,1,0:T(8,128)(2,1)} %dec_qkv.1.q_ref.k_ref.v_ref, bf16[2,1568,1152]{2,1,0:T(8,128)(2,1)} %dec_qkv.1.q_ref.k_ref.v_ref, ...), custom_call_target="tpu_custom_call" | custom-call | flops 18699999232 | tf_op jit(solution)/shard_map/dec_attend_backward_1_1/pallas_call | solution.py:132
  520.4 19.4 %dec_attend_backward_1_2.1 = (bf16[1,1568,128]{2,1,0:T(8,128)(2,1)}, bf16[1,1568,128]{2,1,0:T(8,128)(2,1)}, bf16[1,1568,128]{2,1,0:T(8,128)(2,1)}) custom-call(bf16[2,1568,1152]{2,1,0:T(8,128)(2,1)} %dec_qkv.1.q_ref.k_ref.v_ref, bf16[2,1568,1152]{2,1,0:T(8,128)(2,1)} %dec_qkv.1.q_ref.k_ref.v_ref, bf16[2,1568,1152]{2,1,0:T(8,128)(2,1)} %dec_qkv.1.q_ref.k_ref.v_ref, ...), custom_call_target="tpu_custom_call" | custom-call | flops 18699999232 | tf_op jit(solution)/shard_map/dec_attend_backward_1_2/pallas_call | solution.py:132
  539.8 12.0 %dec_qkv_back_1.1 = (bf16[1,1568,384]{2,1,0:T(8,128)(2,1)}, f32[384,1152]{1,0:T(8,128)}, f32[8,384]{1,0:T(8,128)}) custom-call(f32[2,1568,384]{2,1,0:T(8,128)} %scatter-add.4.h_ref, f32[2,1568,384]{2,1,0:T(8,128)} %get-tuple-element.257.dmid_ref, bf16[384,1152]{1,0:T(8,128)(2,1)} %slice.204.w_ref, f32[1,14592]{1,0:T(1,128)} %bitcast.178, ...), custom_call_target="tpu_custom_call" | custom-call | flops 11000000512 | tf_op jit(solution)/shard_map/dec_qkv_back_1/pallas_call | solution.py:284
  561.0 27.1 %enc_backward.1 = (bf16[320,768]{1,0:T(8,128)(2,1)}, bf16[320,3072]{1,0:T(8,128)(2,1)}, bf16[320,3072]{1,0:T(8,128)(2,1)}, bf16[320,768]{1,0:T(8,128)(2,1)}, f32...) custom-call(bf16[320,384]{1,0:T(8,128)(2,1)} %bitcast.159, f32[320,768]{1,0:T(8,128)} %get-tuple-element.304.h_ref, ...), custom_call_target="tpu_custom_call" | custom-call | flops 5473566720 | bytes 29360128 | tf_op jit(solution)/shard_map/enc_backward/pallas_call | solution.py:434
  593.7 7.0 collective-permute-done.38
  621.9 16.3 %collective-permute-done.45 = f32[2,1,1,1,24,1152]{5,4,3,2,1,0:T(8,128)S(1)} collective-permute-done((f32[2,1,1,1,24,1152]{5,4,3,2,1,0:T(8,128)S(1)}, f32[2,1,1,1,24,1152]{5,4,3,2,1,0:T(8,128)S(1)}, u32[]{:S(2)}, u32[]{:S(2)}) %collective-permute-start.45) | collective-permute-done | bytes 221216 | tf_op jit(solution)/shard_map/ppermute | solution.py:485
  641.8 4.6 collective-permute-done.48
  649.9 6.8 grad_up.1
  657.7 2.9 collective-permute-start.56
  660.6 7.0 grad_wide.1
  668.7 9.8 %grad_tall.1 = f32[4608,384]{1,0:T(8,128)} custom-call(bf16[1,320,4608]{2,1,0:T(8,128)(2,1)} %bitcast.151, bf16[1,320,4608]{2,1,0:T(8,128)(2,1)} %bitcast.62.bl_ref, bf16[2,320,384]{2,1,0:T(8,128)(2,1)} %pad_maximum_fusion.1.ar_ref, bf16[2,320,384]{2,1,0:T(8,128)(2,1)} %copy-done.36), custom_call_target="tpu_custom_call" | custom-call | flops 2264924160 | bytes 7077888 | tf_op jit(solution)/shard_map/grad_tall/pallas_call | solution.py:448
  680.1 2.7 collective-permute-done.58
  683.6 4.8 multiply_convert_fusion
  689.9 3.6 multiply_convert_fusion.2
  702.8 21.6 %collective-permute-done.63 = f32[1,1,1,1,48,384]{5,4,3,2,1,0:T(8,128)} collective-permute-done((f32[1,1,1,1,48,384]{5,4,3,2,1,0:T(8,128)S(1)}, f32[1,1,1,1,48,384]{5,4,3,2,1,0:T(8,128)}, u32[]{:S(2)}, u32[]{:S(2)}) %collective-permute-start.63) | collective-permute-done | bytes 73760 | tf_op jit(solution)/shard_map/ppermute | solution.py:485
  724.4 2.8 collective-permute-done.61
  727.2 2.4 multiply_add_fusion.5
  732.2 2.4 multiply_add_fusion.3
  744.1 13.1 %collective-permute-done.68 = f32[1,1,1,2,48,384]{5,4,3,2,1,0:T(8,128)S(1)} collective-permute-done((f32[1,1,1,2,48,384]{5,4,3,2,1,0:T(8,128)S(1)}, f32[1,1,1,2,48,384]{5,4,3,2,1,0:T(8,128)S(1)}, u32[]{:S(2)}, u32[]{:S(2)}) %collective-permute-start.68) | collective-permute-done | bytes 147488 | tf_op jit(solution)/shard_map/ppermute | solution.py:485
  764.9 7.0 collective-permute-done.70
  779.5 25.7 %collective-permute-done.74 = f16[1,1,1,96,1536]{4,3,2,1,0:T(8,128)(2,1)} collective-permute-done((f16[1,1,1,96,1536]{4,3,2,1,0:T(8,128)(2,1)S(1)}, f16[1,1,1,96,1536]{4,3,2,1,0:T(8,128)(2,1)}, u32[]{:S(2)}, u32[]{:S(2)}) %collective-permute-start.74) | collective-permute-done | bytes 294944 | tf_op jit(solution)/shard_map/ppermute | solution.py:485
  805.2 15.0 %collective-permute-done.75 = f16[1,1,1,96,1536]{4,3,2,1,0:T(8,128)(2,1)} collective-permute-done((f16[1,1,1,96,1536]{4,3,2,1,0:T(8,128)(2,1)S(1)}, f16[1,1,1,96,1536]{4,3,2,1,0:T(8,128)(2,1)}, u32[]{:S(2)}, u32[]{:S(2)}) %collective-permute-start.75) | collective-permute-done | bytes 294944 | tf_op jit(solution)/shard_map/ppermute | solution.py:485
  821.0 3.1 multiply_convert_fusion.10
  824.0 2.4 multiply_convert_fusion.9
  826.4 2.5 multiply_convert_fusion.6
  842.3 3.0 collective-permute-start.78
  858.2 17.5 %collective-permute-start.82 = (f32[1]{0:T(128)}, f32[1]{0:T(128)}, u32[]{:S(2)}, u32[]{:S(2)}) collective-permute-start(f32[1]{0:T(128)} %add.594), channel_id=1, source_target_pairs={{0,8},{2,10},{4,12},{6,14},{8,0},{10,2},{12,4},{14,6},{16,24},{18,... | collective-permute-start | bytes 20 | tf_op jit(solution)/shard_map/ppermute | solution.py:485
  888.5 8.3 fusion.50
  901.6 2.6 fusion.47
  908.6 2.7 convert_multiply_fusion
  911.2 24.1 %fusion.54 = (bf16[384,6528]{1,0:T(8,128)(2,1)}, f32[384,6528]{1,0:T(8,128)}, f32[384,6528]{1,0:T(8,128)}, f32[384,6528]{1,0:T(8,128)}) fusion(f32[384,6528]{1,0:T(8,128)} %param.25, f32[]{:T(128)S(6)} %min.3, f32[384,384]{1,0:T(8,128)} %bitcast.157, f32[384,3072]{1,0:T(8,128)} %convert_multiply_fusion, f32[384,768]{1,0:T(8,128)} %convert_multiply_fusion.2, ...), kind=kLoop, calls=%fused_computation.266 | loop fusion | flops 50135040 | bytes 75202560 | tf_op jit(solution)/shard_map/convert_element_type | solution.py:848
  935.4 21.4 %fusion.52 = (bf16[2304,768]{1,0:T(8,128)(2,1)}, f32[2304,768]{1,0:T(8,128)}, f32[2304,768]{1,0:T(8,128)}, f32[2304,768]{1,0:T(8,128)}) fusion(f32[2304,768]{1,0:T(8,128)} %param.26, f32[]{:T(128)S(6)} %min.3, f32[]{:T(128)S(6)} %div.278, f16[2304,384]{1,0:T(8,128)(2,1)} %bitcast.84, f16[2304,384]{1,0:T(8,128)(2,1)} %collective-permute-done.89, ...), kind=kLoop, calls=%fused_computation.265 | loop fusion | flops 38928384 | bytes 49545224 | tf_op jit(solution)/shard_map/convert_element_type | solution.py:848
  (507 shorter events, 207.3 us)
Async XLA Ops:
  3.1 36.8 %collective-permute-start = (bf16[1,1,1,1,48,6528]{5,4,3,2,1,0:T(8,128)(2,1)}, bf16[1,1,1,1,48,6528]{5,4,3,2,1,0:T(8,128)(2,1)}, u32[]{:S(2)}, u32[]{:S(2)}) collective-permute-start(bf16[1,1,1,1,48,6528]{5,4,3,2,1,0:T(8,128)(2,1)} %dynamic-slice_convert_fusion), channel_id=1, source_target_pairs={{0,1},{1,0},{2,3},{3,2},{4,5},{5,4},{6,7},{7,6},{8,9},{9,8},{10,11... | collective-permute-start | bytes 1880072 | tf_op jit(solution)/shard_map/ppermute | solution.py:635
  8.0 31.8 %collective-permute-start.1 = (bf16[1,1,1,1,288,768]{5,4,3,2,1,0:T(8,128)(2,1)}, bf16[1,1,1,1,288,768]{5,4,3,2,1,0:T(8,128)(2,1)}, u32[]{:S(2)}, u32[]{:S(2)}) collective-permute-start(bf16[1,1,1,1,288,768]{5,4,3,2,1,0:T(8,128)(2,1)} %dynamic-slice_convert_fusion.1), channel_id=1, source_target_pairs={{0,1},{1,0},{2,3},{3,2},{4,5},{5,4},{6,7},{7,6},{8,9},{9,8},{10,11... | collective-permute-start | bytes 1327112 | tf_op jit(solution)/shard_map/ppermute | solution.py:635
  8.8 31.0 %collective-permute-start.2 = (bf16[1,7296]{1,0:T(2,128)(2,1)S(1)}, bf16[1,7296]{1,0:T(2,128)(2,1)S(1)}, u32[]{:S(2)}, u32[]{:S(2)}) collective-permute-start(bf16[1,7296]{1,0:T(2,128)(2,1)S(1)} %reshape.2847), channel_id=1, source_target_pairs={{0,1},{1,0},{2,3},{3,2},{4,5},{5,4},{6,7},{7,6},{8,9},{9,8},{10,11... | collective-permute-start | bytes 43784 | tf_op jit(solution)/shard_map/ppermute | solution.py:635
  12.2 27.7 %collective-permute-start.3 = (f32[1]{0:T(128)}, f32[1]{0:T(128)}, u32[]{:S(2)}, u32[]{:S(2)}) collective-permute-start(f32[1]{0:T(128)} %bitcast.5), channel_id=1, source_target_pairs={{0,2},{2,0},{4,6},{6,4},{8,10},{10,8},{12,14},{14,12},{16,18},{18,... | collective-permute-start | bytes 20 | tf_op jit(solution)/shard_map/ppermute | solution.py:485
  41.5 21.7 %collective-permute-start.4 = (bf16[1,1,1,1,48,6528]{5,4,3,2,1,0:T(8,128)(2,1)}, bf16[1,1,1,1,48,6528]{5,4,3,2,1,0:T(8,128)(2,1)S(1)}, u32[]{:S(2)}, u32[]{:S(2)}) collective-permute-start(bf16[1,1,1,1,48,6528]{5,4,3,2,1,0:T(8,128)(2,1)} %collective-permute-done), channel_id=1, source_target_pairs={{0,4},{2,6},{4,0},{6,2},{8,12},{10,14},{12,8},{14,10},{16,20},{18,... | collective-permute-start | bytes 1880072 | tf_op jit(solution)/shard_map/ppermute | solution.py:485
  43.0 20.2 %collective-permute-start.5 = (bf16[1,1,1,1,288,768]{5,4,3,2,1,0:T(8,128)(2,1)}, bf16[1,1,1,1,288,768]{5,4,3,2,1,0:T(8,128)(2,1)S(1)}, u32[]{:S(2)}, u32[]{:S(2)}) collective-permute-start(bf16[1,1,1,1,288,768]{5,4,3,2,1,0:T(8,128)(2,1)} %collective-permute-done.1), channel_id=1, source_target_pairs={{0,8},{2,10},{4,12},{6,14},{8,0},{10,2},{12,4},{14,6},{16,24},{18,... | collective-permute-start | bytes 1327112 | tf_op jit(solution)/shard_map/ppermute | solution.py:485
  44.6 18.7 %collective-permute-start.7 = (bf16[1,1,1,1,24,4608]{5,4,3,2,1,0:T(8,128)(2,1)S(1)}, bf16[1,1,1,1,24,4608]{5,4,3,2,1,0:T(8,128)(2,1)S(1)}, u32[]{:S(2)}, u32[]{:S(2)}) collective-permute-start(bf16[1,1,1,1,24,4608]{5,4,3,2,1,0:T(8,128)(2,1)S(1)} %copy-done.46), channel_id=1, source_target_pairs={{0,1},{1,0},{2,3},{3,2},{4,5},{5,4},{6,7},{7,6},{8,9},{9,8},{10,11... | collective-permute-start | bytes 663560 | tf_op jit(solution)/shard_map/ppermute | solution.py:635
  45.1 18.1 %collective-permute-start.8 = (bf16[1,1,1,1,96,384]{5,4,3,2,1,0:T(8,128)(2,1)S(1)}, bf16[1,1,1,1,96,384]{5,4,3,2,1,0:T(8,128)(2,1)S(1)}, u32[]{:S(2)}, u32[]{:S(2)}) collective-permute-start(bf16[1,1,1,1,96,384]{5,4,3,2,1,0:T(8,128)(2,1)S(1)} %copy-done.49), channel_id=1, source_target_pairs={{0,1},{1,0},{2,3},{3,2},{4,5},{5,4},{6,7},{7,6},{8,9},{9,8},{10,11... | collective-permute-start | bytes 221192 | tf_op jit(solution)/shard_map/ppermute | solution.py:635
  66.6 77.9 %collective-permute-start.9 = (bf16[1,1,2,1,48,6528]{5,4,3,2,1,0:T(8,128)(2,1)S(1)}, bf16[1,1,2,1,48,6528]{5,4,3,2,1,0:T(8,128)(2,1)}, u32[]{:S(2)}, u32[]{:S(2)}) collective-permute-start(bf16[1,1,2,1,48,6528]{5,4,3,2,1,0:T(8,128)(2,1)S(1)} %maximum_select_fusion.14), channel_id=1, source_target_pairs={{0,8},{2,10},{4,12},{6,14},{8,0},{10,2},{12,4},{14,6},{16,24},{18,... | collective-permute-start | bytes 3760136 | tf_op jit(solution)/shard_map/ppermute | solution.py:485
  69.3 75.1 %collective-permute-start.10 = (bf16[1,1,1,2,288,768]{5,4,3,2,1,0:T(8,128)(2,1)}, bf16[1,1,1,2,288,768]{5,4,3,2,1,0:T(8,128)(2,1)}, u32[]{:S(2)}, u32[]{:S(2)}) collective-permute-start(bf16[1,1,1,2,288,768]{5,4,3,2,1,0:T(8,128)(2,1)} %maximum_select_fusion.20), channel_id=1, source_target_pairs={{0,4},{2,6},{4,0},{6,2},{8,12},{10,14},{12,8},{14,10},{16,20},{18,... | collective-permute-start | bytes 2654216 | tf_op jit(solution)/shard_map/ppermute | solution.py:485
  70.5 73.9 %collective-permute-start.11 = (f32[1]{0:T(128)}, f32[1]{0:T(128)}, u32[]{:S(2)}, u32[]{:S(2)}) collective-permute-start(f32[1]{0:T(128)} %add.533), channel_id=1, source_target_pairs={{0,8},{2,10},{4,12},{6,14},{8,0},{10,2},{12,4},{14,6},{16,24},{18,... | collective-permute-start | bytes 20 | tf_op jit(solution)/shard_map/ppermute | solution.py:485
  93.0 51.5 %collective-permute-start.12 = (bf16[1,1,1,1,24,4608]{5,4,3,2,1,0:T(8,128)(2,1)S(1)}, bf16[1,1,1,1,24,4608]{5,4,3,2,1,0:T(8,128)(2,1)S(1)}, u32[]{:S(2)}, u32[]{:S(2)}) collective-permute-start(bf16[1,1,1,1,24,4608]{5,4,3,2,1,0:T(8,128)(2,1)S(1)} %collective-permute-done.7), channel_id=1, source_target_pairs={{0,4},{2,6},{4,0},{6,2},{8,12},{10,14},{12,8},{14,10},{16,20},{18,... | collective-permute-start | bytes 663560 | tf_op jit(solution)/shard_map/ppermute | solution.py:485
  93.0 51.5 %collective-permute-start.13 = (bf16[1,1,1,1,96,384]{5,4,3,2,1,0:T(8,128)(2,1)S(1)}, bf16[1,1,1,1,96,384]{5,4,3,2,1,0:T(8,128)(2,1)S(1)}, u32[]{:S(2)}, u32[]{:S(2)}) collective-permute-start(bf16[1,1,1,1,96,384]{5,4,3,2,1,0:T(8,128)(2,1)S(1)} %collective-permute-done.8), channel_id=1, source_target_pairs={{0,8},{2,10},{4,12},{6,14},{8,0},{10,2},{12,4},{14,6},{16,24},{18,... | collective-permute-start | bytes 221192 | tf_op jit(solution)/shard_map/ppermute | solution.py:485
  146.6 20.8 %collective-permute-start.14 = (bf16[1,1,2,2,48,6528]{5,4,3,2,1,0:T(8,128)(2,1)S(1)}, bf16[1,1,2,2,48,6528]{5,4,3,2,1,0:T(8,128)(2,1)}, u32[]{:S(2)}, u32[]{:S(2)}) collective-permute-start(bf16[1,1,2,2,48,6528]{5,4,3,2,1,0:T(8,128)(2,1)S(1)} %maximum_select_fusion.7), channel_id=1, source_target_pairs={{0,2},{2,0},{4,6},{6,4},{8,10},{10,8},{12,14},{14,12},{16,18},{18,... | collective-permute-start | bytes 7520264 | tf_op jit(solution)/shard_map/ppermute | solution.py:485
  151.0 16.5 %collective-permute-start.15 = (bf16[1,1,2,2,288,768]{5,4,3,2,1,0:T(8,128)(2,1)}, bf16[1,1,2,2,288,768]{5,4,3,2,1,0:T(8,128)(2,1)}, u32[]{:S(2)}, u32[]{:S(2)}) collective-permute-start(bf16[1,1,2,2,288,768]{5,4,3,2,1,0:T(8,128)(2,1)} %maximum_select_fusion.9), channel_id=1, source_target_pairs={{0,2},{2,0},{4,6},{6,4},{8,10},{10,8},{12,14},{14,12},{16,18},{18,... | collective-permute-start | bytes 5308424 | tf_op jit(solution)/shard_map/ppermute | solution.py:485
  156.1 11.3 %collective-permute-start.17 = (bf16[1,1,2,1,24,4608]{5,4,3,2,1,0:T(8,128)(2,1)S(1)}, bf16[1,1,2,1,24,4608]{5,4,3,2,1,0:T(8,128)(2,1)S(1)}, u32[]{:S(2)}, u32[]{:S(2)}) collective-permute-start(bf16[1,1,2,1,24,4608]{5,4,3,2,1,0:T(8,128)(2,1)S(1)} %maximum_select_fusion.33), channel_id=1, source_target_pairs={{0,8},{2,10},{4,12},{6,14},{8,0},{10,2},{12,4},{14,6},{16,24},{18,... | collective-permute-start | bytes 1327112 | tf_op jit(solution)/shard_map/ppermute | solution.py:485
  175.4 38.1 %collective-permute-start.19 = (f32[1]{0:T(128)}, f32[1]{0:T(128)}, u32[]{:S(2)}, u32[]{:S(2)}) collective-permute-start(f32[1]{0:T(128)} %add.535), channel_id=1, source_target_pairs={{0,1},{1,0},{2,3},{3,2},{4,5},{5,4},{6,7},{7,6},{8,9},{9,8},{10,11... | collective-permute-start | bytes 20 | tf_op jit(solution)/shard_map/ppermute | solution.py:485
  177.4 40.1 %collective-permute-start.20 = (bf16[1,1,2,2,24,4608]{5,4,3,2,1,0:T(8,128)(2,1)S(1)}, bf16[1,1,2,2,24,4608]{5,4,3,2,1,0:T(8,128)(2,1)}, u32[]{:S(2)}, u32[]{:S(2)}) collective-permute-start(bf16[1,1,2,2,24,4608]{5,4,3,2,1,0:T(8,128)(2,1)S(1)} %maximum_select_fusion.22), channel_id=1, source_target_pairs={{0,2},{2,0},{4,6},{6,4},{8,10},{10,8},{12,14},{14,12},{16,18},{18,... | collective-permute-start | bytes 2654216 | tf_op jit(solution)/shard_map/ppermute | solution.py:485
  177.6 40.0 %collective-permute-start.21 = (bf16[1,1,2,2,96,384]{5,4,3,2,1,0:T(8,128)(2,1)S(1)}, bf16[1,1,2,2,96,384]{5,4,3,2,1,0:T(8,128)(2,1)}, u32[]{:S(2)}, u32[]{:S(2)}) collective-permute-start(bf16[1,1,2,2,96,384]{5,4,3,2,1,0:T(8,128)(2,1)S(1)} %maximum_select_fusion.36), channel_id=1, source_target_pairs={{0,2},{2,0},{4,6},{6,4},{8,10},{10,8},{12,14},{14,12},{16,18},{18,... | collective-permute-start | bytes 884744 | tf_op jit(solution)/shard_map/ppermute | solution.py:485
  213.0 167.8 %collective-permute-start.22 = (bf16[320,4608]{1,0:T(8,128)(2,1)}, bf16[320,4608]{1,0:T(8,128)(2,1)}, u32[]{:S(2)}, u32[]{:S(2)}) collective-permute-start(bf16[320,4608]{1,0:T(8,128)(2,1)} %get-tuple-element.260), channel_id=1, source_target_pairs={{0,2},{2,0},{4,6},{6,4},{8,10},{10,8},{12,14},{14,12},{16,18},{18,... | collective-permute-start | bytes 8847368 | tf_op jit(solution)/shard_map/ppermute | solution.py:485
  213.1 167.8 %collective-permute-start.23 = (bf16[2,320,768]{2,1,0:T(8,128)(2,1)}, bf16[2,320,768]{2,1,0:T(8,128)(2,1)}, u32[]{:S(2)}, u32[]{:S(2)}) collective-permute-start(bf16[2,320,768]{2,1,0:T(8,128)(2,1)} %get-tuple-element.261.al_ref), channel_id=1, source_target_pairs={{0,2},{2,0},{4,6},{6,4},{8,10},{10,8},{12,14},{14,12},{16,18},{18,... | collective-permute-start | bytes 2949128 | tf_op jit(solution)/shard_map/ppermute | solution.py:485
  374.6 25.6 %collective-permute-start.25 = (f32[2,1,2,2,24,3456]{5,4,3,2,1,0:T(8,128)S(1)}, f32[2,1,2,2,24,3456]{5,4,3,2,1,0:T(8,128)}, u32[]{:S(2)}, u32[]{:S(2)}) collective-permute-start(f32[2,1,2,2,24,3456]{5,4,3,2,1,0:T(8,128)S(1)} %constant_dynamic-slice_fusion.19), channel_id=1, source_target_pairs={{0,2},{2,0},{4,6},{6,4},{8,10},{10,8},{12,14},{14,12},{16,18},{18,... | collective-permute-start | bytes 7962632 | tf_op jit(solution)/shard_map/ppermute | solution.py:485
  378.6 21.6 %collective-permute-start.26 = (f32[2,1,2,2,96,384]{5,4,3,2,1,0:T(8,128)}, f32[2,1,2,2,96,384]{5,4,3,2,1,0:T(8,128)}, u32[]{:S(2)}, u32[]{:S(2)}) collective-permute-start(f32[2,1,2,2,96,384]{5,4,3,2,1,0:T(8,128)} %constant_dynamic-slice_fusion.18), channel_id=1, source_target_pairs={{0,2},{2,0},{4,6},{6,4},{8,10},{10,8},{12,14},{14,12},{16,18},{18,... | collective-permute-start | bytes 3538952 | tf_op jit(solution)/shard_map/ppermute | solution.py:485
  403.2 31.6 %collective-permute-start.27 = (f32[2,1,1,2,24,3456]{5,4,3,2,1,0:T(8,128)S(1)}, f32[2,1,1,2,24,3456]{5,4,3,2,1,0:T(8,128)}, u32[]{:S(2)}, u32[]{:S(2)}) collective-permute-start(f32[2,1,1,2,24,3456]{5,4,3,2,1,0:T(8,128)S(1)} %constant_dynamic-slice_fusion.17), channel_id=1, source_target_pairs={{0,4},{2,6},{4,0},{6,2},{8,12},{10,14},{12,8},{14,10},{16,20},{18,... | collective-permute-start | bytes 3981320 | tf_op jit(solution)/shard_map/ppermute | solution.py:485
  408.0 19.6 %collective-permute-start.28 = (f32[2,1,2,1,96,384]{5,4,3,2,1,0:T(8,128)}, f32[2,1,2,1,96,384]{5,4,3,2,1,0:T(8,128)}, u32[]{:S(2)}, u32[]{:S(2)}) collective-permute-start(f32[2,1,2,1,96,384]{5,4,3,2,1,0:T(8,128)} %constant_dynamic-slice_fusion.16), channel_id=1, source_target_pairs={{0,8},{2,10},{4,12},{6,14},{8,0},{10,2},{12,4},{14,6},{16,24},{18,... | collective-permute-start | bytes 1769480 | tf_op jit(solution)/shard_map/ppermute | solution.py:485
  456.0 18.4 %collective-permute-start.29 = (f32[2,1,1,1,24,3456]{5,4,3,2,1,0:T(8,128)S(1)}, f32[2,1,1,1,24,3456]{5,4,3,2,1,0:T(8,128)S(1)}, u32[]{:S(2)}, u32[]{:S(2)}) collective-permute-start(f32[2,1,1,1,24,3456]{5,4,3,2,1,0:T(8,128)S(1)} %constant_dynamic-slice_fusion.15), channel_id=1, source_target_pairs={{0,8},{2,10},{4,12},{6,14},{8,0},{10,2},{12,4},{14,6},{16,24},{18,... | collective-permute-start | bytes 1990664 | tf_op jit(solution)/shard_map/ppermute | solution.py:485
  458.2 16.1 %collective-permute-start.30 = (f32[1,1,2,1,96,384]{5,4,3,2,1,0:T(8,128)}, f32[1,1,2,1,96,384]{5,4,3,2,1,0:T(8,128)S(1)}, u32[]{:S(2)}, u32[]{:S(2)}) collective-permute-start(f32[1,1,2,1,96,384]{5,4,3,2,1,0:T(8,128)} %constant_dynamic-slice_fusion.14), channel_id=1, source_target_pairs={{0,1},{1,0},{2,3},{3,2},{4,5},{5,4},{6,7},{7,6},{8,9},{9,8},{10,11... | collective-permute-start | bytes 884744 | tf_op jit(solution)/shard_map/ppermute | solution.py:485
  475.2 22.7 %collective-permute-start.31 = (f32[1,1,1,1,24,3456]{5,4,3,2,1,0:T(8,128)S(1)}, f32[1,1,1,1,24,3456]{5,4,3,2,1,0:T(8,128)S(1)}, u32[]{:S(2)}, u32[]{:S(2)}) collective-permute-start(f32[1,1,1,1,24,3456]{5,4,3,2,1,0:T(8,128)S(1)} %constant_dynamic-slice_fusion.13), channel_id=1, source_target_pairs={{0,1},{1,0},{2,3},{3,2},{4,5},{5,4},{6,7},{7,6},{8,9},{9,8},{10,11... | collective-permute-start | bytes 995336 | tf_op jit(solution)/shard_map/ppermute | solution.py:485
  476.8 21.1 %collective-permute-start.32 = (f32[1,1,1,1,96,384]{5,4,3,2,1,0:T(8,128)S(1)}, f32[1,1,1,1,96,384]{5,4,3,2,1,0:T(8,128)S(1)}, u32[]{:S(2)}, u32[]{:S(2)}) collective-permute-start(f32[1,1,1,1,96,384]{5,4,3,2,1,0:T(8,128)S(1)} %constant_dynamic-slice_fusion.12), channel_id=1, source_target_pairs={{0,4},{2,6},{4,0},{6,2},{8,12},{10,14},{12,8},{14,10},{16,20},{18,... | collective-permute-start | bytes 442376 | tf_op jit(solution)/shard_map/ppermute | solution.py:485
  497.9 22.5 %collective-permute-start.33 = (f32[1,1,1,1,24,3456]{5,4,3,2,1,0:T(8,128)S(1)}, f32[1,1,1,1,24,3456]{5,4,3,2,1,0:T(8,128)S(1)}, u32[]{:S(2)}, u32[]{:S(2)}) collective-permute-start(f32[1,1,1,1,24,3456]{5,4,3,2,1,0:T(8,128)S(1)} %dynamic-slice_add_fusion.8), channel_id=1, source_target_pairs={{0,16},{2,18},{4,20},{6,22},{8,24},{10,26},{12,28},{14,30},{16,0},... | collective-permute-start | bytes 995336 | tf_op jit(solution)/shard_map/ppermute | solution.py:485
  498.3 22.1 %collective-permute-start.34 = (f32[1,1,1,1,96,384]{5,4,3,2,1,0:T(8,128)S(1)}, f32[1,1,1,1,96,384]{5,4,3,2,1,0:T(8,128)S(1)}, u32[]{:S(2)}, u32[]{:S(2)}) collective-permute-start(f32[1,1,1,1,96,384]{5,4,3,2,1,0:T(8,128)S(1)} %dynamic-slice_add_fusion.13), channel_id=1, source_target_pairs={{0,16},{2,18},{4,20},{6,22},{8,24},{10,26},{12,28},{14,30},{16,0},... | collective-permute-start | bytes 442376 | tf_op jit(solution)/shard_map/ppermute | solution.py:485
  556.9 36.8 %collective-permute-start.39 = (f32[1,1,1,1,24,3456]{5,4,2,3,1,0:T(8,128)}, f32[1,1,1,1,24,3456]{5,4,2,3,1,0:T(8,128)}, u32[]{:S(2)}, u32[]{:S(2)}) collective-permute-start(f32[1,1,1,1,24,3456]{5,4,2,3,1,0:T(8,128)} %get-tuple-element.443), channel_id=1, source_target_pairs={{0,4},{2,6},{4,0},{6,2},{8,12},{10,14},{12,8},{14,10},{16,20},{18,... | collective-permute-start | bytes 995336 | tf_op jit(solution)/shard_map/ppermute | solution.py:485
  557.9 35.8 %collective-permute-start.40 = (f32[1,1,1,1,96,384]{5,4,3,2,1,0:T(8,128)S(1)}, f32[1,1,1,1,96,384]{5,4,3,2,1,0:T(8,128)}, u32[]{:S(2)}, u32[]{:S(2)}) collective-permute-start(f32[1,1,1,1,96,384]{5,4,3,2,1,0:T(8,128)S(1)} %get-tuple-element.432), channel_id=1, source_target_pairs={{0,8},{2,10},{4,12},{6,14},{8,0},{10,2},{12,4},{14,6},{16,24},{18,... | collective-permute-start | bytes 442376 | tf_op jit(solution)/shard_map/ppermute | solution.py:485
  590.8 11.6 %collective-permute-start.37 = (f32[2,1,1,2,24,1152]{5,4,3,2,1,0:T(8,128)S(1)}, f32[2,1,1,2,24,1152]{5,4,3,2,1,0:T(8,128)S(1)}, u32[]{:S(2)}, u32[]{:S(2)}) collective-permute-start(f32[2,1,1,2,24,1152]{5,4,3,2,1,0:T(8,128)S(1)} %constant_dynamic-slice_fusion.9), channel_id=1, source_target_pairs={{0,4},{2,6},{4,0},{6,2},{8,12},{10,14},{12,8},{14,10},{16,20},{18,... | collective-permute-start | bytes 1327112 | tf_op jit(solution)/shard_map/ppermute | solution.py:485
  604.8 41.6 %collective-permute-start.41 = (bf16[1,320,1536]{2,1,0:T(8,128)(2,1)}, bf16[1,320,1536]{2,1,0:T(8,128)(2,1)}, u32[]{:S(2)}, u32[]{:S(2)}) collective-permute-start(bf16[1,320,1536]{2,1,0:T(8,128)(2,1)} %get-tuple-element.435), channel_id=1, source_target_pairs={{0,2},{2,0},{4,6},{6,4},{8,10},{10,8},{12,14},{14,12},{16,18},{18,... | collective-permute-start | bytes 2949128 | tf_op jit(solution)/shard_map/ppermute | solution.py:485
  606.0 40.4 %collective-permute-start.42 = (bf16[1,320,1536]{2,1,0:T(8,128)(2,1)}, bf16[1,320,1536]{2,1,0:T(8,128)(2,1)}, u32[]{:S(2)}, u32[]{:S(2)}) collective-permute-start(bf16[1,320,1536]{2,1,0:T(8,128)(2,1)} %maximum_bitcast_fusion.1), channel_id=1, source_target_pairs={{0,2},{2,0},{4,6},{6,4},{8,10},{10,8},{12,14},{14,12},{16,18},{18,... | collective-permute-start | bytes 2949128 | tf_op jit(solution)/shard_map/ppermute | solution.py:485
  616.4 30.0 %collective-permute-start.47 = (f32[1,1,2,1,24,3456]{5,4,2,3,1,0:T(8,128)S(1)}, f32[1,1,2,1,24,3456]{5,4,2,3,1,0:T(8,128)S(1)}, u32[]{:S(2)}, u32[]{:S(2)}) collective-permute-start(f32[1,1,2,1,24,3456]{5,4,2,3,1,0:T(8,128)S(1)} %maximum_select_fusion.25), channel_id=1, source_target_pairs={{0,8},{2,10},{4,12},{6,14},{8,0},{10,2},{12,4},{14,6},{16,24},{18,... | collective-permute-start | bytes 1990664 | tf_op jit(solution)/shard_map/ppermute | solution.py:485
  619.3 18.9 %collective-permute-start.45 = (f32[2,1,1,1,24,1152]{5,4,3,2,1,0:T(8,128)S(1)}, f32[2,1,1,1,24,1152]{5,4,3,2,1,0:T(8,128)S(1)}, u32[]{:S(2)}, u32[]{:S(2)}) collective-permute-start(f32[2,1,1,1,24,1152]{5,4,3,2,1,0:T(8,128)S(1)} %constant_dynamic-slice_fusion.3), channel_id=1, source_target_pairs={{0,8},{2,10},{4,12},{6,14},{8,0},{10,2},{12,4},{14,6},{16,24},{18,... | collective-permute-start | bytes 663560 | tf_op jit(solution)/shard_map/ppermute | solution.py:485
  620.8 25.6 %collective-permute-start.43 = (bf16[2,320,384]{2,1,0:T(8,128)(2,1)S(1)}, bf16[2,320,384]{2,1,0:T(8,128)(2,1)S(1)}, u32[]{:S(2)}, u32[]{:S(2)}) collective-permute-start(bf16[2,320,384]{2,1,0:T(8,128)(2,1)S(1)} %pad_maximum_fusion.2), channel_id=1, source_target_pairs={{0,2},{2,0},{4,6},{6,4},{8,10},{10,8},{12,14},{14,12},{16,18},{18,... | collective-permute-start | bytes 1474568 | tf_op jit(solution)/shard_map/ppermute | solution.py:485
  657.5 11.0 %collective-permute-start.55 = (f32[1,1,1,1,24,1152]{5,4,3,2,1,0:T(8,128)S(1)}, f32[1,1,1,1,24,1152]{5,4,3,2,1,0:T(8,128)S(1)}, u32[]{:S(2)}, u32[]{:S(2)}) collective-permute-start(f32[1,1,1,1,24,1152]{5,4,3,2,1,0:T(8,128)S(1)} %dynamic-slice_add_fusion.14), channel_id=1, source_target_pairs={{0,16},{2,18},{4,20},{6,22},{8,24},{10,26},{12,28},{14,30},{16,0},... | collective-permute-start | bytes 331784 | tf_op jit(solution)/shard_map/ppermute | solution.py:485
  688.4 38.8 %collective-permute-start.61 = (f16[1,2,2,576,384]{4,3,2,1,0:T(8,128)(2,1)}, f16[1,2,2,576,384]{4,3,2,1,0:T(8,128)(2,1)S(1)}, u32[]{:S(2)}, u32[]{:S(2)}) collective-permute-start(f16[1,2,2,576,384]{4,3,2,1,0:T(8,128)(2,1)} %multiply_convert_fusion), channel_id=1, source_target_pairs={{0,1},{1,0},{2,3},{3,2},{4,5},{5,4},{6,7},{7,6},{8,9},{9,8},{10,11... | collective-permute-start | bytes 5308424 | tf_op jit(solution)/shard_map/ppermute | solution.py:485
  693.5 30.9 %collective-permute-start.59 = (f16[2,1,2,96,1536]{4,3,2,1,0:T(8,128)(2,1)}, f16[2,1,2,96,1536]{4,3,2,1,0:T(8,128)(2,1)}, u32[]{:S(2)}, u32[]{:S(2)}) collective-permute-start(f16[2,1,2,96,1536]{4,3,2,1,0:T(8,128)(2,1)} %multiply_convert_fusion.2), channel_id=1, source_target_pairs={{0,4},{2,6},{4,0},{6,2},{8,12},{10,14},{12,8},{14,10},{16,20},{18,... | collective-permute-start | bytes 3538952 | tf_op jit(solution)/shard_map/ppermute | solution.py:485
  697.0 27.4 %collective-permute-start.60 = (f16[2,2,1,96,1536]{4,3,2,1,0:T(8,128)(2,1)}, f16[2,2,1,96,1536]{4,3,2,1,0:T(8,128)(2,1)}, u32[]{:S(2)}, u32[]{:S(2)}) collective-permute-start(f16[2,2,1,96,1536]{4,3,2,1,0:T(8,128)(2,1)} %multiply_convert_fusion.1), channel_id=1, source_target_pairs={{0,8},{2,10},{4,12},{6,14},{8,0},{10,2},{12,4},{14,6},{16,24},{18,... | collective-permute-start | bytes 3538952 | tf_op jit(solution)/shard_map/ppermute | solution.py:485
  699.4 25.0 %collective-permute-start.62 = (f32[1,1,1,1,24,1152]{5,4,2,3,1,0:T(8,128)S(1)}, f32[1,1,1,1,24,1152]{5,4,2,3,1,0:T(8,128)S(1)}, u32[]{:S(2)}, u32[]{:S(2)}) collective-permute-start(f32[1,1,1,1,24,1152]{5,4,2,3,1,0:T(8,128)S(1)} %get-tuple-element.456), channel_id=1, source_target_pairs={{0,4},{2,6},{4,0},{6,2},{8,12},{10,14},{12,8},{14,10},{16,20},{18,... | collective-permute-start | bytes 331784 | tf_op jit(solution)/shard_map/ppermute | solution.py:485
  700.4 24.0 %collective-permute-start.63 = (f32[1,1,1,1,48,384]{5,4,3,2,1,0:T(8,128)S(1)}, f32[1,1,1,1,48,384]{5,4,3,2,1,0:T(8,128)}, u32[]{:S(2)}, u32[]{:S(2)}) collective-permute-start(f32[1,1,1,1,48,384]{5,4,3,2,1,0:T(8,128)S(1)} %get-tuple-element.430), channel_id=1, source_target_pairs={{0,8},{2,10},{4,12},{6,14},{8,0},{10,2},{12,4},{14,6},{16,24},{18,... | collective-permute-start | bytes 221192 | tf_op jit(solution)/shard_map/ppermute | solution.py:485
  730.5 26.7 %collective-permute-start.64 = (f16[2,1,1,96,1536]{4,3,2,1,0:T(8,128)(2,1)S(1)}, f16[2,1,1,96,1536]{4,3,2,1,0:T(8,128)(2,1)S(1)}, u32[]{:S(2)}, u32[]{:S(2)}) collective-permute-start(f16[2,1,1,96,1536]{4,3,2,1,0:T(8,128)(2,1)S(1)} %multiply_convert_fusion.5), channel_id=1, source_target_pairs={{0,8},{2,10},{4,12},{6,14},{8,0},{10,2},{12,4},{14,6},{16,24},{18,... | collective-permute-start | bytes 1769480 | tf_op jit(solution)/shard_map/ppermute | solution.py:485
  735.4 21.7 %collective-permute-start.66 = (f16[1,1,2,576,384]{4,3,2,1,0:T(8,128)(2,1)S(1)}, f16[1,1,2,576,384]{4,3,2,1,0:T(8,128)(2,1)S(1)}, u32[]{:S(2)}, u32[]{:S(2)}) collective-permute-start(f16[1,1,2,576,384]{4,3,2,1,0:T(8,128)(2,1)S(1)} %multiply_convert_fusion.3), channel_id=1, source_target_pairs={{0,4},{2,6},{4,0},{6,2},{8,12},{10,14},{12,8},{14,10},{16,20},{18,... | collective-permute-start | bytes 2654216 | tf_op jit(solution)/shard_map/ppermute | solution.py:485
  739.5 17.7 %collective-permute-start.65 = (f16[1,2,1,96,1536]{4,3,2,1,0:T(8,128)(2,1)S(1)}, f16[1,2,1,96,1536]{4,3,2,1,0:T(8,128)(2,1)S(1)}, u32[]{:S(2)}, u32[]{:S(2)}) collective-permute-start(f16[1,2,1,96,1536]{4,3,2,1,0:T(8,128)(2,1)S(1)} %multiply_convert_fusion.4), channel_id=1, source_target_pairs={{0,1},{1,0},{2,3},{3,2},{4,5},{5,4},{6,7},{7,6},{8,9},{9,8},{10,11... | collective-permute-start | bytes 1769480 | tf_op jit(solution)/shard_map/ppermute | solution.py:485
  741.1 16.0 %collective-permute-start.67 = (f32[1,1,2,1,24,1152]{5,4,2,3,1,0:T(8,128)S(1)}, f32[1,1,2,1,24,1152]{5,4,2,3,1,0:T(8,128)S(1)}, u32[]{:S(2)}, u32[]{:S(2)}) collective-permute-start(f32[1,1,2,1,24,1152]{5,4,2,3,1,0:T(8,128)S(1)} %maximum_select_fusion.40), channel_id=1, source_target_pairs={{0,8},{2,10},{4,12},{6,14},{8,0},{10,2},{12,4},{14,6},{16,24},{18,... | collective-permute-start | bytes 663560 | tf_op jit(solution)/shard_map/ppermute | solution.py:485
  742.6 14.6 %collective-permute-start.68 = (f32[1,1,1,2,48,384]{5,4,3,2,1,0:T(8,128)S(1)}, f32[1,1,1,2,48,384]{5,4,3,2,1,0:T(8,128)S(1)}, u32[]{:S(2)}, u32[]{:S(2)}) collective-permute-start(f32[1,1,1,2,48,384]{5,4,3,2,1,0:T(8,128)S(1)} %maximum_select_fusion.44), channel_id=1, source_target_pairs={{0,4},{2,6},{4,0},{6,2},{8,12},{10,14},{12,8},{14,10},{16,20},{18,... | collective-permute-start | bytes 442376 | tf_op jit(solution)/shard_map/ppermute | solution.py:485
  760.7 11.1 %collective-permute-start.71 = (f16[1,1,1,576,384]{4,3,2,1,0:T(8,128)(2,1)S(1)}, f16[1,1,1,576,384]{4,3,2,1,0:T(8,128)(2,1)S(1)}, u32[]{:S(2)}, u32[]{:S(2)}) collective-permute-start(f16[1,1,1,576,384]{4,3,2,1,0:T(8,128)(2,1)S(1)} %multiply_convert_fusion.8), channel_id=1, source_target_pairs={{0,8},{2,10},{4,12},{6,14},{8,0},{10,2},{12,4},{14,6},{16,24},{18,... | collective-permute-start | bytes 1327112 | tf_op jit(solution)/shard_map/ppermute | solution.py:485
  772.7 32.6 %collective-permute-start.74 = (f16[1,1,1,96,1536]{4,3,2,1,0:T(8,128)(2,1)S(1)}, f16[1,1,1,96,1536]{4,3,2,1,0:T(8,128)(2,1)}, u32[]{:S(2)}, u32[]{:S(2)}) collective-permute-start(f16[1,1,1,96,1536]{4,3,2,1,0:T(8,128)(2,1)S(1)} %multiply_convert_fusion.12), channel_id=1, source_target_pairs={{0,16},{2,18},{4,20},{6,22},{8,24},{10,26},{12,28},{14,30},{16,0},... | collective-permute-start | bytes 884744 | tf_op jit(solution)/shard_map/ppermute | solution.py:485
  775.7 44.5 %collective-permute-start.76 = (f16[1,1,1,576,384]{4,3,2,1,0:T(8,128)(2,1)S(1)}, f16[1,1,1,576,384]{4,3,2,1,0:T(8,128)(2,1)S(1)}, u32[]{:S(2)}, u32[]{:S(2)}) collective-permute-start(f16[1,1,1,576,384]{4,3,2,1,0:T(8,128)(2,1)S(1)} %multiply_convert_fusion.7), channel_id=1, source_target_pairs={{0,16},{2,18},{4,20},{6,22},{8,24},{10,26},{12,28},{14,30},{16,0},... | collective-permute-start | bytes 1327112 | tf_op jit(solution)/shard_map/ppermute | solution.py:485
  777.3 42.9 %collective-permute-start.75 = (f16[1,1,1,96,1536]{4,3,2,1,0:T(8,128)(2,1)S(1)}, f16[1,1,1,96,1536]{4,3,2,1,0:T(8,128)(2,1)}, u32[]{:S(2)}, u32[]{:S(2)}) collective-permute-start(f16[1,1,1,96,1536]{4,3,2,1,0:T(8,128)(2,1)S(1)} %multiply_convert_fusion.11), channel_id=1, source_target_pairs={{0,16},{2,18},{4,20},{6,22},{8,24},{10,26},{12,28},{14,30},{16,0},... | collective-permute-start | bytes 884744 | tf_op jit(solution)/shard_map/ppermute | solution.py:485
  828.9 17.1 %collective-permute-start.79 = (f16[1,1,1,96,1536]{4,3,2,1,0:T(8,128)(2,1)}, f16[1,1,1,96,1536]{4,3,2,1,0:T(8,128)(2,1)}, u32[]{:S(2)}, u32[]{:S(2)}) collective-permute-start(f16[1,1,1,96,1536]{4,3,2,1,0:T(8,128)(2,1)} %get-tuple-element.446), channel_id=1, source_target_pairs={{0,4},{2,6},{4,0},{6,2},{8,12},{10,14},{12,8},{14,10},{16,20},{18,... | collective-permute-start | bytes 884744 | tf_op jit(solution)/shard_map/ppermute | solution.py:485
  830.5 15.5 %collective-permute-start.80 = (f16[1,1,1,96,1536]{4,3,2,1,0:T(8,128)(2,1)S(1)}, f16[1,1,1,96,1536]{4,3,2,1,0:T(8,128)(2,1)}, u32[]{:S(2)}, u32[]{:S(2)}) collective-permute-start(f16[1,1,1,96,1536]{4,3,2,1,0:T(8,128)(2,1)S(1)} %get-tuple-element.444), channel_id=1, source_target_pairs={{0,4},{2,6},{4,0},{6,2},{8,12},{10,14},{12,8},{14,10},{16,20},{18,... | collective-permute-start | bytes 884744 | tf_op jit(solution)/shard_map/ppermute | solution.py:485
  830.9 15.1 %collective-permute-start.81 = (f16[1,1,1,576,384]{4,3,2,1,0:T(8,128)(2,1)S(1)}, f16[1,1,1,576,384]{4,3,2,1,0:T(8,128)(2,1)S(1)}, u32[]{:S(2)}, u32[]{:S(2)}) collective-permute-start(f16[1,1,1,576,384]{4,3,2,1,0:T(8,128)(2,1)S(1)} %get-tuple-element.439), channel_id=1, source_target_pairs={{0,8},{2,10},{4,12},{6,14},{8,0},{10,2},{12,4},{14,6},{16,24},{18,... | collective-permute-start | bytes 1327112 | tf_op jit(solution)/shard_map/ppermute | solution.py:485
  846.4 35.4 %collective-permute-start.86 = (f16[1,1,2,576,384]{4,3,2,1,0:T(8,128)(2,1)S(1)}, f16[1,1,2,576,384]{4,3,2,1,0:T(8,128)(2,1)S(1)}, u32[]{:S(2)}, u32[]{:S(2)}) collective-permute-start(f16[1,1,2,576,384]{4,3,2,1,0:T(8,128)(2,1)S(1)} %maximum_select_fusion.23), channel_id=1, source_target_pairs={{0,4},{2,6},{4,0},{6,2},{8,12},{10,14},{12,8},{14,10},{16,20},{18,... | collective-permute-start | bytes 2654216 | tf_op jit(solution)/shard_map/ppermute | solution.py:485
  849.6 31.3 %collective-permute-start.84 = (f16[1,2,1,96,1536]{4,3,2,1,0:T(8,128)(2,1)S(1)}, f16[1,2,1,96,1536]{4,3,2,1,0:T(8,128)(2,1)S(1)}, u32[]{:S(2)}, u32[]{:S(2)}) collective-permute-start(f16[1,2,1,96,1536]{4,3,2,1,0:T(8,128)(2,1)S(1)} %maximum_select_fusion.29), channel_id=1, source_target_pairs={{0,8},{2,10},{4,12},{6,14},{8,0},{10,2},{12,4},{14,6},{16,24},{18,... | collective-permute-start | bytes 1769480 | tf_op jit(solution)/shard_map/ppermute | solution.py:485
  853.0 27.9 %collective-permute-start.85 = (f16[1,2,1,96,1536]{4,3,2,1,0:T(8,128)(2,1)S(1)}, f16[1,2,1,96,1536]{4,3,2,1,0:T(8,128)(2,1)S(1)}, u32[]{:S(2)}, u32[]{:S(2)}) collective-permute-start(f16[1,2,1,96,1536]{4,3,2,1,0:T(8,128)(2,1)S(1)} %maximum_select_fusion.30), channel_id=1, source_target_pairs={{0,8},{2,10},{4,12},{6,14},{8,0},{10,2},{12,4},{14,6},{16,24},{18,... | collective-permute-start | bytes 1769480 | tf_op jit(solution)/shard_map/ppermute | solution.py:485
  858.2 18.3 %collective-permute-start.82 = (f32[1]{0:T(128)}, f32[1]{0:T(128)}, u32[]{:S(2)}, u32[]{:S(2)}) collective-permute-start(f32[1]{0:T(128)} %add.594), channel_id=1, source_target_pairs={{0,8},{2,10},{4,12},{6,14},{8,0},{10,2},{12,4},{14,6},{16,24},{18,... | collective-permute-start | bytes 20 | tf_op jit(solution)/shard_map/ppermute | solution.py:485
  883.2 21.0 %collective-permute-start.87 = (f16[384,1536]{1,0:T(8,128)(2,1)}, f16[384,1536]{1,0:T(8,128)(2,1)}, u32[]{:S(2)}, u32[]{:S(2)}) collective-permute-start(f16[384,1536]{1,0:T(8,128)(2,1)} %bitcast.81), channel_id=1, source_target_pairs={{0,2},{2,0},{4,6},{6,4},{8,10},{10,8},{12,14},{14,12},{16,18},{18,... | collective-permute-start | bytes 3538952 | tf_op jit(solution)/shard_map/ppermute | solution.py:485
  897.4 11.1 %collective-permute-start.88 = (f16[384,1536]{1,0:T(8,128)(2,1)S(1)}, f16[384,1536]{1,0:T(8,128)(2,1)S(1)}, u32[]{:S(2)}, u32[]{:S(2)}) collective-permute-start(f16[384,1536]{1,0:T(8,128)(2,1)S(1)} %bitcast.147), channel_id=1, source_target_pairs={{0,2},{2,0},{4,6},{6,4},{8,10},{10,8},{12,14},{14,12},{16,18},{18,... | collective-permute-start | bytes 3538952 | tf_op jit(solution)/shard_map/ppermute | solution.py:485
  900.2 35.2 %collective-permute-start.89 = (f16[2304,384]{1,0:T(8,128)(2,1)}, f16[2304,384]{1,0:T(8,128)(2,1)}, u32[]{:S(2)}, u32[]{:S(2)}) collective-permute-start(f16[2304,384]{1,0:T(8,128)(2,1)} %bitcast.84), channel_id=1, source_target_pairs={{0,2},{2,0},{4,6},{6,4},{8,10},{10,8},{12,14},{14,12},{16,18},{18,... | collective-permute-start | bytes 5308424 | tf_op jit(solution)/shard_map/ppermute | solution.py:485
  (108 other events, 801.3 us)

commit v2 on v1

--- a/solution.py
+++ b/solution.py
@@ -50,13 +50,13 @@
     for h in range(2):
         own = (lane < 64) if h == 0 else (lane >= 64)
         qh = jnp.where(own, q, jnp.zeros_like(q))
-        s = dot(qh, k, NT)
-        peak = jnp.max(s, axis=1, keepdims=True)
+        s = dot(k, qh, NT)
+        peak = jnp.max(s, axis=0, keepdims=True)
         e = jnp.exp2((s - peak) * (scale * LOG2E))
-        tot = jnp.sum(e, axis=1, keepdims=True)
+        tot = jnp.sum(e, axis=0, keepdims=True)
         p = (e * (1.0 / tot)).astype(bf16)
-        outs.append(dot(p, v, NN))
-        lse_ref[0, 0, h:h+1, :] = (peak * (scale * LOG2E) + jnp.log2(tot)).T
+        outs.append(dot(p, v, TN))
+        lse_ref[0, 0, h:h+1, :] = peak * (scale * LOG2E) + jnp.log2(tot)
     o_ref[0] = jnp.where(lane < 64, outs[0], outs[1]).astype(bf16)
 
 def attn_fwd(qkv, heads, rows, bq):
@@ -73,7 +73,7 @@
                    pl.BlockSpec((1, 1, 2, bq), lambda c, p, i: (c * pairs + p, i, 0, 0))],
         out_shape=[jax.ShapeDtypeStruct((clips, rows, w3 // 3), bf16),
                    jax.ShapeDtypeStruct((clips * pairs, nb, 2, bq), f32)],
-        compiler_params=pltpu.CompilerParams(vmem_limit_bytes=60 << 20), name="dec_attend_forward", cost_estimate=cost(70),
+        compiler_params=pltpu.CompilerParams(vmem_limit_bytes=60 << 20), name="dec_attend_forward", cost_estimate=cost(65),
     )(qkv, qkv, qkv)
 
 def bwd_body(scale, nb, mode, q_ref, k_ref, v_ref, do_ref, lse_ref, dq_ref, dk_ref, dv_ref, dk_acc, dv_acc, kt_ref):
@@ -327,7 +327,30 @@
     e = jnp.exp2((s - peak) * (0.125 * LOG2E))
     return q, k, v, qh, own, e * (1.0 / jnp.sum(e, axis=1, keepdims=True))
 
-def enc_fwd_body(clips, seen, x_ref, pos_ref, wr_ref, wc_ref, v_ref,
+def fetches(at_ref, sources, whole, sems):
+    rows = sources[0].shape[0]
+    copies = [(sources[0], at_ref[0] * rows)]
+    for far in range((len(sources) - 1) // 2):
+        for side in range(2):
+            start = at_ref[2 + far] * rows + (at_ref[1] if side == 0 else 1 - at_ref[1]) * (rows // 2)
+            copies.append((sources[1 + 2 * far + side], start))
+    return [
+        pltpu.make_async_copy(source, whole.at[pl.ds(pl.multiple_of(start, 16), source.shape[0])], sems.at[k])
+        for k, (source, start) in enumerate(copies)
+    ]
+
+def enc_fwd_body(clips, seen, count, at_ref, x_ref, pos_ref, v_ref, *refs):
+    row_sources, col_sources = refs[:count], refs[count:2 * count]
+    (h_ref, qkv_ref, h1_ref, inner_ref, enc_ref, proj_ref, tall_ref, pair_ref, m_ref, lat_ref, most_ref,
+     wr_ref, wc_ref, row_sems, col_sems) = refs[2 * count:]
+    col_copies = fetches(at_ref, col_sources, wc_ref, col_sems)
+    row_copies = fetches(at_ref, row_sources, wr_ref, row_sems)
+    for copy in col_copies + row_copies: copy.start()
+    for copy in col_copies: copy.wait()
+    enc_fwd_math(clips, seen, row_copies, x_ref, pos_ref, wr_ref, wc_ref, v_ref, h_ref, qkv_ref, h1_ref, inner_ref,
+                 enc_ref, proj_ref, tall_ref, pair_ref, m_ref, lat_ref, most_ref)
+
+def enc_fwd_math(clips, seen, row_copies, x_ref, pos_ref, wr_ref, wc_ref, v_ref,
                  h_ref, qkv_ref, h1_ref, inner_ref, enc_ref, proj_ref, tall_ref, pair_ref, m_ref, lat_ref, most_ref):
     x = x_ref[...]
     h = dot(x, wc_ref[:PATCH], NN) + pos_ref[...]
@@ -335,6 +358,7 @@
     s1, _ = ln(h)
     a = (s1 * enc_vec(v_ref, 0) + enc_vec(v_ref, 1)).astype(bf16)
     pair_ref[0] = a
+    for copy in row_copies: copy.wait()
     qkv_ref[...] = dot(a, wr_ref[:, QKV], NN).astype(bf16)
     n = h.shape[0] // clips
     for c in range(clips):
@@ -368,19 +392,30 @@
 
 def whole(shape): return pl.BlockSpec(shape, lambda: (0,) * len(shape))
 
-def enc_fwd(x, pos, wr, wc, vec, clips, seen):
+def weight_scratch(row_sources, col_sources, shard):
+    scratch = [pltpu.VMEM((shard * s[0].shape[0], s[0].shape[1]), bf16) for s in (row_sources, col_sources)]
+    return scratch + [pltpu.SemaphoreType.DMA((len(row_sources),))] * 2
+
+def enc_fwd(at, x, pos, vec, row_sources, col_sources, clips, seen, shard):
     n = x.shape[0]
     shapes = [((n, D), f32), ((n, 3 * D), bf16), ((n, D), f32), ((n, FF), f32), ((n, D), f32), ((n, DD), f32),
               ((n, PATCH + FF), bf16), ((2, n, D), bf16), ((n, D), bf16), ((n, D), bf16), ((8, 128), f32)]
-    return pl.pallas_call(functools.partial(enc_fwd_body, clips, seen),
-        in_specs=[whole(a.shape) for a in (x, pos, wr, wc, vec)],
+    count = len(row_sources)
+    return pl.pallas_call(functools.partial(enc_fwd_body, clips, seen, count),
+        in_specs=[pl.BlockSpec(memory_space=pltpu.SMEM)] + [whole(a.shape) for a in (x, pos, vec)]
+        + [pl.BlockSpec(memory_space=pl.ANY)] * (2 * count),
         out_specs=[whole(s) for s, _ in shapes], out_shape=[jax.ShapeDtypeStruct(s, d) for s, d in shapes],
-        compiler_params=pltpu.CompilerParams(vmem_limit_bytes=62 << 20), name="enc_forward",
-        cost_estimate=pl.CostEstimate(flops=2 * n * 8552448, transcendentals=n * FF, bytes_accessed=26 << 20),
-    )(x, pos, wr, wc, vec)
-
-def enc_bwd_body(clips, seen, dp_ref, h_ref, qkv_ref, h1_ref, inner_ref, enc_ref, wr_ref, wc_ref, v_ref,
-                 gdown_ref, gup_ref, gwide_ref, gin_ref, s_ref, sup_ref, most_ref):
+        scratch_shapes=weight_scratch(row_sources, col_sources, shard),
+        compiler_params=pltpu.CompilerParams(vmem_limit_bytes=62 << 20), name="enc_forward", cost_estimate=cost(19),
+    )(at, x, pos, vec, *row_sources, *col_sources)
+
+def enc_bwd_body(clips, seen, count, at_ref, dp_ref, h_ref, qkv_ref, h1_ref, inner_ref, enc_ref, v_ref, *refs):
+    row_sources, col_sources = refs[:count], refs[count:2 * count]
+    (gdown_ref, gup_ref, gwide_ref, gin_ref, s_ref, sup_ref, most_ref, wr_ref, wc_ref, row_sems, col_sems) = refs[2 * count:]
+    row_copies = fetches(at_ref, row_sources, wr_ref, row_sems)
+    col_copies = fetches(at_ref, col_sources, wc_ref, col_sems)
+    for copy in row_copies + col_copies: copy.start()
+    for copy in row_copies: copy.wait()
     sf, invf = ln(enc_ref[...])
     up = dot(dp_ref[...], wr_ref[:, PROJ], NT)
     s_ref[4:5, :] = col(up * sf); s_ref[5:6, :] = col(up)
@@ -388,6 +423,7 @@
     dl = dout.astype(bf16)
     gdown_ref[...] = dl
     s_ref[6:7, :] = col(dl.astype(f32))
+    for copy in col_copies: copy.wait()
     din = (dot(dl, wc_ref[PATCH:], NT) * gelu_parts(inner_ref[...])[1]).astype(bf16)
     gup_ref[...] = din
     sup_ref[...] = col(din.astype(f32))
@@ -427,16 +463,18 @@
     for at, y in enumerate((gin, dl, gwide_ref[:, :3 * D], bl, din)):
         most_ref[at:at + 1, :] = jnp.broadcast_to(most(y).reshape(1, 1), (1, 128))
 
-def enc_bwd(dp, h, qkv, h1, inner, enc, wr, wc, vec, clips, seen):
+def enc_bwd(at, dp, h, qkv, h1, inner, enc, vec, row_sources, col_sources, clips, seen, shard):
     n = h.shape[0]
     shapes = [((n, D), bf16), ((n, FF), bf16), ((n, 4 * D), bf16), ((n, D), bf16), ((8, D), f32), ((1, FF), f32), ((8, 128), f32)]
-    ins = (dp, h, qkv, h1, inner, enc, wr, wc, vec)
-    return pl.pallas_call(functools.partial(enc_bwd_body, clips, seen),
-        in_specs=[whole(a.shape) for a in ins],
+    ins = (dp, h, qkv, h1, inner, enc, vec)
+    count = len(row_sources)
+    return pl.pallas_call(functools.partial(enc_bwd_body, clips, seen, count),
+        in_specs=[pl.BlockSpec(memory_space=pltpu.SMEM)] + [whole(a.shape) for a in ins]
+        + [pl.BlockSpec(memory_space=pl.ANY)] * (2 * count),
         out_specs=[whole(s) for s, _ in shapes], out_shape=[jax.ShapeDtypeStruct(s, d) for s, d in shapes],
-        compiler_params=pltpu.CompilerParams(vmem_limit_bytes=62 << 20), name="enc_backward",
-        cost_estimate=pl.CostEstimate(flops=2 * n * 8552448, transcendentals=n * FF, bytes_accessed=28 << 20),
-    )(*ins)
+        scratch_shapes=weight_scratch(row_sources, col_sources, shard),
+        compiler_params=pltpu.CompilerParams(vmem_limit_bytes=62 << 20), name="enc_backward", cost_estimate=cost(27),
+    )(at, *ins, *row_sources, *col_sources)
 
 def pair_body(al_ref, bl_ref, ar_ref, br_ref, o_ref):
     o_ref[...] = dot(al_ref[0], ar_ref[0], TN) + dot(bl_ref[0], br_ref[0], TN)
@@ -448,7 +486,7 @@
     return pl.pallas_call(pair_body, grid=(rows // bm, cols // bn), in_specs=[ls, ls, rs, rs],
         out_specs=pl.BlockSpec((bm, bn), lambda i, j: (i, j)), out_shape=jax.ShapeDtypeStruct((rows, cols), f32),
         compiler_params=pltpu.CompilerParams(vmem_limit_bytes=60 << 20), name=name,
-        cost_estimate=pl.CostEstimate(flops=4 * n * rows * cols, transcendentals=0, bytes_accessed=4 * rows * cols),
+        cost_estimate=cost(8),
     )(lefts[0], lefts[1], rights[0], rights[1])
 def dec_parts(dec_low_rows, dec_low_fc2):
     mats = (
@@ -467,14 +505,21 @@
     return (master - learn_rate * (stepped + decay_rate * master), new_one, new_two)
 
 
-BLOCK = 480
+BLOCK = 720
 
 
 def sinusoid_at(places, feat_width):
     column = jnp.arange(feat_width)
     expo = (2 * (column // 2)).astype(jnp.float32) / feat_width
     angles = places.astype(jnp.float32)[..., None] / jnp.power(jnp.float32(10000.0), expo)
-    return jnp.where(column % 2 == 0, jnp.sin(angles), jnp.cos(angles))
+    turns = jnp.round(angles * 0.6366197723675814)
+    r = ((angles - turns * 1.5703125) - turns * 4.837512969970703125e-4) - turns * 7.54978995489188216e-8
+    z = r * r
+    sine = ((-1.9515295891e-4 * z + 8.3321608736e-3) * z - 1.6666654611e-1) * z * r + r
+    cosine = ((2.443315711809948e-5 * z - 1.388731625493765e-3) * z + 4.166664568298827e-2) * z * z - 0.5 * z + 1.0
+    quarter = turns.astype(jnp.int32) + column % 2
+    value = jnp.where(quarter % 2 == 0, sine, cosine)
+    return jnp.where(quarter % 4 < 2, value, -value)
 
 
 def bit_of(name, hop):
@@ -566,13 +611,13 @@
                     parts[at] = both * (1.0 / scale)
         return parts
 
-    def spread(self, pieces, turns, core):
+    def spread(self, pieces, turns, core, across=None):
         pieces = list(pieces)
         rest = self.inner[1:]
         orders = []
         for turn in turns:
             turn = turn % len(rest) if rest else 0
-            orders.append(rest[turn:] + rest[:turn] + (self.inner[:1] if core else []))
+            orders.append(rest[turn:] + rest[:turn] + (self.inner[:1] if (core if across is None else across) else []))
         for step in range(len(orders[0])):
             moving = yield [self.swap(piece, order[step]) for piece, order in zip(pieces, orders)]
             pieces = [
@@ -619,13 +664,21 @@
     return (yield [links.swap(value, hop) for value in values])
 
 
-def over_all(links, value, combine, skip=()):
-    for name, size in links.sizes:
-        for k in range(size.bit_length() - 1):
-            if (name, 1 << k) not in skip:
-                other = yield links.swap(value, (name, 1 << k))
-                value = combine(value, other)
+def over_all(links, value, combine, hops):
+    for hop in hops:
+        if isinstance(hop[0], tuple):
+            near, far = hop
+            both = (near[0], near[1] ^ far[1])
+            came = yield [links.swap(value, each) for each in (near, far, both)]
+            value = combine(combine(value, came[0]), combine(came[1], came[2]))
+        else:
+            other = yield links.swap(value, hop)
+            value = combine(value, other)
     return value
+
+
+def paired(hops):
+    return [tuple(hops[:2])] + hops[2:] if len(hops) > 1 else hops
 
 
 def from_owners(links, owned, fars):
@@ -668,56 +721,65 @@
     vec_own = masters[4].astype(jnp.bfloat16).reshape(1, -1)
     fars = range(1, shard)
     first = Steps(from_owners(links, blocks[:2] + [vec_own], fars))
-    counts = Steps(over_all(links, jnp.sum(loss_counts).astype(jnp.float32).reshape(1), jnp.add))
+    core, inner, outer, owners = links.inner[:1], links.inner[1:], links.outer, links.owners
+    counts = jnp.sum(loss_counts).astype(jnp.float32).reshape(1)
+    counts = Steps(over_all(links, counts, jnp.add, core + inner[:1] + owners + inner[1:] + outer))
 
     seen_idx = jnp.pad(visible_idx, ((0, 0), (0, seen_rows - seen_count)), constant_values=-1)
     hidden_idx = jnp.pad(masked_idx, ((0, 0), (0, query_rows - hidden_count)), constant_values=-1)
     seen_pixels = None
     for clip in range(seq_count):
         seen_pixels = pick_rows(clips, seen_idx, seen_rows, clip, "pick_seen", seen_pixels)
+    seen_pixels = arrive([counts], seen_pixels)
     lows = [master.astype(jnp.bfloat16) for master in masters[:4]]
-    seen_pixels, lows, hidden_idx, dec_blocks = arrive([first, counts], (seen_pixels, lows, hidden_idx, blocks[2:]))
-    enc_came = [came[:2] for came in first.result]
+    place_seen = jnp.pad(sinusoid_at(visible_idx, D), ((0, 0), (0, seen_rows - seen_count), (0, 0)))
+    place_seen, seen_pixels, lows, hidden_idx = arrive(
+        [counts, first], (place_seen, seen_pixels, lows, hidden_idx)
+    )
+    enc_came = [block for came in first.result for block in came[:2]]
     vec_parts = [came[2] for came in first.result]
-    share = Steps(links.spread([block for came in enc_came for block in came], (0, 1) * len(fars), True))
-    second = Steps(from_owners(links, dec_blocks, fars))
-
-    pixels = None
-    for clip in range(seq_count):
-        pixels = pick_rows(clips, hidden_idx, BLOCK, clip, "pick_hidden", pixels)
-        if clip == 0:
-            pixels, hidden_idx, visible_idx, masked_idx, vec_own, vec_parts = arrive(
-                [share, counts, second], (pixels, hidden_idx, visible_idx, masked_idx, vec_own, vec_parts)
-            )
-    dec_share = Steps(links.spread([block for came in second.result for block in came], (0, 1) * len(fars), True))
+    share = Steps(links.spread(enc_came, (0, 1) * len(fars), True, False))
     vec = assembled(vec_own, vec_parts, me).reshape(1, -1).astype(jnp.float32)
     token = vec[:, DEC_VEC - DD : DEC_VEC]
-    place = (
-        jnp.pad(sinusoid_at(visible_idx, D), ((0, 0), (0, seen_rows - seen_count), (0, 0))),
-        jnp.concatenate([sinusoid_at(masked_idx, DD) + token, sinusoid_at(visible_idx, DD)], axis=1),
-    )
-    pixels, place = arrive([share, counts, dec_share], (pixels, place))
-    place = arrive([share, counts, dec_share], place)
+
+    pixels = pick_rows(clips, hidden_idx, BLOCK, 0, "pick_hidden")
+    pixels, hidden_idx, dec_blocks, order = arrive(
+        [share], (pixels, hidden_idx, blocks[2:], (masked_idx, visible_idx))
+    )
+    second = Steps(from_owners(links, dec_blocks, fars))
+    for clip in range(1, seq_count):
+        pixels = pick_rows(clips, hidden_idx, BLOCK, clip, "pick_hidden", pixels)
+    pixels, order = arrive([share, second], (pixels, order))
+    near = share.result
+    far_core = Steps(one_hop(links, near, core[0]))
+    dec_came = [block for came in second.result for block in came]
+    dec_share = Steps(links.spread(dec_came, (0, 1) * len(fars), True, True))
+    place = jnp.concatenate([sinusoid_at(order[0], DD) + token, sinusoid_at(order[1], DD)], axis=1)
+    place, place_seen, near = arrive([far_core, dec_share], (place, place_seen, near))
     flat = lambda whole: whole.reshape(-1, whole.shape[-1])
-    enc_low_rows, enc_low_cols = [
-        flat(assembled(lows[at], share.result[at :: 2], me)) for at in (0, 1)
+    halves = [(flat(mine), flat(other)) for mine, other in zip(near, far_core.result)]
+    sources = [
+        [lows[at]] + [half for pair_of in halves[at::2] for half in pair_of] for at in (0, 1)
     ]
+    at = jnp.stack([me, bit_of(*core[0])] + [(me - far) % shard for far in fars]).astype(jnp.int32)
     (enc_h, enc_qkv, enc_mid, enc_inner, encoded, projected, tall, pair, normed_two, latent, left_most) = enc_fwd(
-        seen_pixels.reshape(-1, PATCH), place[0].reshape(-1, D), enc_low_rows, enc_low_cols, vec, seq_count, seen_count
-    )
-    core = links.inner[0]
+        at, seen_pixels.reshape(-1, PATCH), place_seen.reshape(-1, D), vec, *sources, seq_count, seen_count, shard
+    )
+    projected, tall = arrive([counts, dec_share], (projected, tall))
+    core = core[0]
+    complete(dec_share)
     left_swap = Steps(one_hop(links, (tall, pair, normed_two), core))
-    complete(dec_share)
-    projected = arrive([counts], projected)
+    dec_low_rows, u_down = [
+        flat(assembled(lows[2 + k], dec_share.result[k::2], me)) for k in (0, 1)
+    ]
+    (u_qkv, u_out, u_up, _), w_head = dec_parts(dec_low_rows, u_down)
+
+    projected = projected.reshape(seq_count, seen_rows, DD)[:, :seen_count]
+    hidden = place.at[:, hidden_count:].add(projected)
+    qkv = arrive([counts], dec_qkv(hidden, u_qkv, vec, tube_count // 2))
+    mixed, log_sums = attn_fwd(qkv, DHEADS, query_rows, BLOCK)
+    log_sums = arrive([counts, left_swap], log_sums)
     count_sum = complete(counts)[0][0]
-    dec_low_rows, u_down = [flat(assembled(lows[2 + at], dec_share.result[at::2], me)) for at in (0, 1)]
-    (u_qkv, u_out, u_up, _), w_head = dec_parts(dec_low_rows, u_down)
-
-    projected = projected.reshape(seq_count, seen_rows, DD)[:, :seen_count]
-    hidden = place[1].at[:, hidden_count:].add(projected)
-    qkv = dec_qkv(hidden, u_qkv, vec, tube_count // 2)
-    mixed, log_sums = attn_fwd(qkv, DHEADS, query_rows, BLOCK)
-    log_sums = arrive([left_swap], log_sums)
     far_lefts = left_swap.result
     (middle_grad, mixed_grad, grad_row_part, grad_dec_fc2, narrow_grads, wide_grads, loss_part) = dec_post(
         loss_counts, (2.0 / (PATCH * count_sum)).reshape(1), hidden, mixed, pixels,
@@ -746,7 +808,7 @@
     proj_grad = arrive([late], proj_grad)
     dec_spread = Steps(links.spread(dec_sums, (0, 1), True))
     grad_down, grad_up, grad_wide, grad_in, enc_sums, up_sums, right_most = enc_bwd(
-        proj_grad, enc_h, enc_qkv, enc_mid, enc_inner, encoded, enc_low_rows, enc_low_cols, vec, seq_count, seen_count
+        at, proj_grad, enc_h, enc_qkv, enc_mid, enc_inner, encoded, vec, *sources, seq_count, seen_count, shard
     )
     grad_vectors = jnp.concatenate(
         [enc_sums[at] for at in range(6)] + [up_sums[0], enc_sums[6], one_grads[2], one_grads[0], one_grads[1]]
@@ -763,14 +825,15 @@
         jnp.stack([half_of(grad_in, b), half_of(grad_down, b)]),
     )
     right_swap = Steps(one_hop(links, shape_right(1 - bit), core))
-    rights = shape_right(bit)
+    rights = arrive([right_swap], shape_right(bit))
     norms = jnp.sqrt(left_most[:5, 0] * right_most[:5, 0])
     bounds = jnp.stack([norms[4], jnp.maximum(norms[2], norms[3]), jnp.maximum(norms[0], norms[1])])
     size = grad_vectors.shape[0]
     is_sum = lax.broadcasted_iota(jnp.int32, (1, size + 128), 1) < size + 1
     message = jnp.concatenate([grad_vectors, loss_part[0], bounds, jnp.zeros(124, jnp.float32)]).reshape(1, -1)
-    vector_flight = Steps(over_all(links, message, lambda x, y: jnp.where(is_sum, x + y, jnp.maximum(x, y))))
-    rights = arrive([right_swap, vector_flight, late, dec_spread], rights)
+    hops = [core] + inner[:1] + owners + paired(inner[1:] + outer)
+    vector_flight = Steps(over_all(links, message, lambda x, y: jnp.where(is_sum, x + y, jnp.maximum(x, y)), hops))
+    rights = arrive([vector_flight], rights)
     far_rights = right_swap.result
     wide_cols, tall_rows = 2 * D, PATCH + FF
     zero = lambda i, j: (0, 0, i)
@@ -808,10 +871,10 @@
     squares = jnp.float32(0.0)
     for part in enc_parts_sum + dec_sums + late_sums:
         squares = squares + jnp.sum(part * part)
-    norm = Steps(over_all(links, squares.reshape(1), jnp.add, links.outer))
-    while enc_spread.result is None:
+    norm = Steps(over_all(links, squares.reshape(1), jnp.add, [core] + owners + paired(inner)))
+    for _ in owners:
         arrive([norm])
-        arrive([norm, enc_spread])
+    arrive([norm, enc_spread])
     everyone = complete(norm)[0]
     loss = loss_sum / count_sum
     grad_norm = jnp.sqrt(everyone[0] + jnp.sum(vector_sum * vector_sum))
@@ -821,7 +884,14 @@
     dec_rows_sum, dec_fc2_sum, dec_qkv_sum, proj_sum = [
         flat_piece(piece) for piece in dec_spread.result + late_spread.result
     ]
-    halves = [flat_piece(piece) for piece in enc_spread.result]
+    own_vectors = lax.dynamic_slice_in_dim(vector_sum, me * masters[4].shape[0], masters[4].shape[0])
+    updates = {}
+    for index, gradient in (
+        (2, jnp.concatenate([dec_qkv_sum, dec_rows_sum], axis=1)), (3, dec_fc2_sum), (4, own_vectors),
+    ):
+        updates[index] = adam_update(masters[index], firsts[index], seconds[index], gradient * factor)
+    updates = arrive([enc_spread], updates)
+    halves = [flat_piece(piece) for piece in complete(enc_spread)[0]]
     other = [links.swap(half, core) for half in halves]
 
     def sided(mine, yours):
@@ -835,16 +905,10 @@
             wide_parts + [sided(halves[0], other[0]).astype(jnp.float32) * (1.0 / scales[0]), proj_sum], axis=1
         ),
         sided(halves[2], other[2]).astype(jnp.float32) * (1.0 / scales[2]),
-        jnp.concatenate([dec_qkv_sum, dec_rows_sum], axis=1),
-        dec_fc2_sum,
-        lax.dynamic_slice_in_dim(vector_sum, me * masters[4].shape[0], masters[4].shape[0]),
     ]
-    new_w, new_m, new_v = [], [], []
-    for index in range(5):
-        updated = adam_update(masters[index], firsts[index], seconds[index], grads[index] * factor)
-        new_w.append(updated[0])
-        new_m.append(updated[1])
-        new_v.append(updated[2])
+    for index in (0, 1):
+        updates[index] = adam_update(masters[index], firsts[index], seconds[index], grads[index] * factor)
+    new_w, new_m, new_v = [[updates[index][kind] for index in range(5)] for kind in range(3)]
     return (loss, grad_norm, *new_w, *new_m, *new_v, *[w.astype(jnp.bfloat16) for w in new_w])
 
 

time: 969 us -> 894 us (0.923)
  starting transfers between devices: 129 us -> 95.4 us
  other arithmetic: 223 us -> 206 us
  waiting for transfers between devices: 141 us -> 127 us
    ppermute x85 -> x87, starting transfers between devices: 122 us -> 88.9 us  [swap(): return lax.ppermute(value, name, [(i, i ^ hop) for i in range(size)])]
    add x2, other arithmetic: 27.7 us -> 8.73 us  [the longest x1 7.5 us: local(): sinusoid_at(order[0], DD) + token]
    ppermute x85 -> x87, waiting for transfers between devices: 141 us -> 127 us  [swap(): return lax.ppermute(value, name, [(i, i ^ hop) for i in range(size)])]
    sub x0 -> x3, other arithmetic: none -> 10.9 us  [adam_update(): master - learn_rate * (stepped + decay_rate * master)]
    select_n x33 -> x29, other arithmetic: 52 us -> 41.1 us  [join(): jnp.where(bit == 0, jnp.concatenate([mine, other], axis=dim), jnp.concate...]
  transfers between devices with their start and end apart: 90 -> 92, of which waited for: 22 -> 20; matrix products, arithmetic and copies ran while one was open for 21% -> 22% of each run, Pallas kernels for 35% -> 29%
where the time goes in v2:
time: 894 us; the launch traced here: 887 us
  Pallas kernels  383 us (43%)
  other arithmetic  206 us (23%)
  waiting for transfers between devices  127 us (14%)
  starting transfers between devices  95.4 us (11%)
  local copies, waits for them, and re-layouts  53.1 us (6%)
  between operations  22.6 us (3%)
    ppermute x87, waiting for transfers between devices, swap(): return lax.ppermute(value, name, [(i, i ^ hop) for i in range(size)])  127 us
    pallas_call x6, Pallas kernels, attn_bwd(): pl.pallas_call(functools.partial(bwd_body, 64 ** (-0.5), nb, 0), grid=(1,...  116 us
    ppermute x87, starting transfers between devices, swap(): return lax.ppermute(value, name, [(i, i ^ hop) for i in range(size)])  88.9 us
    pallas_call x1, Pallas kernels, dec_post(): pl.pallas_call(functools.partial(post_body, nb, R, keys), grid=(clips, nb...  64.1 us
    pallas_call x1, Pallas kernels, attn_fwd(): pl.pallas_call(body, grid=(clips, pairs, nb), in_specs=[pl.BlockSpec((1,...  63.8 us
    convert_element_type x5, other arithmetic, local(): w.astype(jnp.bfloat16)  48 us
    select_n x29, other arithmetic, join(): jnp.where(bit == 0, jnp.concatenate([mine, other], axis=dim), jnp.concate...  41.1 us
    pallas_call x4, Pallas kernels, pick_rows(): pl.pallas_call(pick_body, grid=(m // R,), in_specs=[pl.BlockSpec((1, R, 1...  33.6 us
  transfers between devices with their start and end apart: 92, of which 20 were waited for; matrix products, arithmetic and copies ran while one was open for 22% of the time, Pallas kernels for 29%

profile of v2, /device:TPU:0, one launch (start us, length us, event | category | flops | bytes accessed | tf_op | source)
XLA Modules:
  0.0 886.7 jit_solution(5325591067565065560)
XLA Ops:
  6.3 2.5 collective-permute-start.2
  16.3 4.3 pick_seen_0.1.refs_0_
  20.6 4.5 pick_seen_1.1
  27.3 2.7 negate_select_fusion.4
  30.6 6.8 convert_element_type.195.refs_0_
  44.1 2.9 collective-permute-start.1
  49.4 12.5 %pick_hidden_0.1.refs_0_ = bf16[2,1440,1536]{2,1,0:T(8,128)(2,1)} custom-call(s32[2,1440,1]{2,1,0:T(8,128)} %copy.80.idx_ref, bf16[2,1568,1536]{2,1,0:T(8,128)(2,1)} %x_ref.7), custom_call_target="tpu_custom_call" | custom-call | flops 11314285568 | tf_op jit(solution)/shard_map/pick_hidden_0/pallas_call | solution.py:299
  68.6 5.2 collective-permute-done.6
  73.8 2.7 collective-permute-done.5
  78.2 2.6 maximum_select_fusion.10
  88.0 12.2 %pick_hidden_1.1.t_ref = bf16[2,1440,1536]{2,1,0:T(8,128)(2,1)} custom-call(s32[2,1440,1]{2,1,0:T(8,128)} %copy.81.idx_ref, bf16[2,1568,1536]{2,1,0:T(8,128)(2,1)} %x_ref.7, bf16[2,1440,1536]{2,1,0:T(8,128)(2,1)} %pick_hidden_0.1.refs_0_), custom_call_target="tpu_custom_call", output_to_operand_aliasing={{}: (2, {})} | custom-call | flops 11314285568 | tf_op jit(solution)/shard_map/pick_hidden_1/pallas_call | solution.py:299
  103.6 4.3 collective-permute-done.7
  109.1 2.6 maximum_select_fusion.5
  114.9 7.5 fusion.7
  123.4 2.5 pad_maximum_fusion
  128.0 20.5 %enc_forward.1 = (f32[320,768]{1,0:T(8,128)}, bf16[320,2304]{1,0:T(8,128)(2,1)}, f32[320,768]{1,0:T(8,128)}, f32[320,3072]{1,0:T(8,128)}, f32[320,768]{1,0:T(8,1...) custom-call(s32[3]{0:T(128)} %pad_add_fusion.at_ref, ...), custom_call_target="tpu_custom_call" | custom-call | flops 20899999744 | tf_op jit(solution)/shard_map/enc_forward/pallas_call | solution.py:404
  162.1 9.4 %dec_qkv.1.q_ref.k_ref.v_ref = bf16[2,1568,1152]{2,1,0:T(8,128)(2,1)} custom-call(f32[2,1568,384]{2,1,0:T(8,128)} %scatter-add.4.h_ref, bf16[384,1152]{1,0:T(8,128)(2,1)} %slice.204.w_ref, f32[1,14592]{1,0:T(1,128)} %bitcast.182), custom_call_target="tpu_custom_call" | custom-call | flops 9900000256 | tf_op jit(solution)/shard_map/dec_qkv/pallas_call | solution.py:249
  171.5 63.8 %dec_attend_forward.1 = (bf16[2,1440,384]{2,1,0:T(8,128)(2,1)}, f32[6,2,2,720]{3,2,1,0:T(2,128)}) custom-call(bf16[2,1568,1152]{2,1,0:T(8,128)(2,1)} %dec_qkv.1.q_ref.k_ref.v_ref, bf16[2,1568,1152]{2,1,0:T(8,128)(2,1)} %dec_qkv.1.q_ref.k_ref.v_ref, bf16[2,1568,1152]{2,1,0:T(8,128)(2,1)} %dec_qkv.1.q_ref.k_ref.v_ref), custom_call_target="tpu_custom_call" | custom-call | flops 71499997184 | tf_op jit(solution)/shard_map/dec_attend_forward/pallas_call | solution.py:67
  236.6 4.0 collective-permute-start.21
  245.6 64.1 %dec_post.1 = (f32[2,1568,384]{2,1,0:T(8,128)}, bf16[2,1440,384]{2,1,0:T(8,128)(2,1)}, f32[384,3456]{1,0:T(8,128)}, f32[1536,384]{1,0:T(8,128)}, f32[8,384]{1,0:...) custom-call(s32[2]{0:T(128)} %cnt_ref.1, f32[1]{0:T(128)} %bitcast.32.inv_ref, f32[2,1568,384]{2,1,0:T(8,128)} %scatter-add.4.h_ref, ...), custom_call_target="tpu_custom_call" | custom-call | flops 73699999744 | tf_op jit(solution)/shard_map/dec_post/pallas_call | solution.py:233
  313.0 2.4 constant_dynamic-slice_fusion.18
  317.9 19.0 %dec_attend_backward_0_0.1 = (bf16[1,1568,128]{2,1,0:T(8,128)(2,1)}, bf16[1,1568,128]{2,1,0:T(8,128)(2,1)}, bf16[1,1568,128]{2,1,0:T(8,128)(2,1)}) custom-call(bf16[2,1568,1152]{2,1,0:T(8,128)(2,1)} %dec_qkv.1.q_ref.k_ref.v_ref, bf16[2,1568,1152]{2,1,0:T(8,128)(2,1)} %dec_qkv.1.q_ref.k_ref.v_ref, bf16[2,1568,1152]{2,1,0:T(8,128)(2,1)} %dec_qkv.1.q_ref.k_ref.v_ref, ...), custom_call_target="tpu_custom_call" | custom-call | flops 18699999232 | tf_op jit(solution)/shard_map/dec_attend_backward_0_0/pallas_call | solution.py:132
  336.9 2.8 dynamic-slice_add_fusion
  345.9 19.1 %dec_attend_backward_0_1.1 = (bf16[1,1568,128]{2,1,0:T(8,128)(2,1)}, bf16[1,1568,128]{2,1,0:T(8,128)(2,1)}, bf16[1,1568,128]{2,1,0:T(8,128)(2,1)}) custom-call(bf16[2,1568,1152]{2,1,0:T(8,128)(2,1)} %dec_qkv.1.q_ref.k_ref.v_ref, bf16[2,1568,1152]{2,1,0:T(8,128)(2,1)} %dec_qkv.1.q_ref.k_ref.v_ref, bf16[2,1568,1152]{2,1,0:T(8,128)(2,1)} %dec_qkv.1.q_ref.k_ref.v_ref, ...), custom_call_target="tpu_custom_call" | custom-call | flops 18699999232 | tf_op jit(solution)/shard_map/dec_attend_backward_0_1/pallas_call | solution.py:132
  365.0 6.2 collective-permute-done.27
  371.2 19.5 %dec_attend_backward_0_2.1 = (bf16[1,1568,128]{2,1,0:T(8,128)(2,1)}, bf16[1,1568,128]{2,1,0:T(8,128)(2,1)}, bf16[1,1568,128]{2,1,0:T(8,128)(2,1)}) custom-call(bf16[2,1568,1152]{2,1,0:T(8,128)(2,1)} %dec_qkv.1.q_ref.k_ref.v_ref, bf16[2,1568,1152]{2,1,0:T(8,128)(2,1)} %dec_qkv.1.q_ref.k_ref.v_ref, bf16[2,1568,1152]{2,1,0:T(8,128)(2,1)} %dec_qkv.1.q_ref.k_ref.v_ref, ...), custom_call_target="tpu_custom_call" | custom-call | flops 18699999232 | tf_op jit(solution)/shard_map/dec_attend_backward_0_2/pallas_call | solution.py:132
  397.9 11.8 %dec_qkv_back_0.1 = (bf16[1,1568,384]{2,1,0:T(8,128)(2,1)}, f32[384,1152]{1,0:T(8,128)}, f32[8,384]{1,0:T(8,128)}) custom-call(f32[2,1568,384]{2,1,0:T(8,128)} %scatter-add.4.h_ref, f32[2,1568,384]{2,1,0:T(8,128)} %get-tuple-element.285.dmid_ref, bf16[384,1152]{1,0:T(8,128)(2,1)} %slice.204.w_ref, f32[1,14592]{1,0:T(1,128)} %bitcast.184, ...), custom_call_target="tpu_custom_call" | custom-call | flops 11000000512 | tf_op jit(solution)/shard_map/dec_qkv_back_0/pallas_call | solution.py:284
  414.8 19.2 %dec_attend_backward_1_0.1 = (bf16[1,1568,128]{2,1,0:T(8,128)(2,1)}, bf16[1,1568,128]{2,1,0:T(8,128)(2,1)}, bf16[1,1568,128]{2,1,0:T(8,128)(2,1)}) custom-call(bf16[2,1568,1152]{2,1,0:T(8,128)(2,1)} %dec_qkv.1.q_ref.k_ref.v_ref, bf16[2,1568,1152]{2,1,0:T(8,128)(2,1)} %dec_qkv.1.q_ref.k_ref.v_ref, bf16[2,1568,1152]{2,1,0:T(8,128)(2,1)} %dec_qkv.1.q_ref.k_ref.v_ref, ...), custom_call_target="tpu_custom_call" | custom-call | flops 18699999232 | tf_op jit(solution)/shard_map/dec_attend_backward_1_0/pallas_call | solution.py:132
  434.5 2.6 collective-permute-start.34
  437.1 19.3 %dec_attend_backward_1_1.1 = (bf16[1,1568,128]{2,1,0:T(8,128)(2,1)}, bf16[1,1568,128]{2,1,0:T(8,128)(2,1)}, bf16[1,1568,128]{2,1,0:T(8,128)(2,1)}) custom-call(bf16[2,1568,1152]{2,1,0:T(8,128)(2,1)} %dec_qkv.1.q_ref.k_ref.v_ref, bf16[2,1568,1152]{2,1,0:T(8,128)(2,1)} %dec_qkv.1.q_ref.k_ref.v_ref, bf16[2,1568,1152]{2,1,0:T(8,128)(2,1)} %dec_qkv.1.q_ref.k_ref.v_ref, ...), custom_call_target="tpu_custom_call" | custom-call | flops 18699999232 | tf_op jit(solution)/shard_map/dec_attend_backward_1_1/pallas_call | solution.py:132
  456.5 19.5 %dec_attend_backward_1_2.1 = (bf16[1,1568,128]{2,1,0:T(8,128)(2,1)}, bf16[1,1568,128]{2,1,0:T(8,128)(2,1)}, bf16[1,1568,128]{2,1,0:T(8,128)(2,1)}) custom-call(bf16[2,1568,1152]{2,1,0:T(8,128)(2,1)} %dec_qkv.1.q_ref.k_ref.v_ref, bf16[2,1568,1152]{2,1,0:T(8,128)(2,1)} %dec_qkv.1.q_ref.k_ref.v_ref, bf16[2,1568,1152]{2,1,0:T(8,128)(2,1)} %dec_qkv.1.q_ref.k_ref.v_ref, ...), custom_call_target="tpu_custom_call" | custom-call | flops 18699999232 | tf_op jit(solution)/shard_map/dec_attend_backward_1_2/pallas_call | solution.py:132
  476.0 11.9 %dec_qkv_back_1.1 = (bf16[1,1568,384]{2,1,0:T(8,128)(2,1)}, f32[384,1152]{1,0:T(8,128)}, f32[8,384]{1,0:T(8,128)}) custom-call(f32[2,1568,384]{2,1,0:T(8,128)} %scatter-add.4.h_ref, f32[2,1568,384]{2,1,0:T(8,128)} %get-tuple-element.285.dmid_ref, bf16[384,1152]{1,0:T(8,128)(2,1)} %slice.204.w_ref, f32[1,14592]{1,0:T(1,128)} %bitcast.185, ...), custom_call_target="tpu_custom_call" | custom-call | flops 11000000512 | tf_op jit(solution)/shard_map/dec_qkv_back_1/pallas_call | solution.py:284
  497.4 28.0 %enc_backward.1 = (bf16[320,768]{1,0:T(8,128)(2,1)}, bf16[320,3072]{1,0:T(8,128)(2,1)}, bf16[320,3072]{1,0:T(8,128)(2,1)}, bf16[320,768]{1,0:T(8,128)(2,1)}, f32...) custom-call(s32[3]{0:T(128)} %pad_add_fusion.at_ref, bf16[320,384]{1,0:T(8,128)(2,1)} %bitcast.169, ...), custom_call_target="tpu_custom_call" | custom-call | flops 29699999744 | tf_op jit(solution)/shard_map/enc_backward/pallas_call | solution.py:471
  530.8 7.3 collective-permute-done.38
  565.7 6.8 grad_up.1
  572.6 6.4 collective-permute-done.48
  587.0 7.1 grad_wide.1
  597.2 2.4 collective-permute-start.57
  600.7 2.8 collective-permute-start.59
  603.5 10.0 %grad_tall.1 = f32[4608,384]{1,0:T(8,128)} custom-call(bf16[1,320,4608]{2,1,0:T(8,128)(2,1)} %bitcast.188, bf16[1,320,4608]{2,1,0:T(8,128)(2,1)} %bitcast.67.bl_ref, bf16[2,320,384]{2,1,0:T(8,128)(2,1)} %pad_maximum_fusion.1.ar_ref, bf16[2,320,384]{2,1,0:T(8,128)(2,1)} %collective-permute-done.43.br_ref), custom_call_target="tpu_custom_call" | custom-call | flops 8800000000 | tf_op jit(solution)/shard_map/grad_tall/pallas_call | solution.py:486
  614.4 4.8 multiply_convert_fusion
  620.5 3.6 multiply_convert_fusion.2
  633.4 22.1 %collective-permute-done.64 = f32[1,1,1,1,48,384]{5,4,3,2,1,0:T(8,128)} collective-permute-done((f32[1,1,1,1,48,384]{5,4,3,2,1,0:T(8,128)S(1)}, f32[1,1,1,1,48,384]{5,4,3,2,1,0:T(8,128)}, u32[]{:S(2)}, u32[]{:S(2)}) %collective-permute-start.64) | collective-permute-done | bytes 73760 | tf_op jit(solution)/shard_map/ppermute | solution.py:530
  655.5 3.9 collective-permute-done.62
  659.3 2.4 multiply_add_fusion.6
  663.0 2.5 multiply_add_fusion.4
  676.0 13.7 %collective-permute-done.69 = f32[1,1,1,2,48,384]{5,4,3,2,1,0:T(8,128)S(1)} collective-permute-done((f32[1,1,1,2,48,384]{5,4,3,2,1,0:T(8,128)S(1)}, f32[1,1,1,2,48,384]{5,4,3,2,1,0:T(8,128)S(1)}, u32[]{:S(2)}, u32[]{:S(2)}) %collective-permute-start.69) | collective-permute-done | bytes 147488 | tf_op jit(solution)/shard_map/ppermute | solution.py:530
  698.9 8.4 collective-permute-done.71
  711.2 3.0 collective-permute-start.76
  718.0 23.1 %collective-permute-done.75 = f16[1,1,1,96,1536]{4,3,2,1,0:T(8,128)(2,1)S(1)} collective-permute-done((f16[1,1,1,96,1536]{4,3,2,1,0:T(8,128)(2,1)S(1)}, f16[1,1,1,96,1536]{4,3,2,1,0:T(8,128)(2,1)S(1)}, u32[]{:S(2)}, u32[]{:S(2)}) %collective-permute-start.75) | collective-permute-done | bytes 294944 | tf_op jit(solution)/shard_map/ppermute | solution.py:530
  741.1 6.3 collective-permute-done.76
  747.4 9.2 %collective-permute-done.77 = f16[1,1,1,576,384]{4,3,2,1,0:T(8,128)(2,1)S(1)} collective-permute-done((f16[1,1,1,576,384]{4,3,2,1,0:T(8,128)(2,1)S(1)}, f16[1,1,1,576,384]{4,3,2,1,0:T(8,128)(2,1)S(1)}, u32[]{:S(2)}, u32[]{:S(2)}) %collective-permute-start.77) | collective-permute-done | bytes 442400 | tf_op jit(solution)/shard_map/ppermute | solution.py:530
  781.5 3.3 collective-permute-start.84
  784.8 2.4 collective-permute-start.85
  787.2 2.3 maximum_select_fusion.26
  791.5 2.3 maximum_select_fusion.25
  793.8 2.7 maximum_select_fusion.20
  799.7 8.0 multiply_subtract_fusion.2
  814.6 2.5 maximum_select_fusion.14
  817.2 3.1 maximum_select_fusion.15
  825.0 4.1 maximum_select_fusion.8
  834.2 4.9 convert_multiply_fusion
  839.1 24.1 %fusion.80 = (bf16[384,6528]{1,0:T(8,128)(2,1)}, f32[384,6528]{1,0:T(8,128)}, f32[384,6528]{1,0:T(8,128)}, f32[384,6528]{1,0:T(8,128)}) fusion(f32[384,6528]{1,0:T(8,128)} %param.25, f32[]{:T(128)S(6)} %min.3, f32[384,384]{1,0:T(8,128)} %bitcast.160, f32[384,3072]{1,0:T(8,128)} %convert_multiply_fusion, f32[384,768]{1,0:T(8,128)} %convert_multiply_fusion.2, ...), kind=kLoop, calls=%fused_computation.332 | loop fusion | flops 50135040 | bytes 75202560 | tf_op jit(solution)/shard_map/convert_element_type | solution.py:912
  863.3 21.0 %fusion.78 = (bf16[2304,768]{1,0:T(8,128)(2,1)}, f32[2304,768]{1,0:T(8,128)}, f32[2304,768]{1,0:T(8,128)}, f32[2304,768]{1,0:T(8,128)}) fusion(f32[2304,768]{1,0:T(8,128)} %param.26, f32[]{:T(128)S(6)} %min.3, f32[]{:T(128)S(6)} %div.277, f16[2304,384]{1,0:T(8,128)(2,1)} %bitcast.92, f16[2304,384]{1,0:T(8,128)(2,1)} %collective-permute-done.91, ...), kind=kLoop, calls=%fused_computation.331 | loop fusion | flops 38928384 | bytes 49545224 | tf_op jit(solution)/shard_map/convert_element_type | solution.py:912
  (506 shorter events, 218.5 us)
Async XLA Ops:
  2.6 40.8 %collective-permute-start = (f32[1]{0:T(128)}, f32[1]{0:T(128)}, u32[]{:S(2)}, u32[]{:S(2)}) collective-permute-start(f32[1]{0:T(128)} %bitcast.4), channel_id=1, source_target_pairs={{0,2},{2,0},{4,6},{6,4},{8,10},{10,8},{12,14},{14,12},{16,18},{18,... | collective-permute-start | bytes 20 | tf_op jit(solution)/shard_map/ppermute | solution.py:530
  6.3 41.5 %collective-permute-start.2 = (bf16[1,1,1,1,48,6528]{5,4,3,2,1,0:T(8,128)(2,1)}, bf16[1,1,1,1,48,6528]{5,4,3,2,1,0:T(8,128)(2,1)}, u32[]{:S(2)}, u32[]{:S(2)}) collective-permute-start(bf16[1,1,1,1,48,6528]{5,4,3,2,1,0:T(8,128)(2,1)} %dynamic-slice_convert_fusion), channel_id=1, source_target_pairs={{0,1},{1,0},{2,3},{3,2},{4,5},{5,4},{6,7},{7,6},{8,9},{9,8},{10,11... | collective-permute-start | bytes 1880072 | tf_op jit(solution)/shard_map/ppermute | solution.py:688
  10.8 37.0 %collective-permute-start.3 = (bf16[1,1,1,1,288,768]{5,4,3,2,1,0:T(8,128)(2,1)}, bf16[1,1,1,1,288,768]{5,4,3,2,1,0:T(8,128)(2,1)}, u32[]{:S(2)}, u32[]{:S(2)}) collective-permute-start(bf16[1,1,1,1,288,768]{5,4,3,2,1,0:T(8,128)(2,1)} %dynamic-slice_convert_fusion.1), channel_id=1, source_target_pairs={{0,1},{1,0},{2,3},{3,2},{4,5},{5,4},{6,7},{7,6},{8,9},{9,8},{10,11... | collective-permute-start | bytes 1327112 | tf_op jit(solution)/shard_map/ppermute | solution.py:688
  12.2 35.6 %collective-permute-start.4 = (bf16[1,7296]{1,0:T(2,128)(2,1)}, bf16[1,7296]{1,0:T(2,128)(2,1)}, u32[]{:S(2)}, u32[]{:S(2)}) collective-permute-start(bf16[1,7296]{1,0:T(2,128)(2,1)} %reshape.2735), channel_id=1, source_target_pairs={{0,1},{1,0},{2,3},{3,2},{4,5},{5,4},{6,7},{7,6},{8,9},{9,8},{10,11... | collective-permute-start | bytes 43784 | tf_op jit(solution)/shard_map/ppermute | solution.py:688
  62.0 14.6 %collective-permute-start.5 = (bf16[1,1,1,1,48,6528]{5,4,3,2,1,0:T(8,128)(2,1)}, bf16[1,1,1,1,48,6528]{5,4,3,2,1,0:T(8,128)(2,1)S(1)}, u32[]{:S(2)}, u32[]{:S(2)}) collective-permute-start(bf16[1,1,1,1,48,6528]{5,4,3,2,1,0:T(8,128)(2,1)} %collective-permute-done.2), channel_id=1, source_target_pairs={{0,4},{2,6},{4,0},{6,2},{8,12},{10,14},{12,8},{14,10},{16,20},{18,... | collective-permute-start | bytes 1880072 | tf_op jit(solution)/shard_map/ppermute | solution.py:530
  66.7 81.8 %collective-permute-start.15 = (f32[1]{0:T(128)}, f32[1]{0:T(128)}, u32[]{:S(2)}, u32[]{:S(2)}) collective-permute-start(f32[1]{0:T(128)} %add.707), channel_id=1, source_target_pairs={{0,1},{1,0},{2,3},{3,2},{4,5},{5,4},{6,7},{7,6},{8,9},{9,8},{10,11... | collective-permute-start | bytes 20 | tf_op jit(solution)/shard_map/ppermute | solution.py:530
  80.7 27.2 %collective-permute-start.7 = (bf16[1,1,2,1,48,6528]{5,4,3,2,1,0:T(8,128)(2,1)}, bf16[1,1,2,1,48,6528]{5,4,3,2,1,0:T(8,128)(2,1)S(1)}, u32[]{:S(2)}, u32[]{:S(2)}) collective-permute-start(bf16[1,1,2,1,48,6528]{5,4,3,2,1,0:T(8,128)(2,1)} %maximum_select_fusion.10), channel_id=1, source_target_pairs={{0,8},{2,10},{4,12},{6,14},{8,0},{10,2},{12,4},{14,6},{16,24},{18,... | collective-permute-start | bytes 3760136 | tf_op jit(solution)/shard_map/ppermute | solution.py:530
  84.5 19.1 %collective-permute-start.8 = (bf16[1,1,1,2,288,768]{5,4,3,2,1,0:T(8,128)(2,1)}, bf16[1,1,1,2,288,768]{5,4,3,2,1,0:T(8,128)(2,1)}, u32[]{:S(2)}, u32[]{:S(2)}) collective-permute-start(bf16[1,1,1,2,288,768]{5,4,3,2,1,0:T(8,128)(2,1)} %maximum_select_fusion.16), channel_id=1, source_target_pairs={{0,4},{2,6},{4,0},{6,2},{8,12},{10,14},{12,8},{14,10},{16,20},{18,... | collective-permute-start | bytes 2654216 | tf_op jit(solution)/shard_map/ppermute | solution.py:530
  86.0 17.1 %collective-permute-start.9 = (bf16[1,1,1,1,24,4608]{5,4,3,2,1,0:T(8,128)(2,1)S(1)}, bf16[1,1,1,1,24,4608]{5,4,3,2,1,0:T(8,128)(2,1)S(1)}, u32[]{:S(2)}, u32[]{:S(2)}) collective-permute-start(bf16[1,1,1,1,24,4608]{5,4,3,2,1,0:T(8,128)(2,1)S(1)} %copy-done.43), channel_id=1, source_target_pairs={{0,1},{1,0},{2,3},{3,2},{4,5},{5,4},{6,7},{7,6},{8,9},{9,8},{10,11... | collective-permute-start | bytes 663560 | tf_op jit(solution)/shard_map/ppermute | solution.py:688
  86.5 16.6 %collective-permute-start.10 = (bf16[1,1,1,1,96,384]{5,4,3,2,1,0:T(8,128)(2,1)S(1)}, bf16[1,1,1,1,96,384]{5,4,3,2,1,0:T(8,128)(2,1)S(1)}, u32[]{:S(2)}, u32[]{:S(2)}) collective-permute-start(bf16[1,1,1,1,96,384]{5,4,3,2,1,0:T(8,128)(2,1)S(1)} %copy-done.49), channel_id=1, source_target_pairs={{0,1},{1,0},{2,3},{3,2},{4,5},{5,4},{6,7},{7,6},{8,9},{9,8},{10,11... | collective-permute-start | bytes 221192 | tf_op jit(solution)/shard_map/ppermute | solution.py:688
  109.0 16.9 %collective-permute-start.11 = (bf16[1,1,2,2,48,6528]{5,4,3,2,1,0:T(8,128)(2,1)S(1)}, bf16[1,1,2,2,48,6528]{5,4,3,2,1,0:T(8,128)(2,1)S(1)}, u32[]{:S(2)}, u32[]{:S(2)}) collective-permute-start(bf16[1,1,2,2,48,6528]{5,4,3,2,1,0:T(8,128)(2,1)S(1)} %maximum_select_fusion.3), channel_id=1, source_target_pairs={{0,2},{2,0},{4,6},{6,4},{8,10},{10,8},{12,14},{14,12},{16,18},{18,... | collective-permute-start | bytes 7520264 | tf_op jit(solution)/shard_map/ppermute | solution.py:530
  111.7 14.2 %collective-permute-start.12 = (bf16[1,1,2,2,288,768]{5,4,3,2,1,0:T(8,128)(2,1)S(1)}, bf16[1,1,2,2,288,768]{5,4,3,2,1,0:T(8,128)(2,1)S(1)}, u32[]{:S(2)}, u32[]{:S(2)}) collective-permute-start(bf16[1,1,2,2,288,768]{5,4,3,2,1,0:T(8,128)(2,1)S(1)} %maximum_select_fusion.5), channel_id=1, source_target_pairs={{0,2},{2,0},{4,6},{6,4},{8,10},{10,8},{12,14},{14,12},{16,18},{18,... | collective-permute-start | bytes 5308424 | tf_op jit(solution)/shard_map/ppermute | solution.py:530
  111.8 14.1 %collective-permute-start.13 = (bf16[1,1,1,1,24,4608]{5,4,3,2,1,0:T(8,128)(2,1)S(1)}, bf16[1,1,1,1,24,4608]{5,4,3,2,1,0:T(8,128)(2,1)S(1)}, u32[]{:S(2)}, u32[]{:S(2)}) collective-permute-start(bf16[1,1,1,1,24,4608]{5,4,3,2,1,0:T(8,128)(2,1)S(1)} %collective-permute-done.9), channel_id=1, source_target_pairs={{0,4},{2,6},{4,0},{6,2},{8,12},{10,14},{12,8},{14,10},{16,20},{18,... | collective-permute-start | bytes 663560 | tf_op jit(solution)/shard_map/ppermute | solution.py:530
  126.0 22.5 %collective-permute-start.16 = (bf16[1,1,2,1,24,4608]{5,4,3,2,1,0:T(8,128)(2,1)S(1)}, bf16[1,1,2,1,24,4608]{5,4,3,2,1,0:T(8,128)(2,1)}, u32[]{:S(2)}, u32[]{:S(2)}) collective-permute-start(bf16[1,1,2,1,24,4608]{5,4,3,2,1,0:T(8,128)(2,1)S(1)} %maximum_select_fusion.29), channel_id=1, source_target_pairs={{0,8},{2,10},{4,12},{6,14},{8,0},{10,2},{12,4},{14,6},{16,24},{18,... | collective-permute-start | bytes 1327112 | tf_op jit(solution)/shard_map/ppermute | solution.py:530
  126.6 21.9 %collective-permute-start.17 = (bf16[1,1,1,2,96,384]{5,4,3,2,1,0:T(8,128)(2,1)S(1)}, bf16[1,1,1,2,96,384]{5,4,3,2,1,0:T(8,128)(2,1)S(1)}, u32[]{:S(2)}, u32[]{:S(2)}) collective-permute-start(bf16[1,1,1,2,96,384]{5,4,3,2,1,0:T(8,128)(2,1)S(1)} %maximum_select_fusion.38), channel_id=1, source_target_pairs={{0,4},{2,6},{4,0},{6,2},{8,12},{10,14},{12,8},{14,10},{16,20},{18,... | collective-permute-start | bytes 442376 | tf_op jit(solution)/shard_map/ppermute | solution.py:530
  152.2 92.8 %collective-permute-start.23 = (bf16[2,320,768]{2,1,0:T(8,128)(2,1)}, bf16[2,320,768]{2,1,0:T(8,128)(2,1)}, u32[]{:S(2)}, u32[]{:S(2)}) collective-permute-start(bf16[2,320,768]{2,1,0:T(8,128)(2,1)} %get-tuple-element.278.al_ref), channel_id=1, source_target_pairs={{0,2},{2,0},{4,6},{6,4},{8,10},{10,8},{12,14},{14,12},{16,18},{18,... | collective-permute-start | bytes 2949128 | tf_op jit(solution)/shard_map/ppermute | solution.py:530
  152.3 92.7 %collective-permute-start.24 = (bf16[320,768]{1,0:T(8,128)(2,1)}, bf16[320,768]{1,0:T(8,128)(2,1)}, u32[]{:S(2)}, u32[]{:S(2)}) collective-permute-start(bf16[320,768]{1,0:T(8,128)(2,1)} %get-tuple-element.279), channel_id=1, source_target_pairs={{0,2},{2,0},{4,6},{6,4},{8,10},{10,8},{12,14},{14,12},{16,18},{18,... | collective-permute-start | bytes 1474568 | tf_op jit(solution)/shard_map/ppermute | solution.py:530
  153.3 18.2 %collective-permute-start.20 = (f32[1]{0:T(128)}, f32[1]{0:T(128)}, u32[]{:S(2)}, u32[]{:S(2)}) collective-permute-start(f32[1]{0:T(128)} %add.709), channel_id=1, source_target_pairs={{0,8},{2,10},{4,12},{6,14},{8,0},{10,2},{12,4},{14,6},{16,24},{18,... | collective-permute-start | bytes 20 | tf_op jit(solution)/shard_map/ppermute | solution.py:530
  158.6 86.4 %collective-permute-start.22 = (bf16[320,4608]{1,0:T(8,128)(2,1)}, bf16[320,4608]{1,0:T(8,128)(2,1)}, u32[]{:S(2)}, u32[]{:S(2)}) collective-permute-start(bf16[320,4608]{1,0:T(8,128)(2,1)} %get-tuple-element.277), channel_id=1, source_target_pairs={{0,2},{2,0},{4,6},{6,4},{8,10},{10,8},{12,14},{14,12},{16,18},{18,... | collective-permute-start | bytes 8847368 | tf_op jit(solution)/shard_map/ppermute | solution.py:530
  311.7 25.2 %collective-permute-start.25 = (f32[2,1,2,2,24,3456]{5,4,3,2,1,0:T(8,128)S(1)}, f32[2,1,2,2,24,3456]{5,4,3,2,1,0:T(8,128)}, u32[]{:S(2)}, u32[]{:S(2)}) collective-permute-start(f32[2,1,2,2,24,3456]{5,4,3,2,1,0:T(8,128)S(1)} %constant_dynamic-slice_fusion.19), channel_id=1, source_target_pairs={{0,2},{2,0},{4,6},{6,4},{8,10},{10,8},{12,14},{14,12},{16,18},{18,... | collective-permute-start | bytes 7962632 | tf_op jit(solution)/shard_map/ppermute | solution.py:530
  315.3 21.6 %collective-permute-start.26 = (f32[2,1,2,2,96,384]{5,4,3,2,1,0:T(8,128)}, f32[2,1,2,2,96,384]{5,4,3,2,1,0:T(8,128)}, u32[]{:S(2)}, u32[]{:S(2)}) collective-permute-start(f32[2,1,2,2,96,384]{5,4,3,2,1,0:T(8,128)} %constant_dynamic-slice_fusion.18), channel_id=1, source_target_pairs={{0,2},{2,0},{4,6},{6,4},{8,10},{10,8},{12,14},{14,12},{16,18},{18,... | collective-permute-start | bytes 3538952 | tf_op jit(solution)/shard_map/ppermute | solution.py:530
  339.9 31.3 %collective-permute-start.27 = (f32[2,1,1,2,24,3456]{5,4,3,2,1,0:T(8,128)S(1)}, f32[2,1,1,2,24,3456]{5,4,3,2,1,0:T(8,128)}, u32[]{:S(2)}, u32[]{:S(2)}) collective-permute-start(f32[2,1,1,2,24,3456]{5,4,3,2,1,0:T(8,128)S(1)} %constant_dynamic-slice_fusion.17), channel_id=1, source_target_pairs={{0,4},{2,6},{4,0},{6,2},{8,12},{10,14},{12,8},{14,10},{16,20},{18,... | collective-permute-start | bytes 3981320 | tf_op jit(solution)/shard_map/ppermute | solution.py:530
  344.7 20.3 %collective-permute-start.28 = (f32[2,1,2,1,96,384]{5,4,3,2,1,0:T(8,128)}, f32[2,1,2,1,96,384]{5,4,3,2,1,0:T(8,128)}, u32[]{:S(2)}, u32[]{:S(2)}) collective-permute-start(f32[2,1,2,1,96,384]{5,4,3,2,1,0:T(8,128)} %constant_dynamic-slice_fusion.16), channel_id=1, source_target_pairs={{0,8},{2,10},{4,12},{6,14},{8,0},{10,2},{12,4},{14,6},{16,24},{18,... | collective-permute-start | bytes 1769480 | tf_op jit(solution)/shard_map/ppermute | solution.py:530
  392.2 18.3 %collective-permute-start.29 = (f32[2,1,1,1,24,3456]{5,4,3,2,1,0:T(8,128)S(1)}, f32[2,1,1,1,24,3456]{5,4,3,2,1,0:T(8,128)S(1)}, u32[]{:S(2)}, u32[]{:S(2)}) collective-permute-start(f32[2,1,1,1,24,3456]{5,4,3,2,1,0:T(8,128)S(1)} %constant_dynamic-slice_fusion.15), channel_id=1, source_target_pairs={{0,8},{2,10},{4,12},{6,14},{8,0},{10,2},{12,4},{14,6},{16,24},{18,... | collective-permute-start | bytes 1990664 | tf_op jit(solution)/shard_map/ppermute | solution.py:530
  395.4 15.2 %collective-permute-start.30 = (f32[1,1,2,1,96,384]{5,4,3,2,1,0:T(8,128)}, f32[1,1,2,1,96,384]{5,4,3,2,1,0:T(8,128)S(1)}, u32[]{:S(2)}, u32[]{:S(2)}) collective-permute-start(f32[1,1,2,1,96,384]{5,4,3,2,1,0:T(8,128)} %constant_dynamic-slice_fusion.14), channel_id=1, source_target_pairs={{0,1},{1,0},{2,3},{3,2},{4,5},{5,4},{6,7},{7,6},{8,9},{9,8},{10,11... | collective-permute-start | bytes 884744 | tf_op jit(solution)/shard_map/ppermute | solution.py:530
  411.4 22.6 %collective-permute-start.31 = (f32[1,1,1,1,24,3456]{5,4,3,2,1,0:T(8,128)S(1)}, f32[1,1,1,1,24,3456]{5,4,3,2,1,0:T(8,128)S(1)}, u32[]{:S(2)}, u32[]{:S(2)}) collective-permute-start(f32[1,1,1,1,24,3456]{5,4,3,2,1,0:T(8,128)S(1)} %constant_dynamic-slice_fusion.13), channel_id=1, source_target_pairs={{0,1},{1,0},{2,3},{3,2},{4,5},{5,4},{6,7},{7,6},{8,9},{9,8},{10,11... | collective-permute-start | bytes 995336 | tf_op jit(solution)/shard_map/ppermute | solution.py:530
  414.0 20.0 %collective-permute-start.32 = (f32[1,1,1,1,96,384]{5,4,3,2,1,0:T(8,128)S(1)}, f32[1,1,1,1,96,384]{5,4,3,2,1,0:T(8,128)S(1)}, u32[]{:S(2)}, u32[]{:S(2)}) collective-permute-start(f32[1,1,1,1,96,384]{5,4,3,2,1,0:T(8,128)S(1)} %constant_dynamic-slice_fusion.12), channel_id=1, source_target_pairs={{0,4},{2,6},{4,0},{6,2},{8,12},{10,14},{12,8},{14,10},{16,20},{18,... | collective-permute-start | bytes 442376 | tf_op jit(solution)/shard_map/ppermute | solution.py:530
  434.1 22.4 %collective-permute-start.33 = (f32[1,1,1,1,24,3456]{5,4,3,2,1,0:T(8,128)S(1)}, f32[1,1,1,1,24,3456]{5,4,3,2,1,0:T(8,128)S(1)}, u32[]{:S(2)}, u32[]{:S(2)}) collective-permute-start(f32[1,1,1,1,24,3456]{5,4,3,2,1,0:T(8,128)S(1)} %dynamic-slice_add_fusion.8), channel_id=1, source_target_pairs={{0,16},{2,18},{4,20},{6,22},{8,24},{10,26},{12,28},{14,30},{16,0},... | collective-permute-start | bytes 995336 | tf_op jit(solution)/shard_map/ppermute | solution.py:530
  434.5 21.9 %collective-permute-start.34 = (f32[1,1,1,1,96,384]{5,4,3,2,1,0:T(8,128)S(1)}, f32[1,1,1,1,96,384]{5,4,3,2,1,0:T(8,128)S(1)}, u32[]{:S(2)}, u32[]{:S(2)}) collective-permute-start(f32[1,1,1,1,96,384]{5,4,3,2,1,0:T(8,128)S(1)} %dynamic-slice_add_fusion.13), channel_id=1, source_target_pairs={{0,16},{2,18},{4,20},{6,22},{8,24},{10,26},{12,28},{14,30},{16,0},... | collective-permute-start | bytes 442376 | tf_op jit(solution)/shard_map/ppermute | solution.py:530
  493.0 37.8 %collective-permute-start.39 = (f32[1,1,1,1,24,3456]{5,4,2,3,1,0:T(8,128)}, f32[1,1,1,1,24,3456]{5,4,2,3,1,0:T(8,128)}, u32[]{:S(2)}, u32[]{:S(2)}) collective-permute-start(f32[1,1,1,1,24,3456]{5,4,2,3,1,0:T(8,128)} %get-tuple-element.480), channel_id=1, source_target_pairs={{0,4},{2,6},{4,0},{6,2},{8,12},{10,14},{12,8},{14,10},{16,20},{18,... | collective-permute-start | bytes 995336 | tf_op jit(solution)/shard_map/ppermute | solution.py:530
  494.9 35.8 %collective-permute-start.40 = (f32[1,1,1,1,96,384]{5,4,3,2,1,0:T(8,128)S(1)}, f32[1,1,1,1,96,384]{5,4,3,2,1,0:T(8,128)}, u32[]{:S(2)}, u32[]{:S(2)}) collective-permute-start(f32[1,1,1,1,96,384]{5,4,3,2,1,0:T(8,128)S(1)} %get-tuple-element.469), channel_id=1, source_target_pairs={{0,8},{2,10},{4,12},{6,14},{8,0},{10,2},{12,4},{14,6},{16,24},{18,... | collective-permute-start | bytes 442376 | tf_op jit(solution)/shard_map/ppermute | solution.py:530
  542.2 20.6 %collective-permute-start.41 = (bf16[1,320,1536]{2,1,0:T(8,128)(2,1)}, bf16[1,320,1536]{2,1,0:T(8,128)(2,1)}, u32[]{:S(2)}, u32[]{:S(2)}) collective-permute-start(bf16[1,320,1536]{2,1,0:T(8,128)(2,1)} %get-tuple-element.472), channel_id=1, source_target_pairs={{0,2},{2,0},{4,6},{6,4},{8,10},{10,8},{12,14},{14,12},{16,18},{18,... | collective-permute-start | bytes 2949128 | tf_op jit(solution)/shard_map/ppermute | solution.py:530
  543.4 20.1 %collective-permute-start.42 = (bf16[1,320,1536]{2,1,0:T(8,128)(2,1)}, bf16[1,320,1536]{2,1,0:T(8,128)(2,1)}, u32[]{:S(2)}, u32[]{:S(2)}) collective-permute-start(bf16[1,320,1536]{2,1,0:T(8,128)(2,1)} %maximum_bitcast_fusion.1), channel_id=1, source_target_pairs={{0,2},{2,0},{4,6},{6,4},{8,10},{10,8},{12,14},{14,12},{16,18},{18,... | collective-permute-start | bytes 2949128 | tf_op jit(solution)/shard_map/ppermute | solution.py:530
  545.6 16.5 %collective-permute-start.43 = (bf16[2,320,384]{2,1,0:T(8,128)(2,1)}, bf16[2,320,384]{2,1,0:T(8,128)(2,1)}, u32[]{:S(2)}, u32[]{:S(2)}) collective-permute-start(bf16[2,320,384]{2,1,0:T(8,128)(2,1)} %pad_maximum_fusion.2), channel_id=1, source_target_pairs={{0,2},{2,0},{4,6},{6,4},{8,10},{10,8},{12,14},{14,12},{16,18},{18,... | collective-permute-start | bytes 1474568 | tf_op jit(solution)/shard_map/ppermute | solution.py:530
  550.3 14.7 %collective-permute-start.44 = (f32[1,14720]{1,0:T(1,128)S(1)}, f32[1,14720]{1,0:T(1,128)S(1)}, u32[]{:S(2)}, u32[]{:S(2)}) collective-permute-start(f32[1,14720]{1,0:T(1,128)S(1)} %reshape.2750), channel_id=1, source_target_pairs={{0,2},{2,0},{4,6},{6,4},{8,10},{10,8},{12,14},{14,12},{16,18},{18,... | collective-permute-start | bytes 176648 | tf_op jit(solution)/shard_map/ppermute | solution.py:530
  552.6 20.0 %collective-permute-start.46 = (f32[2,1,1,1,24,1152]{5,4,3,2,1,0:T(8,128)}, f32[2,1,1,1,24,1152]{5,4,3,2,1,0:T(8,128)}, u32[]{:S(2)}, u32[]{:S(2)}) collective-permute-start(f32[2,1,1,1,24,1152]{5,4,3,2,1,0:T(8,128)} %constant_dynamic-slice_fusion.3), channel_id=1, source_target_pairs={{0,8},{2,10},{4,12},{6,14},{8,0},{10,2},{12,4},{14,6},{16,24},{18,... | collective-permute-start | bytes 663560 | tf_op jit(solution)/shard_map/ppermute | solution.py:530
  562.7 16.3 %collective-permute-start.48 = (f32[1,1,2,1,24,3456]{5,4,2,3,1,0:T(8,128)S(1)}, f32[1,1,2,1,24,3456]{5,4,2,3,1,0:T(8,128)S(1)}, u32[]{:S(2)}, u32[]{:S(2)}) collective-permute-start(f32[1,1,2,1,24,3456]{5,4,2,3,1,0:T(8,128)S(1)} %maximum_select_fusion.21), channel_id=1, source_target_pairs={{0,8},{2,10},{4,12},{6,14},{8,0},{10,2},{12,4},{14,6},{16,24},{18,... | collective-permute-start | bytes 1990664 | tf_op jit(solution)/shard_map/ppermute | solution.py:530
  579.1 15.0 %collective-permute-start.50 = (f32[1,14720]{1,0:T(1,128)S(1)}, f32[1,14720]{1,0:T(1,128)}, u32[]{:S(2)}, u32[]{:S(2)}) collective-permute-start(f32[1,14720]{1,0:T(1,128)S(1)} %maximum_select_fusion.44), channel_id=1, source_target_pairs={{0,1},{1,0},{2,3},{3,2},{4,5},{5,4},{6,7},{7,6},{8,9},{9,8},{10,11... | collective-permute-start | bytes 176648 | tf_op jit(solution)/shard_map/ppermute | solution.py:530
  595.1 18.4 %collective-permute-start.55 = (f32[1,14720]{1,0:T(1,128)S(1)}, f32[1,14720]{1,0:T(1,128)S(1)}, u32[]{:S(2)}, u32[]{:S(2)}) collective-permute-start(f32[1,14720]{1,0:T(1,128)S(1)} %maximum_select_fusion.43), channel_id=1, source_target_pairs={{0,8},{2,10},{4,12},{6,14},{8,0},{10,2},{12,4},{14,6},{16,24},{18,... | collective-permute-start | bytes 176648 | tf_op jit(solution)/shard_map/ppermute | solution.py:530
  596.8 16.8 %collective-permute-start.56 = (f32[1,14720]{1,0:T(1,128)S(1)}, f32[1,14720]{1,0:T(1,128)S(1)}, u32[]{:S(2)}, u32[]{:S(2)}) collective-permute-start(f32[1,14720]{1,0:T(1,128)S(1)} %maximum_select_fusion.43), channel_id=1, source_target_pairs={{0,16},{2,18},{4,20},{6,22},{8,24},{10,26},{12,28},{14,30},{16,0},... | collective-permute-start | bytes 176648 | tf_op jit(solution)/shard_map/ppermute | solution.py:530
  597.2 16.4 %collective-permute-start.57 = (f32[1,14720]{1,0:T(1,128)S(1)}, f32[1,14720]{1,0:T(1,128)S(1)}, u32[]{:S(2)}, u32[]{:S(2)}) collective-permute-start(f32[1,14720]{1,0:T(1,128)S(1)} %maximum_select_fusion.43), channel_id=1, source_target_pairs={{0,24},{2,26},{4,28},{6,30},{8,16},{10,18},{12,20},{14,22},{16,8},... | collective-permute-start | bytes 176648 | tf_op jit(solution)/shard_map/ppermute | solution.py:530
  619.2 40.1 %collective-permute-start.62 = (f16[1,2,2,576,384]{4,3,2,1,0:T(8,128)(2,1)}, f16[1,2,2,576,384]{4,3,2,1,0:T(8,128)(2,1)S(1)}, u32[]{:S(2)}, u32[]{:S(2)}) collective-permute-start(f16[1,2,2,576,384]{4,3,2,1,0:T(8,128)(2,1)} %multiply_convert_fusion), channel_id=1, source_target_pairs={{0,1},{1,0},{2,3},{3,2},{4,5},{5,4},{6,7},{7,6},{8,9},{9,8},{10,11... | collective-permute-start | bytes 5308424 | tf_op jit(solution)/shard_map/ppermute | solution.py:530
  624.1 31.4 %collective-permute-start.60 = (f16[2,1,2,96,1536]{4,3,2,1,0:T(8,128)(2,1)}, f16[2,1,2,96,1536]{4,3,2,1,0:T(8,128)(2,1)}, u32[]{:S(2)}, u32[]{:S(2)}) collective-permute-start(f16[2,1,2,96,1536]{4,3,2,1,0:T(8,128)(2,1)} %multiply_convert_fusion.2), channel_id=1, source_target_pairs={{0,4},{2,6},{4,0},{6,2},{8,12},{10,14},{12,8},{14,10},{16,20},{18,... | collective-permute-start | bytes 3538952 | tf_op jit(solution)/shard_map/ppermute | solution.py:530
  627.3 28.2 %collective-permute-start.61 = (f16[2,2,1,96,1536]{4,3,2,1,0:T(8,128)(2,1)}, f16[2,2,1,96,1536]{4,3,2,1,0:T(8,128)(2,1)}, u32[]{:S(2)}, u32[]{:S(2)}) collective-permute-start(f16[2,2,1,96,1536]{4,3,2,1,0:T(8,128)(2,1)} %multiply_convert_fusion.1), channel_id=1, source_target_pairs={{0,8},{2,10},{4,12},{6,14},{8,0},{10,2},{12,4},{14,6},{16,24},{18,... | collective-permute-start | bytes 3538952 | tf_op jit(solution)/shard_map/ppermute | solution.py:530
  627.9 27.5 %collective-permute-start.63 = (f32[1,1,1,1,24,1152]{5,4,2,3,1,0:T(8,128)S(1)}, f32[1,1,1,1,24,1152]{5,4,2,3,1,0:T(8,128)S(1)}, u32[]{:S(2)}, u32[]{:S(2)}) collective-permute-start(f32[1,1,1,1,24,1152]{5,4,2,3,1,0:T(8,128)S(1)} %get-tuple-element.493), channel_id=1, source_target_pairs={{0,4},{2,6},{4,0},{6,2},{8,12},{10,14},{12,8},{14,10},{16,20},{18,... | collective-permute-start | bytes 331784 | tf_op jit(solution)/shard_map/ppermute | solution.py:530
  630.0 25.5 %collective-permute-start.64 = (f32[1,1,1,1,48,384]{5,4,3,2,1,0:T(8,128)S(1)}, f32[1,1,1,1,48,384]{5,4,3,2,1,0:T(8,128)}, u32[]{:S(2)}, u32[]{:S(2)}) collective-permute-start(f32[1,1,1,1,48,384]{5,4,3,2,1,0:T(8,128)S(1)} %get-tuple-element.467), channel_id=1, source_target_pairs={{0,8},{2,10},{4,12},{6,14},{8,0},{10,2},{12,4},{14,6},{16,24},{18,... | collective-permute-start | bytes 221192 | tf_op jit(solution)/shard_map/ppermute | solution.py:530
  662.7 27.0 %collective-permute-start.65 = (f16[2,1,1,96,1536]{4,3,2,1,0:T(8,128)(2,1)S(1)}, f16[2,1,1,96,1536]{4,3,2,1,0:T(8,128)(2,1)S(1)}, u32[]{:S(2)}, u32[]{:S(2)}) collective-permute-start(f16[2,1,1,96,1536]{4,3,2,1,0:T(8,128)(2,1)S(1)} %multiply_convert_fusion.5), channel_id=1, source_target_pairs={{0,8},{2,10},{4,12},{6,14},{8,0},{10,2},{12,4},{14,6},{16,24},{18,... | collective-permute-start | bytes 1769480 | tf_op jit(solution)/shard_map/ppermute | solution.py:530
  666.4 23.3 %collective-permute-start.67 = (f16[1,1,2,576,384]{4,3,2,1,0:T(8,128)(2,1)S(1)}, f16[1,1,2,576,384]{4,3,2,1,0:T(8,128)(2,1)S(1)}, u32[]{:S(2)}, u32[]{:S(2)}) collective-permute-start(f16[1,1,2,576,384]{4,3,2,1,0:T(8,128)(2,1)S(1)} %multiply_convert_fusion.3), channel_id=1, source_target_pairs={{0,4},{2,6},{4,0},{6,2},{8,12},{10,14},{12,8},{14,10},{16,20},{18,... | collective-permute-start | bytes 2654216 | tf_op jit(solution)/shard_map/ppermute | solution.py:530
  669.6 20.1 %collective-permute-start.66 = (f16[1,2,1,96,1536]{4,3,2,1,0:T(8,128)(2,1)S(1)}, f16[1,2,1,96,1536]{4,3,2,1,0:T(8,128)(2,1)S(1)}, u32[]{:S(2)}, u32[]{:S(2)}) collective-permute-start(f16[1,2,1,96,1536]{4,3,2,1,0:T(8,128)(2,1)S(1)} %multiply_convert_fusion.4), channel_id=1, source_target_pairs={{0,1},{1,0},{2,3},{3,2},{4,5},{5,4},{6,7},{7,6},{8,9},{9,8},{10,11... | collective-permute-start | bytes 1769480 | tf_op jit(solution)/shard_map/ppermute | solution.py:530
  671.1 18.6 %collective-permute-start.68 = (f32[1,1,2,1,24,1152]{5,4,2,3,1,0:T(8,128)S(1)}, f32[1,1,2,1,24,1152]{5,4,2,3,1,0:T(8,128)S(1)}, u32[]{:S(2)}, u32[]{:S(2)}) collective-permute-start(f32[1,1,2,1,24,1152]{5,4,2,3,1,0:T(8,128)S(1)} %maximum_select_fusion.36), channel_id=1, source_target_pairs={{0,8},{2,10},{4,12},{6,14},{8,0},{10,2},{12,4},{14,6},{16,24},{18,... | collective-permute-start | bytes 663560 | tf_op jit(solution)/shard_map/ppermute | solution.py:530
  673.7 16.0 %collective-permute-start.69 = (f32[1,1,1,2,48,384]{5,4,3,2,1,0:T(8,128)S(1)}, f32[1,1,1,2,48,384]{5,4,3,2,1,0:T(8,128)S(1)}, u32[]{:S(2)}, u32[]{:S(2)}) collective-permute-start(f32[1,1,1,2,48,384]{5,4,3,2,1,0:T(8,128)S(1)} %maximum_select_fusion.40), channel_id=1, source_target_pairs={{0,4},{2,6},{4,0},{6,2},{8,12},{10,14},{12,8},{14,10},{16,20},{18,... | collective-permute-start | bytes 442376 | tf_op jit(solution)/shard_map/ppermute | solution.py:530
  709.2 31.9 %collective-permute-start.75 = (f16[1,1,1,96,1536]{4,3,2,1,0:T(8,128)(2,1)S(1)}, f16[1,1,1,96,1536]{4,3,2,1,0:T(8,128)(2,1)S(1)}, u32[]{:S(2)}, u32[]{:S(2)}) collective-permute-start(f16[1,1,1,96,1536]{4,3,2,1,0:T(8,128)(2,1)S(1)} %multiply_convert_fusion.12), channel_id=1, source_target_pairs={{0,16},{2,18},{4,20},{6,22},{8,24},{10,26},{12,28},{14,30},{16,0},... | collective-permute-start | bytes 884744 | tf_op jit(solution)/shard_map/ppermute | solution.py:530
  711.2 36.2 %collective-permute-start.76 = (f16[1,1,1,96,1536]{4,3,2,1,0:T(8,128)(2,1)S(1)}, f16[1,1,1,96,1536]{4,3,2,1,0:T(8,128)(2,1)S(1)}, u32[]{:S(2)}, u32[]{:S(2)}) collective-permute-start(f16[1,1,1,96,1536]{4,3,2,1,0:T(8,128)(2,1)S(1)} %multiply_convert_fusion.11), channel_id=1, source_target_pairs={{0,16},{2,18},{4,20},{6,22},{8,24},{10,26},{12,28},{14,30},{16,0},... | collective-permute-start | bytes 884744 | tf_op jit(solution)/shard_map/ppermute | solution.py:530
  716.0 40.6 %collective-permute-start.77 = (f16[1,1,1,576,384]{4,3,2,1,0:T(8,128)(2,1)S(1)}, f16[1,1,1,576,384]{4,3,2,1,0:T(8,128)(2,1)S(1)}, u32[]{:S(2)}, u32[]{:S(2)}) collective-permute-start(f16[1,1,1,576,384]{4,3,2,1,0:T(8,128)(2,1)S(1)} %multiply_convert_fusion.7), channel_id=1, source_target_pairs={{0,16},{2,18},{4,20},{6,22},{8,24},{10,26},{12,28},{14,30},{16,0},... | collective-permute-start | bytes 1327112 | tf_op jit(solution)/shard_map/ppermute | solution.py:530
  763.1 16.0 %collective-permute-start.80 = (f16[1,1,1,96,1536]{4,3,2,1,0:T(8,128)(2,1)}, f16[1,1,1,96,1536]{4,3,2,1,0:T(8,128)(2,1)}, u32[]{:S(2)}, u32[]{:S(2)}) collective-permute-start(f16[1,1,1,96,1536]{4,3,2,1,0:T(8,128)(2,1)} %get-tuple-element.483), channel_id=1, source_target_pairs={{0,4},{2,6},{4,0},{6,2},{8,12},{10,14},{12,8},{14,10},{16,20},{18,... | collective-permute-start | bytes 884744 | tf_op jit(solution)/shard_map/ppermute | solution.py:530
  763.5 15.7 %collective-permute-start.81 = (f16[1,1,1,96,1536]{4,3,2,1,0:T(8,128)(2,1)}, f16[1,1,1,96,1536]{4,3,2,1,0:T(8,128)(2,1)}, u32[]{:S(2)}, u32[]{:S(2)}) collective-permute-start(f16[1,1,1,96,1536]{4,3,2,1,0:T(8,128)(2,1)} %get-tuple-element.481), channel_id=1, source_target_pairs={{0,4},{2,6},{4,0},{6,2},{8,12},{10,14},{12,8},{14,10},{16,20},{18,... | collective-permute-start | bytes 884744 | tf_op jit(solution)/shard_map/ppermute | solution.py:530
  765.2 14.0 %collective-permute-start.82 = (f16[1,1,1,576,384]{4,3,2,1,0:T(8,128)(2,1)}, f16[1,1,1,576,384]{4,3,2,1,0:T(8,128)(2,1)}, u32[]{:S(2)}, u32[]{:S(2)}) collective-permute-start(f16[1,1,1,576,384]{4,3,2,1,0:T(8,128)(2,1)} %get-tuple-element.476), channel_id=1, source_target_pairs={{0,8},{2,10},{4,12},{6,14},{8,0},{10,2},{12,4},{14,6},{16,24},{18,... | collective-permute-start | bytes 1327112 | tf_op jit(solution)/shard_map/ppermute | solution.py:530
  779.8 16.8 %collective-permute-start.83 = (f32[1]{0:T(128)}, f32[1]{0:T(128)}, u32[]{:S(2)}, u32[]{:S(2)}) collective-permute-start(f32[1]{0:T(128)} %add.769), channel_id=1, source_target_pairs={{0,4},{2,6},{4,0},{6,2},{8,12},{10,14},{12,8},{14,10},{16,20},{18,... | collective-permute-start | bytes 20 | tf_op jit(solution)/shard_map/ppermute | solution.py:530
  781.5 15.7 %collective-permute-start.84 = (f32[1]{0:T(128)}, f32[1]{0:T(128)}, u32[]{:S(2)}, u32[]{:S(2)}) collective-permute-start(f32[1]{0:T(128)} %add.769), channel_id=1, source_target_pairs={{0,8},{2,10},{4,12},{6,14},{8,0},{10,2},{12,4},{14,6},{16,24},{18,... | collective-permute-start | bytes 20 | tf_op jit(solution)/shard_map/ppermute | solution.py:530
  789.5 22.8 %collective-permute-start.86 = (f16[1,2,1,96,1536]{4,3,2,1,0:T(8,128)(2,1)}, f16[1,2,1,96,1536]{4,3,2,1,0:T(8,128)(2,1)}, u32[]{:S(2)}, u32[]{:S(2)}) collective-permute-start(f16[1,2,1,96,1536]{4,3,2,1,0:T(8,128)(2,1)} %maximum_select_fusion.26), channel_id=1, source_target_pairs={{0,8},{2,10},{4,12},{6,14},{8,0},{10,2},{12,4},{14,6},{16,24},{18,... | collective-permute-start | bytes 1769480 | tf_op jit(solution)/shard_map/ppermute | solution.py:530
  793.8 20.6 %collective-permute-start.87 = (f16[1,2,1,96,1536]{4,3,2,1,0:T(8,128)(2,1)}, f16[1,2,1,96,1536]{4,3,2,1,0:T(8,128)(2,1)}, u32[]{:S(2)}, u32[]{:S(2)}) collective-permute-start(f16[1,2,1,96,1536]{4,3,2,1,0:T(8,128)(2,1)} %maximum_select_fusion.25), channel_id=1, source_target_pairs={{0,8},{2,10},{4,12},{6,14},{8,0},{10,2},{12,4},{14,6},{16,24},{18,... | collective-permute-start | bytes 1769480 | tf_op jit(solution)/shard_map/ppermute | solution.py:530
  796.6 18.1 %collective-permute-start.88 = (f16[1,1,2,576,384]{4,3,2,1,0:T(8,128)(2,1)}, f16[1,1,2,576,384]{4,3,2,1,0:T(8,128)(2,1)}, u32[]{:S(2)}, u32[]{:S(2)}) collective-permute-start(f16[1,1,2,576,384]{4,3,2,1,0:T(8,128)(2,1)} %maximum_select_fusion.20), channel_id=1, source_target_pairs={{0,4},{2,6},{4,0},{6,2},{8,12},{10,14},{12,8},{14,10},{16,20},{18,... | collective-permute-start | bytes 2654216 | tf_op jit(solution)/shard_map/ppermute | solution.py:530
  817.1 14.9 %collective-permute-start.89 = (f16[384,1536]{1,0:T(8,128)(2,1)S(1)}, f16[384,1536]{1,0:T(8,128)(2,1)S(1)}, u32[]{:S(2)}, u32[]{:S(2)}) collective-permute-start(f16[384,1536]{1,0:T(8,128)(2,1)S(1)} %bitcast.148), channel_id=1, source_target_pairs={{0,2},{2,0},{4,6},{6,4},{8,10},{10,8},{12,14},{14,12},{16,18},{18,... | collective-permute-start | bytes 3538952 | tf_op jit(solution)/shard_map/ppermute | solution.py:530
  829.1 34.2 %collective-permute-start.91 = (f16[2304,384]{1,0:T(8,128)(2,1)}, f16[2304,384]{1,0:T(8,128)(2,1)}, u32[]{:S(2)}, u32[]{:S(2)}) collective-permute-start(f16[2304,384]{1,0:T(8,128)(2,1)} %bitcast.92), channel_id=1, source_target_pairs={{0,2},{2,0},{4,6},{6,4},{8,10},{10,8},{12,14},{14,12},{16,18},{18,... | collective-permute-start | bytes 5308424 | tf_op jit(solution)/shard_map/ppermute | solution.py:530
  (108 other events, 806.7 us)

commit v3 on v2

--- a/solution.py
+++ b/solution.py
@@ -677,6 +677,12 @@
     return value
 
 
+def over_and_back(links, parts, turns):
+    blocks = yield from links.reduce(parts, (None,) * len(parts), turns, True)
+    rows = yield from links.spread(blocks, turns, True)
+    return blocks, rows
+
+
 def paired(hops):
     return [tuple(hops[:2])] + hops[2:] if len(hops) > 1 else hops
 
@@ -786,7 +792,7 @@
         u_out, u_up, u_down, w_head, vec, BLOCK,
     )
     view = functools.partial(split_view, shard=shard, ways=links.ways)
-    dec_flight = Steps(links.reduce([view(grad_row_part), view(grad_dec_fc2)], (None, None), (0, 1), True))
+    dec_flight = Steps(over_and_back(links, [view(grad_row_part), view(grad_dec_fc2)], (0, 1)))
     input_grads, before = [], [jnp.zeros((DD, 3 * DD), jnp.float32), jnp.zeros((8, DD), jnp.float32)]
     parts = [[], []]
     for clip in range(seq_count):
@@ -799,14 +805,10 @@
         input_grads.append(back[0])
         before = back[1:]
     grad_qkv, one_grads = before
-    dec_sums = complete(dec_flight)[0]
-
     proj_grad = jnp.concatenate([grad[:, hidden_count:] for grad in input_grads], axis=0)
     proj_grad = jnp.pad(proj_grad, ((0, 0), (0, seen_rows - seen_count), (0, 0))).reshape(-1, DD)
     grad_proj = product_tn(latent, proj_grad)
-    late = Steps(links.reduce([view(grad_qkv), view(grad_proj)], (None, None), (0, 1), True))
-    proj_grad = arrive([late], proj_grad)
-    dec_spread = Steps(links.spread(dec_sums, (0, 1), True))
+    late = Steps(over_and_back(links, [view(grad_qkv), view(grad_proj)], (0, 1)))
     grad_down, grad_up, grad_wide, grad_in, enc_sums, up_sums, right_most = enc_bwd(
         at, proj_grad, enc_h, enc_qkv, enc_mid, enc_inner, encoded, vec, *sources, seq_count, seen_count, shard
     )
@@ -816,9 +818,6 @@
     )
 
     bit = bit_of(*core)
-    grad_up, grad_wide, grad_in, grad_down, right_most, grad_vectors = arrive(
-        [late, dec_spread], (grad_up, grad_wide, grad_in, grad_down, right_most, grad_vectors)
-    )
     shape_right = lambda b: (
         half_of(grad_up, b)[None],
         jnp.concatenate([half_of(grad_wide[:, : 3 * D], b), half_of(grad_wide[:, 3 * D :], b)], axis=1)[None],
@@ -837,7 +836,7 @@
     far_rights = right_swap.result
     wide_cols, tall_rows = 2 * D, PATCH + FF
     zero = lambda i, j: (0, 0, i)
-    hops = [vector_flight, late, dec_spread]
+    hops = [vector_flight, late, dec_flight]
     sum_up = pair_product(
         (normed_two[None], far_lefts[2][None]), (rights[0], far_rights[0]), D, wide_cols, D, D // 2,
         zero, lambda i, j: (0, 0, j), "grad_up",
@@ -853,17 +852,15 @@
         zero, lambda i, j: (jnp.minimum(i // 2, 1), 0, j), "grad_tall",
     )
     sum_up, sum_wide, sum_tall = arrive(hops, (sum_up, sum_wide, sum_tall))
-    totals = complete(*hops)[0]
+    totals = complete(vector_flight)[0]
     vector_sum, loss_sum = totals[0, :size], totals[0, size]
     bounds = totals[0, size + 1 : size + 4] * (2.0 * rep * shard)
     scales = list(jnp.exp2(jnp.floor(15.0 - jnp.log2(jnp.maximum(bounds, 1e-30)))))
     slim = functools.partial(split_view, shard=shard, ways=links.ways - 1)
     enc_flight = Steps(links.reduce([slim(sum_up), slim(sum_wide), slim(sum_tall)], scales, (0, 1, 2), False))
-    late_sums = late.result
-    late_spread = Steps(links.spread(late_sums, (0, 1), True))
     while enc_flight.result is None:
-        arrive([enc_flight, late_spread])
-    complete(late_spread)
+        arrive([enc_flight, late, dec_flight])
+    (late_sums, late_rows), (dec_sums, dec_rows_all) = complete(late, dec_flight)
     enc_parts_sum = enc_flight.result
 
     lowered = [(part * scale).astype(jnp.float16) for part, scale in zip(enc_parts_sum, scales)]
@@ -882,34 +879,38 @@
 
     flat_piece = lambda piece: piece.reshape(-1, piece.shape[-1])
     dec_rows_sum, dec_fc2_sum, dec_qkv_sum, proj_sum = [
-        flat_piece(piece) for piece in dec_spread.result + late_spread.result
+        flat_piece(piece) for piece in dec_rows_all + late_rows
     ]
     own_vectors = lax.dynamic_slice_in_dim(vector_sum, me * masters[4].shape[0], masters[4].shape[0])
+    def update(index, gradient):
+        updated = adam_update(masters[index], firsts[index], seconds[index], gradient * factor)
+        return (*updated, updated[0].astype(jnp.bfloat16))
+
     updates = {}
     for index, gradient in (
         (2, jnp.concatenate([dec_qkv_sum, dec_rows_sum], axis=1)), (3, dec_fc2_sum), (4, own_vectors),
     ):
-        updates[index] = adam_update(masters[index], firsts[index], seconds[index], gradient * factor)
+        updates[index] = update(index, gradient)
     updates = arrive([enc_spread], updates)
-    halves = [flat_piece(piece) for piece in complete(enc_spread)[0]]
-    other = [links.swap(half, core) for half in halves]
-
-    def sided(mine, yours):
-        return jnp.where(bit == 0, jnp.concatenate([mine, yours], 1), jnp.concatenate([yours, mine], 1))
-
-    wide_parts = []
-    for at, (lo, hi) in enumerate(((0, 3 * D // 2), (3 * D // 2, 2 * D))):
-        wide_parts.append(sided(halves[1][:, lo:hi], other[1][:, lo:hi]).astype(jnp.float32) * (1.0 / scales[1]))
-    grads = [
-        jnp.concatenate(
-            wide_parts + [sided(halves[0], other[0]).astype(jnp.float32) * (1.0 / scales[0]), proj_sum], axis=1
-        ),
-        sided(halves[2], other[2]).astype(jnp.float32) * (1.0 / scales[2]),
-    ]
-    for index in (0, 1):
-        updates[index] = adam_update(masters[index], firsts[index], seconds[index], grads[index] * factor)
-    new_w, new_m, new_v = [[updates[index][kind] for index in range(5)] for kind in range(3)]
-    return (loss, grad_norm, *new_w, *new_m, *new_v, *[w.astype(jnp.bfloat16) for w in new_w])
+    near16 = [flat_piece(piece) for piece in complete(enc_spread)[0]]
+    tall_swap = Steps(one_hop(links, near16[2:], core))
+    wide_swap = Steps(one_hop(links, near16[:2], core))
+
+    def sided(mine, yours, k):
+        both = jnp.where(bit == 0, jnp.concatenate([mine, yours], 1), jnp.concatenate([yours, mine], 1))
+        return both.astype(jnp.float32) * (1.0 / scales[k])
+
+    near16 = arrive([tall_swap], near16)
+    updates[1] = update(1, sided(near16[2], tall_swap.result[0], 2))
+    near16, updates[1] = arrive([wide_swap], (near16, updates[1]))
+    far_up, far_wide = wide_swap.result
+    cut = 3 * D // 2
+    updates[0] = update(0, jnp.concatenate([
+        sided(near16[1][:, :cut], far_wide[:, :cut], 1), sided(near16[1][:, cut:], far_wide[:, cut:], 1),
+        sided(near16[0], far_up, 0), proj_sum,
+    ], axis=1))
+    new_w, new_m, new_v, lows = [[updates[index][kind] for index in range(5)] for kind in range(4)]
+    return (loss, grad_norm, *new_w, *new_m, *new_v, *lows)
 
 
 def solution(mesh):

time: 894 us -> 879 us (0.983)
  other arithmetic: 206 us -> 189 us
    sub x3 -> x0, other arithmetic: 10.9 us -> none  [adam_update(): master - learn_rate * (stepped + decay_rate * master)]
  transfers between devices with their start and end apart: 92 -> 92, of which waited for: 20 -> 18; matrix products, arithmetic and copies ran while one was open for 22% -> 19% of each run, Pallas kernels for 29% -> 30%
where the time goes in v3:
time: 879 us; the launch traced here: 871 us
  Pallas kernels  383 us (44%)
  other arithmetic  189 us (22%)
  waiting for transfers between devices  125 us (14%)
  starting transfers between devices  96.3 us (11%)
  local copies, waits for them, and re-layouts  56.1 us (6%)
  between operations  22.2 us (3%)
    ppermute x87, waiting for transfers between devices, swap(): return lax.ppermute(value, name, [(i, i ^ hop) for i in range(size)])  125 us
    pallas_call x6, Pallas kernels, attn_bwd(): pl.pallas_call(functools.partial(bwd_body, 64 ** (-0.5), nb, 0), grid=(1,...  116 us
    ppermute x87, starting transfers between devices, swap(): return lax.ppermute(value, name, [(i, i ^ hop) for i in range(size)])  89.7 us
    pallas_call x1, Pallas kernels, dec_post(): pl.pallas_call(functools.partial(post_body, nb, R, keys), grid=(clips, nb...  64.1 us
    pallas_call x1, Pallas kernels, attn_fwd(): pl.pallas_call(body, grid=(clips, pairs, nb), in_specs=[pl.BlockSpec((1,...  63.8 us
    convert_element_type x5, other arithmetic, update(): return (*updated, updated[0].astype(jnp.bfloat16))  54.1 us
    pallas_call x4, Pallas kernels, pick_rows(): pl.pallas_call(pick_body, grid=(m // R,), in_specs=[pl.BlockSpec((1, R, 1...  33.4 us
    select_n x29, other arithmetic, join(): jnp.where(bit == 0, jnp.concatenate([mine, other], axis=dim), jnp.concate...  33.4 us
  transfers between devices with their start and end apart: 92, of which 18 were waited for; matrix products, arithmetic and copies ran while one was open for 19% of the time, Pallas kernels for 30%

profile of v3, /device:TPU:0, one launch (start us, length us, event | category | flops | bytes accessed | tf_op | source)
XLA Modules:
  0.0 870.9 jit_solution(3851538780653611690)
XLA Ops:
  5.0 2.6 collective-permute-start.4
  9.7 2.2 dynamic-slice_convert_fusion
  18.7 4.3 pick_seen_0.1.refs_0_
  23.1 4.3 pick_seen_1.1
  27.4 3.5 negate_select_fusion.4
  32.4 3.5 convert_element_type.197
  35.9 5.3 convert_element_type.196.refs_3_
  41.2 2.8 convert_element_type.195.refs_0_
  45.7 2.9 collective-permute-start.1
  56.6 12.5 %pick_hidden_0.1.refs_0_ = bf16[2,1440,1536]{2,1,0:T(8,128)(2,1)} custom-call(s32[2,1440,1]{2,1,0:T(8,128)} %copy.80.idx_ref, bf16[2,1568,1536]{2,1,0:T(8,128)(2,1)} %x_ref.7), custom_call_target="tpu_custom_call" | custom-call | flops 11314285568 | tf_op jit(solution)/shard_map/pick_hidden_0/pallas_call | solution.py:299
  72.8 2.2 maximum_select_fusion.16
  78.5 12.2 %pick_hidden_1.1.t_ref = bf16[2,1440,1536]{2,1,0:T(8,128)(2,1)} custom-call(s32[2,1440,1]{2,1,0:T(8,128)} %copy.81.idx_ref, bf16[2,1568,1536]{2,1,0:T(8,128)(2,1)} %x_ref.7, bf16[2,1440,1536]{2,1,0:T(8,128)(2,1)} %pick_hidden_0.1.refs_0_), custom_call_target="tpu_custom_call", output_to_operand_aliasing={{}: (2, {})} | custom-call | flops 11314285568 | tf_op jit(solution)/shard_map/pick_hidden_1/pallas_call | solution.py:299
  93.3 10.1 %collective-permute-done.7 = bf16[1,1,2,1,48,6528]{5,4,3,2,1,0:T(8,128)(2,1)S(1)} collective-permute-done((bf16[1,1,2,1,48,6528]{5,4,3,2,1,0:T(8,128)(2,1)}, bf16[1,1,2,1,48,6528]{5,4,3,2,1,0:T(8,128)(2,1)S(1)}, u32[]{:S(2)}, u32[]{:S(2)}) %collective-permute-start.7) | collective-permute-done | bytes 1253408 | tf_op jit(solution)/shard_map/ppermute | solution.py:530
  109.5 7.5 fusion.7
  117.9 2.5 pad_maximum_fusion
  124.5 20.5 %enc_forward.1 = (f32[320,768]{1,0:T(8,128)}, bf16[320,2304]{1,0:T(8,128)(2,1)}, f32[320,768]{1,0:T(8,128)}, f32[320,3072]{1,0:T(8,128)}, f32[320,768]{1,0:T(8,1...) custom-call(s32[3]{0:T(128)} %pad_add_fusion.at_ref, ...), custom_call_target="tpu_custom_call" | custom-call | flops 20899999744 | tf_op jit(solution)/shard_map/enc_forward/pallas_call | solution.py:404
  149.1 2.3 collective-permute-start.20
  158.7 9.4 %dec_qkv.1.q_ref.k_ref.v_ref = bf16[2,1568,1152]{2,1,0:T(8,128)(2,1)} custom-call(f32[2,1568,384]{2,1,0:T(8,128)} %scatter-add.4.h_ref, bf16[384,1152]{1,0:T(8,128)(2,1)} %slice.204.w_ref, f32[1,14592]{1,0:T(1,128)} %bitcast.185), custom_call_target="tpu_custom_call" | custom-call | flops 9900000256 | tf_op jit(solution)/shard_map/dec_qkv/pallas_call | solution.py:249
  168.8 3.9 collective-permute-start.21
  172.7 63.8 %dec_attend_forward.1 = (bf16[2,1440,384]{2,1,0:T(8,128)(2,1)}, f32[6,2,2,720]{3,2,1,0:T(2,128)}) custom-call(bf16[2,1568,1152]{2,1,0:T(8,128)(2,1)} %dec_qkv.1.q_ref.k_ref.v_ref, bf16[2,1568,1152]{2,1,0:T(8,128)(2,1)} %dec_qkv.1.q_ref.k_ref.v_ref, bf16[2,1568,1152]{2,1,0:T(8,128)(2,1)} %dec_qkv.1.q_ref.k_ref.v_ref), custom_call_target="tpu_custom_call" | custom-call | flops 71499997184 | tf_op jit(solution)/shard_map/dec_attend_forward/pallas_call | solution.py:67
  241.4 64.1 %dec_post.1 = (f32[2,1568,384]{2,1,0:T(8,128)}, bf16[2,1440,384]{2,1,0:T(8,128)(2,1)}, f32[384,3456]{1,0:T(8,128)}, f32[1536,384]{1,0:T(8,128)}, f32[8,384]{1,0:...) custom-call(s32[2]{0:T(128)} %cnt_ref.1, f32[1]{0:T(128)} %bitcast.32.inv_ref, f32[2,1568,384]{2,1,0:T(8,128)} %scatter-add.4.h_ref, ...), custom_call_target="tpu_custom_call" | custom-call | flops 73699999744 | tf_op jit(solution)/shard_map/dec_post/pallas_call | solution.py:233
  308.7 2.4 constant_dynamic-slice_fusion.18
  313.7 19.1 %dec_attend_backward_0_0.1 = (bf16[1,1568,128]{2,1,0:T(8,128)(2,1)}, bf16[1,1568,128]{2,1,0:T(8,128)(2,1)}, bf16[1,1568,128]{2,1,0:T(8,128)(2,1)}) custom-call(bf16[2,1568,1152]{2,1,0:T(8,128)(2,1)} %dec_qkv.1.q_ref.k_ref.v_ref, bf16[2,1568,1152]{2,1,0:T(8,128)(2,1)} %dec_qkv.1.q_ref.k_ref.v_ref, bf16[2,1568,1152]{2,1,0:T(8,128)(2,1)} %dec_qkv.1.q_ref.k_ref.v_ref, ...), custom_call_target="tpu_custom_call" | custom-call | flops 18699999232 | tf_op jit(solution)/shard_map/dec_attend_backward_0_0/pallas_call | solution.py:132
  334.5 2.8 dynamic-slice_add_fusion
  341.9 19.3 %dec_attend_backward_0_1.1 = (bf16[1,1568,128]{2,1,0:T(8,128)(2,1)}, bf16[1,1568,128]{2,1,0:T(8,128)(2,1)}, bf16[1,1568,128]{2,1,0:T(8,128)(2,1)}) custom-call(bf16[2,1568,1152]{2,1,0:T(8,128)(2,1)} %dec_qkv.1.q_ref.k_ref.v_ref, bf16[2,1568,1152]{2,1,0:T(8,128)(2,1)} %dec_qkv.1.q_ref.k_ref.v_ref, bf16[2,1568,1152]{2,1,0:T(8,128)(2,1)} %dec_qkv.1.q_ref.k_ref.v_ref, ...), custom_call_target="tpu_custom_call" | custom-call | flops 18699999232 | tf_op jit(solution)/shard_map/dec_attend_backward_0_1/pallas_call | solution.py:132
  361.2 10.4 %collective-permute-done.27 = f32[2,1,1,2,24,3456]{5,4,3,2,1,0:T(8,128)} collective-permute-done((f32[2,1,1,2,24,3456]{5,4,3,2,1,0:T(8,128)}, f32[2,1,1,2,24,3456]{5,4,3,2,1,0:T(8,128)}, u32[]{:S(2)}, u32[]{:S(2)}) %collective-permute-start.27) | collective-permute-done | bytes 1327136 | tf_op jit(solution)/shard_map/ppermute | solution.py:530
  377.1 19.4 %dec_attend_backward_0_2.1 = (bf16[1,1568,128]{2,1,0:T(8,128)(2,1)}, bf16[1,1568,128]{2,1,0:T(8,128)(2,1)}, bf16[1,1568,128]{2,1,0:T(8,128)(2,1)}) custom-call(bf16[2,1568,1152]{2,1,0:T(8,128)(2,1)} %dec_qkv.1.q_ref.k_ref.v_ref, bf16[2,1568,1152]{2,1,0:T(8,128)(2,1)} %dec_qkv.1.q_ref.k_ref.v_ref, bf16[2,1568,1152]{2,1,0:T(8,128)(2,1)} %dec_qkv.1.q_ref.k_ref.v_ref, ...), custom_call_target="tpu_custom_call" | custom-call | flops 18699999232 | tf_op jit(solution)/shard_map/dec_attend_backward_0_2/pallas_call | solution.py:132
  398.4 11.8 %dec_qkv_back_0.1 = (bf16[1,1568,384]{2,1,0:T(8,128)(2,1)}, f32[384,1152]{1,0:T(8,128)}, f32[8,384]{1,0:T(8,128)}) custom-call(f32[2,1568,384]{2,1,0:T(8,128)} %scatter-add.4.h_ref, f32[2,1568,384]{2,1,0:T(8,128)} %get-tuple-element.293.dmid_ref, bf16[384,1152]{1,0:T(8,128)(2,1)} %slice.204.w_ref, f32[1,14592]{1,0:T(1,128)} %bitcast.187, ...), custom_call_target="tpu_custom_call" | custom-call | flops 11000000512 | tf_op jit(solution)/shard_map/dec_qkv_back_0/pallas_call | solution.py:284
  413.6 19.2 %dec_attend_backward_1_0.1 = (bf16[1,1568,128]{2,1,0:T(8,128)(2,1)}, bf16[1,1568,128]{2,1,0:T(8,128)(2,1)}, bf16[1,1568,128]{2,1,0:T(8,128)(2,1)}) custom-call(bf16[2,1568,1152]{2,1,0:T(8,128)(2,1)} %dec_qkv.1.q_ref.k_ref.v_ref, bf16[2,1568,1152]{2,1,0:T(8,128)(2,1)} %dec_qkv.1.q_ref.k_ref.v_ref, bf16[2,1568,1152]{2,1,0:T(8,128)(2,1)} %dec_qkv.1.q_ref.k_ref.v_ref, ...), custom_call_target="tpu_custom_call" | custom-call | flops 18699999232 | tf_op jit(solution)/shard_map/dec_attend_backward_1_0/pallas_call | solution.py:132
  433.3 2.6 collective-permute-start.33
  435.9 19.3 %dec_attend_backward_1_1.1 = (bf16[1,1568,128]{2,1,0:T(8,128)(2,1)}, bf16[1,1568,128]{2,1,0:T(8,128)(2,1)}, bf16[1,1568,128]{2,1,0:T(8,128)(2,1)}) custom-call(bf16[2,1568,1152]{2,1,0:T(8,128)(2,1)} %dec_qkv.1.q_ref.k_ref.v_ref, bf16[2,1568,1152]{2,1,0:T(8,128)(2,1)} %dec_qkv.1.q_ref.k_ref.v_ref, bf16[2,1568,1152]{2,1,0:T(8,128)(2,1)} %dec_qkv.1.q_ref.k_ref.v_ref, ...), custom_call_target="tpu_custom_call" | custom-call | flops 18699999232 | tf_op jit(solution)/shard_map/dec_attend_backward_1_1/pallas_call | solution.py:132
  455.2 19.6 %dec_attend_backward_1_2.1 = (bf16[1,1568,128]{2,1,0:T(8,128)(2,1)}, bf16[1,1568,128]{2,1,0:T(8,128)(2,1)}, bf16[1,1568,128]{2,1,0:T(8,128)(2,1)}) custom-call(bf16[2,1568,1152]{2,1,0:T(8,128)(2,1)} %dec_qkv.1.q_ref.k_ref.v_ref, bf16[2,1568,1152]{2,1,0:T(8,128)(2,1)} %dec_qkv.1.q_ref.k_ref.v_ref, bf16[2,1568,1152]{2,1,0:T(8,128)(2,1)} %dec_qkv.1.q_ref.k_ref.v_ref, ...), custom_call_target="tpu_custom_call" | custom-call | flops 18699999232 | tf_op jit(solution)/shard_map/dec_attend_backward_1_2/pallas_call | solution.py:132
  474.8 11.8 %dec_qkv_back_1.1 = (bf16[1,1568,384]{2,1,0:T(8,128)(2,1)}, f32[384,1152]{1,0:T(8,128)}, f32[8,384]{1,0:T(8,128)}) custom-call(f32[2,1568,384]{2,1,0:T(8,128)} %scatter-add.4.h_ref, f32[2,1568,384]{2,1,0:T(8,128)} %get-tuple-element.293.dmid_ref, bf16[384,1152]{1,0:T(8,128)(2,1)} %slice.204.w_ref, f32[1,14592]{1,0:T(1,128)} %bitcast.188, ...), custom_call_target="tpu_custom_call" | custom-call | flops 11000000512 | tf_op jit(solution)/shard_map/dec_qkv_back_1/pallas_call | solution.py:284
  488.3 28.1 %enc_backward.1 = (bf16[320,768]{1,0:T(8,128)(2,1)}, bf16[320,3072]{1,0:T(8,128)(2,1)}, bf16[320,3072]{1,0:T(8,128)(2,1)}, bf16[320,768]{1,0:T(8,128)(2,1)}, f32...) custom-call(s32[3]{0:T(128)} %pad_add_fusion.at_ref, bf16[320,384]{1,0:T(8,128)(2,1)} %bitcast.173, ...), custom_call_target="tpu_custom_call" | custom-call | flops 29699999744 | tf_op jit(solution)/shard_map/enc_backward/pallas_call | solution.py:471
  528.2 2.8 concatenate.1099
  550.2 7.0 grad_up.1
  557.3 8.3 collective-permute-done.44
  574.4 7.1 grad_wide.1
  581.5 4.5 collective-permute-done.47
  593.6 10.0 %grad_tall.1 = f32[4608,384]{1,0:T(8,128)} custom-call(bf16[1,320,4608]{2,1,0:T(8,128)(2,1)} %bitcast.191, bf16[1,320,4608]{2,1,0:T(8,128)(2,1)} %bitcast.67.bl_ref, bf16[2,320,384]{2,1,0:T(8,128)(2,1)} %pad_maximum_fusion.1.ar_ref, bf16[2,320,384]{2,1,0:T(8,128)(2,1)} %copy-done.77), custom_call_target="tpu_custom_call" | custom-call | flops 8800000000 | tf_op jit(solution)/shard_map/grad_tall/pallas_call | solution.py:486
  604.5 4.8 multiply_convert_fusion
  610.8 3.6 multiply_convert_fusion.2
  623.6 18.0 %collective-permute-done.60 = f32[1,1,1,1,48,384]{5,4,3,2,1,0:T(8,128)S(1)} collective-permute-done((f32[1,1,1,1,48,384]{5,4,3,2,1,0:T(8,128)}, f32[1,1,1,1,48,384]{5,4,3,2,1,0:T(8,128)S(1)}, u32[]{:S(2)}, u32[]{:S(2)}) %collective-permute-start.60) | collective-permute-done | bytes 73760 | tf_op jit(solution)/shard_map/ppermute | solution.py:530
  641.6 8.6 collective-permute-done.59
  650.2 2.4 multiply_add_fusion.5
  655.2 2.4 multiply_add_fusion.4
  663.5 2.7 collective-permute-start.65
  666.2 9.8 %collective-permute-done.65 = f32[1,1,1,1,48,384]{5,4,3,2,1,0:T(8,128)S(1)} collective-permute-done((f32[1,1,1,1,48,384]{5,4,3,2,1,0:T(8,128)S(1)}, f32[1,1,1,1,48,384]{5,4,3,2,1,0:T(8,128)S(1)}, u32[]{:S(2)}, u32[]{:S(2)}) %collective-permute-start.65) | collective-permute-done | bytes 73760 | tf_op jit(solution)/shard_map/ppermute | solution.py:530
  688.2 6.1 collective-permute-done.70
  709.7 6.6 collective-permute-done.74
  716.3 21.1 %collective-permute-done.72 = f16[1,1,1,96,1536]{4,3,2,1,0:T(8,128)(2,1)S(1)} collective-permute-done((f16[1,1,1,96,1536]{4,3,2,1,0:T(8,128)(2,1)S(1)}, f16[1,1,1,96,1536]{4,3,2,1,0:T(8,128)(2,1)S(1)}, u32[]{:S(2)}, u32[]{:S(2)}) %collective-permute-start.72) | collective-permute-done | bytes 294944 | tf_op jit(solution)/shard_map/ppermute | solution.py:530
  737.4 5.2 collective-permute-done.71
  756.8 2.5 collective-permute-start.77
  765.3 4.0 collective-permute-done.78
  769.3 2.8 collective-permute-done.80
  772.8 2.8 collective-permute-start.83
  775.6 3.0 collective-permute-start.82
  791.0 8.3 fusion.87
  801.6 2.6 fusion.84
  804.1 4.9 collective-permute-done.86
  809.1 2.8 maximum_select_fusion.7
  820.8 18.4 %fusion.80 = (bf16[2304,768]{1,0:T(8,128)(2,1)}, f32[2304,768]{1,0:T(8,128)}, f32[2304,768]{1,0:T(8,128)}, f32[2304,768]{1,0:T(8,128)}) fusion(f32[2304,768]{1,0:T(8,128)} %param.26, f32[]{:T(128)S(6)} %min.3, f32[]{:T(128)S(6)} %div.277, f16[2304,384]{1,0:T(8,128)(2,1)S(1)} %bitcast.138, f16[2304,384]{1,0:T(8,128)(2,1)S(1)} %collective-permute-done.89, ...), kind=kLoop, calls=%fused_computation.314 | loop fusion | flops 38928384 | bytes 49545224 | tf_op jit(solution)/shard_map/convert_element_type | solution.py:887
  841.6 2.7 convert_multiply_fusion
  844.3 24.1 %fusion.78 = (bf16[384,6528]{1,0:T(8,128)(2,1)}, f32[384,6528]{1,0:T(8,128)}, f32[384,6528]{1,0:T(8,128)}, f32[384,6528]{1,0:T(8,128)}) fusion(f32[384,6528]{1,0:T(8,128)} %param.25, f32[]{:T(128)S(6)} %min.3, f32[384,384]{1,0:T(8,128)} %bitcast.165, f32[384,3072]{1,0:T(8,128)} %convert_multiply_fusion, f32[384,768]{1,0:T(8,128)} %convert_multiply_fusion.2, ...), kind=kLoop, calls=%fused_computation.313 | loop fusion | flops 50135040 | bytes 75202560 | tf_op jit(solution)/shard_map/convert_element_type | solution.py:887
  (494 shorter events, 210.5 us)
Async XLA Ops:
  2.7 42.3 %collective-permute-start = (f32[1]{0:T(128)}, f32[1]{0:T(128)}, u32[]{:S(2)}, u32[]{:S(2)}) collective-permute-start(f32[1]{0:T(128)} %bitcast.4), channel_id=1, source_target_pairs={{0,2},{2,0},{4,6},{6,4},{8,10},{10,8},{12,14},{14,12},{16,18},{18,... | collective-permute-start | bytes 20 | tf_op jit(solution)/shard_map/ppermute | solution.py:530
  5.0 44.4 %collective-permute-start.4 = (bf16[1,7296]{1,0:T(2,128)(2,1)S(1)}, bf16[1,7296]{1,0:T(2,128)(2,1)}, u32[]{:S(2)}, u32[]{:S(2)}) collective-permute-start(bf16[1,7296]{1,0:T(2,128)(2,1)S(1)} %reshape.2737), channel_id=1, source_target_pairs={{0,1},{1,0},{2,3},{3,2},{4,5},{5,4},{6,7},{7,6},{8,9},{9,8},{10,11... | collective-permute-start | bytes 43784 | tf_op jit(solution)/shard_map/ppermute | solution.py:694
  9.6 39.9 %collective-permute-start.3 = (bf16[1,1,1,1,288,768]{5,4,3,2,1,0:T(8,128)(2,1)}, bf16[1,1,1,1,288,768]{5,4,3,2,1,0:T(8,128)(2,1)}, u32[]{:S(2)}, u32[]{:S(2)}) collective-permute-start(bf16[1,1,1,1,288,768]{5,4,3,2,1,0:T(8,128)(2,1)} %dynamic-slice_convert_fusion.1), channel_id=1, source_target_pairs={{0,1},{1,0},{2,3},{3,2},{4,5},{5,4},{6,7},{7,6},{8,9},{9,8},{10,11... | collective-permute-start | bytes 1327112 | tf_op jit(solution)/shard_map/ppermute | solution.py:694
  11.9 37.6 %collective-permute-start.2 = (bf16[1,1,1,1,48,6528]{5,4,3,2,1,0:T(8,128)(2,1)}, bf16[1,1,1,1,48,6528]{5,4,3,2,1,0:T(8,128)(2,1)S(1)}, u32[]{:S(2)}, u32[]{:S(2)}) collective-permute-start(bf16[1,1,1,1,48,6528]{5,4,3,2,1,0:T(8,128)(2,1)} %dynamic-slice_convert_fusion), channel_id=1, source_target_pairs={{0,1},{1,0},{2,3},{3,2},{4,5},{5,4},{6,7},{7,6},{8,9},{9,8},{10,11... | collective-permute-start | bytes 1880072 | tf_op jit(solution)/shard_map/ppermute | solution.py:694
  50.1 96.0 %collective-permute-start.15 = (f32[1]{0:T(128)}, f32[1]{0:T(128)}, u32[]{:S(2)}, u32[]{:S(2)}) collective-permute-start(f32[1]{0:T(128)} %add.707), channel_id=1, source_target_pairs={{0,1},{1,0},{2,3},{3,2},{4,5},{5,4},{6,7},{7,6},{8,9},{9,8},{10,11... | collective-permute-start | bytes 20 | tf_op jit(solution)/shard_map/ppermute | solution.py:530
  51.6 19.2 %collective-permute-start.6 = (bf16[1,1,1,1,288,768]{5,4,3,2,1,0:T(8,128)(2,1)}, bf16[1,1,1,1,288,768]{5,4,3,2,1,0:T(8,128)(2,1)S(1)}, u32[]{:S(2)}, u32[]{:S(2)}) collective-permute-start(bf16[1,1,1,1,288,768]{5,4,3,2,1,0:T(8,128)(2,1)} %collective-permute-done.3), channel_id=1, source_target_pairs={{0,8},{2,10},{4,12},{6,14},{8,0},{10,2},{12,4},{14,6},{16,24},{18,... | collective-permute-start | bytes 1327112 | tf_op jit(solution)/shard_map/ppermute | solution.py:530
  53.6 17.3 %collective-permute-start.5 = (bf16[1,1,1,1,48,6528]{5,4,3,2,1,0:T(8,128)(2,1)S(1)}, bf16[1,1,1,1,48,6528]{5,4,3,2,1,0:T(8,128)(2,1)S(1)}, u32[]{:S(2)}, u32[]{:S(2)}) collective-permute-start(bf16[1,1,1,1,48,6528]{5,4,3,2,1,0:T(8,128)(2,1)S(1)} %collective-permute-done.2), channel_id=1, source_target_pairs={{0,4},{2,6},{4,0},{6,2},{8,12},{10,14},{12,8},{14,10},{16,20},{18,... | collective-permute-start | bytes 1880072 | tf_op jit(solution)/shard_map/ppermute | solution.py:530
  70.8 21.4 %collective-permute-start.10 = (bf16[1,1,1,1,96,384]{5,4,3,2,1,0:T(8,128)(2,1)S(1)}, bf16[1,1,1,1,96,384]{5,4,3,2,1,0:T(8,128)(2,1)}, u32[]{:S(2)}, u32[]{:S(2)}) collective-permute-start(bf16[1,1,1,1,96,384]{5,4,3,2,1,0:T(8,128)(2,1)S(1)} %dynamic-slice_convert_fusion.3), channel_id=1, source_target_pairs={{0,1},{1,0},{2,3},{3,2},{4,5},{5,4},{6,7},{7,6},{8,9},{9,8},{10,11... | collective-permute-start | bytes 221192 | tf_op jit(solution)/shard_map/ppermute | solution.py:694
  72.3 19.9 %collective-permute-start.9 = (bf16[1,1,1,1,24,4608]{5,4,3,2,1,0:T(8,128)(2,1)S(1)}, bf16[1,1,1,1,24,4608]{5,4,3,2,1,0:T(8,128)(2,1)}, u32[]{:S(2)}, u32[]{:S(2)}) collective-permute-start(bf16[1,1,1,1,24,4608]{5,4,3,2,1,0:T(8,128)(2,1)S(1)} %copy-done.55), channel_id=1, source_target_pairs={{0,1},{1,0},{2,3},{3,2},{4,5},{5,4},{6,7},{7,6},{8,9},{9,8},{10,11... | collective-permute-start | bytes 663560 | tf_op jit(solution)/shard_map/ppermute | solution.py:694
  75.0 18.2 %collective-permute-start.8 = (bf16[1,1,1,2,288,768]{5,4,3,2,1,0:T(8,128)(2,1)}, bf16[1,1,1,2,288,768]{5,4,3,2,1,0:T(8,128)(2,1)}, u32[]{:S(2)}, u32[]{:S(2)}) collective-permute-start(bf16[1,1,1,2,288,768]{5,4,3,2,1,0:T(8,128)(2,1)} %maximum_select_fusion.16), channel_id=1, source_target_pairs={{0,4},{2,6},{4,0},{6,2},{8,12},{10,14},{12,8},{14,10},{16,20},{18,... | collective-permute-start | bytes 2654216 | tf_op jit(solution)/shard_map/ppermute | solution.py:530
  76.8 26.6 %collective-permute-start.7 = (bf16[1,1,2,1,48,6528]{5,4,3,2,1,0:T(8,128)(2,1)}, bf16[1,1,2,1,48,6528]{5,4,3,2,1,0:T(8,128)(2,1)S(1)}, u32[]{:S(2)}, u32[]{:S(2)}) collective-permute-start(bf16[1,1,2,1,48,6528]{5,4,3,2,1,0:T(8,128)(2,1)} %maximum_select_fusion.10), channel_id=1, source_target_pairs={{0,8},{2,10},{4,12},{6,14},{8,0},{10,2},{12,4},{14,6},{16,24},{18,... | collective-permute-start | bytes 3760136 | tf_op jit(solution)/shard_map/ppermute | solution.py:530
  103.4 17.0 %collective-permute-start.14 = (bf16[1,1,1,1,96,384]{5,4,3,2,1,0:T(8,128)(2,1)}, bf16[1,1,1,1,96,384]{5,4,3,2,1,0:T(8,128)(2,1)S(1)}, u32[]{:S(2)}, u32[]{:S(2)}) collective-permute-start(bf16[1,1,1,1,96,384]{5,4,3,2,1,0:T(8,128)(2,1)} %collective-permute-done.10), channel_id=1, source_target_pairs={{0,8},{2,10},{4,12},{6,14},{8,0},{10,2},{12,4},{14,6},{16,24},{18,... | collective-permute-start | bytes 221192 | tf_op jit(solution)/shard_map/ppermute | solution.py:530
  104.4 16.0 %collective-permute-start.13 = (bf16[1,1,1,1,24,4608]{5,4,3,2,1,0:T(8,128)(2,1)}, bf16[1,1,1,1,24,4608]{5,4,3,2,1,0:T(8,128)(2,1)S(1)}, u32[]{:S(2)}, u32[]{:S(2)}) collective-permute-start(bf16[1,1,1,1,24,4608]{5,4,3,2,1,0:T(8,128)(2,1)} %collective-permute-done.9), channel_id=1, source_target_pairs={{0,4},{2,6},{4,0},{6,2},{8,12},{10,14},{12,8},{14,10},{16,20},{18,... | collective-permute-start | bytes 663560 | tf_op jit(solution)/shard_map/ppermute | solution.py:530
  121.6 24.5 %collective-permute-start.17 = (bf16[1,1,1,2,96,384]{5,4,3,2,1,0:T(8,128)(2,1)S(1)}, bf16[1,1,1,2,96,384]{5,4,3,2,1,0:T(8,128)(2,1)S(1)}, u32[]{:S(2)}, u32[]{:S(2)}) collective-permute-start(bf16[1,1,1,2,96,384]{5,4,3,2,1,0:T(8,128)(2,1)S(1)} %maximum_select_fusion.38), channel_id=1, source_target_pairs={{0,4},{2,6},{4,0},{6,2},{8,12},{10,14},{12,8},{14,10},{16,20},{18,... | collective-permute-start | bytes 442376 | tf_op jit(solution)/shard_map/ppermute | solution.py:530
  123.4 22.8 %collective-permute-start.16 = (bf16[1,1,2,1,24,4608]{5,4,3,2,1,0:T(8,128)(2,1)S(1)}, bf16[1,1,2,1,24,4608]{5,4,3,2,1,0:T(8,128)(2,1)S(1)}, u32[]{:S(2)}, u32[]{:S(2)}) collective-permute-start(bf16[1,1,2,1,24,4608]{5,4,3,2,1,0:T(8,128)(2,1)S(1)} %maximum_select_fusion.29), channel_id=1, source_target_pairs={{0,8},{2,10},{4,12},{6,14},{8,0},{10,2},{12,4},{14,6},{16,24},{18,... | collective-permute-start | bytes 1327112 | tf_op jit(solution)/shard_map/ppermute | solution.py:530
  148.0 92.8 %collective-permute-start.24 = (bf16[320,768]{1,0:T(8,128)(2,1)}, bf16[320,768]{1,0:T(8,128)(2,1)}, u32[]{:S(2)}, u32[]{:S(2)}) collective-permute-start(bf16[320,768]{1,0:T(8,128)(2,1)} %get-tuple-element.287), channel_id=1, source_target_pairs={{0,2},{2,0},{4,6},{6,4},{8,10},{10,8},{12,14},{14,12},{16,18},{18,... | collective-permute-start | bytes 1474568 | tf_op jit(solution)/shard_map/ppermute | solution.py:530
  148.1 92.7 %collective-permute-start.23 = (bf16[2,320,768]{2,1,0:T(8,128)(2,1)}, bf16[2,320,768]{2,1,0:T(8,128)(2,1)}, u32[]{:S(2)}, u32[]{:S(2)}) collective-permute-start(bf16[2,320,768]{2,1,0:T(8,128)(2,1)} %get-tuple-element.286.al_ref), channel_id=1, source_target_pairs={{0,2},{2,0},{4,6},{6,4},{8,10},{10,8},{12,14},{14,12},{16,18},{18,... | collective-permute-start | bytes 2949128 | tf_op jit(solution)/shard_map/ppermute | solution.py:530
  149.1 19.0 %collective-permute-start.20 = (f32[1]{0:T(128)}, f32[1]{0:T(128)}, u32[]{:S(2)}, u32[]{:S(2)}) collective-permute-start(f32[1]{0:T(128)} %add.709), channel_id=1, source_target_pairs={{0,8},{2,10},{4,12},{6,14},{8,0},{10,2},{12,4},{14,6},{16,24},{18,... | collective-permute-start | bytes 20 | tf_op jit(solution)/shard_map/ppermute | solution.py:530
  154.5 86.3 %collective-permute-start.22 = (bf16[320,4608]{1,0:T(8,128)(2,1)}, bf16[320,4608]{1,0:T(8,128)(2,1)}, u32[]{:S(2)}, u32[]{:S(2)}) collective-permute-start(bf16[320,4608]{1,0:T(8,128)(2,1)} %get-tuple-element.285), channel_id=1, source_target_pairs={{0,2},{2,0},{4,6},{6,4},{8,10},{10,8},{12,14},{14,12},{16,18},{18,... | collective-permute-start | bytes 8847368 | tf_op jit(solution)/shard_map/ppermute | solution.py:530
  168.8 72.0 %collective-permute-start.21 = (f32[1]{0:T(128)}, f32[1]{0:T(128)}, u32[]{:S(2)}, u32[]{:S(2)}) collective-permute-start(f32[1]{0:T(128)} %add.710), channel_id=1, source_target_pairs={{0,16},{2,18},{4,20},{6,22},{8,24},{10,26},{12,28},{14,30},{16,0},... | collective-permute-start | bytes 20 | tf_op jit(solution)/shard_map/ppermute | solution.py:530
  307.5 25.2 %collective-permute-start.25 = (f32[2,1,2,2,24,3456]{5,4,3,2,1,0:T(8,128)S(1)}, f32[2,1,2,2,24,3456]{5,4,3,2,1,0:T(8,128)}, u32[]{:S(2)}, u32[]{:S(2)}) collective-permute-start(f32[2,1,2,2,24,3456]{5,4,3,2,1,0:T(8,128)S(1)} %constant_dynamic-slice_fusion.19), channel_id=1, source_target_pairs={{0,2},{2,0},{4,6},{6,4},{8,10},{10,8},{12,14},{14,12},{16,18},{18,... | collective-permute-start | bytes 7962632 | tf_op jit(solution)/shard_map/ppermute | solution.py:530
  311.1 21.6 %collective-permute-start.26 = (f32[2,1,2,2,96,384]{5,4,3,2,1,0:T(8,128)}, f32[2,1,2,2,96,384]{5,4,3,2,1,0:T(8,128)}, u32[]{:S(2)}, u32[]{:S(2)}) collective-permute-start(f32[2,1,2,2,96,384]{5,4,3,2,1,0:T(8,128)} %constant_dynamic-slice_fusion.18), channel_id=1, source_target_pairs={{0,2},{2,0},{4,6},{6,4},{8,10},{10,8},{12,14},{14,12},{16,18},{18,... | collective-permute-start | bytes 3538952 | tf_op jit(solution)/shard_map/ppermute | solution.py:530
  338.2 23.0 %collective-permute-start.28 = (f32[2,1,2,1,96,384]{5,4,3,2,1,0:T(8,128)}, f32[2,1,2,1,96,384]{5,4,3,2,1,0:T(8,128)}, u32[]{:S(2)}, u32[]{:S(2)}) collective-permute-start(f32[2,1,2,1,96,384]{5,4,3,2,1,0:T(8,128)} %constant_dynamic-slice_fusion.16), channel_id=1, source_target_pairs={{0,8},{2,10},{4,12},{6,14},{8,0},{10,2},{12,4},{14,6},{16,24},{18,... | collective-permute-start | bytes 1769480 | tf_op jit(solution)/shard_map/ppermute | solution.py:530
  340.4 31.2 %collective-permute-start.27 = (f32[2,1,1,2,24,3456]{5,4,3,2,1,0:T(8,128)}, f32[2,1,1,2,24,3456]{5,4,3,2,1,0:T(8,128)}, u32[]{:S(2)}, u32[]{:S(2)}) collective-permute-start(f32[2,1,1,2,24,3456]{5,4,3,2,1,0:T(8,128)} %constant_dynamic-slice_fusion.17), channel_id=1, source_target_pairs={{0,4},{2,6},{4,0},{6,2},{8,12},{10,14},{12,8},{14,10},{16,20},{18,... | collective-permute-start | bytes 3981320 | tf_op jit(solution)/shard_map/ppermute | solution.py:530
  374.4 36.8 %collective-permute-start.30 = (f32[1,1,2,1,96,384]{5,4,3,2,1,0:T(8,128)S(1)}, f32[1,1,2,1,96,384]{5,4,3,2,1,0:T(8,128)S(1)}, u32[]{:S(2)}, u32[]{:S(2)}) collective-permute-start(f32[1,1,2,1,96,384]{5,4,3,2,1,0:T(8,128)S(1)} %constant_dynamic-slice_fusion.14), channel_id=1, source_target_pairs={{0,1},{1,0},{2,3},{3,2},{4,5},{5,4},{6,7},{7,6},{8,9},{9,8},{10,11... | collective-permute-start | bytes 884744 | tf_op jit(solution)/shard_map/ppermute | solution.py:530
  376.1 35.2 %collective-permute-start.29 = (f32[2,1,1,1,24,3456]{5,4,3,2,1,0:T(8,128)S(1)}, f32[2,1,1,1,24,3456]{5,4,3,2,1,0:T(8,128)S(1)}, u32[]{:S(2)}, u32[]{:S(2)}) collective-permute-start(f32[2,1,1,1,24,3456]{5,4,3,2,1,0:T(8,128)S(1)} %constant_dynamic-slice_fusion.15), channel_id=1, source_target_pairs={{0,8},{2,10},{4,12},{6,14},{8,0},{10,2},{12,4},{14,6},{16,24},{18,... | collective-permute-start | bytes 1990664 | tf_op jit(solution)/shard_map/ppermute | solution.py:530
  411.4 21.4 %collective-permute-start.32 = (f32[1,1,1,1,96,384]{5,4,3,2,1,0:T(8,128)S(1)}, f32[1,1,1,1,96,384]{5,4,3,2,1,0:T(8,128)S(1)}, u32[]{:S(2)}, u32[]{:S(2)}) collective-permute-start(f32[1,1,1,1,96,384]{5,4,3,2,1,0:T(8,128)S(1)} %constant_dynamic-slice_fusion.12), channel_id=1, source_target_pairs={{0,4},{2,6},{4,0},{6,2},{8,12},{10,14},{12,8},{14,10},{16,20},{18,... | collective-permute-start | bytes 442376 | tf_op jit(solution)/shard_map/ppermute | solution.py:530
  413.0 19.8 %collective-permute-start.31 = (f32[1,1,1,1,24,3456]{5,4,3,2,1,0:T(8,128)S(1)}, f32[1,1,1,1,24,3456]{5,4,3,2,1,0:T(8,128)S(1)}, u32[]{:S(2)}, u32[]{:S(2)}) collective-permute-start(f32[1,1,1,1,24,3456]{5,4,3,2,1,0:T(8,128)S(1)} %constant_dynamic-slice_fusion.13), channel_id=1, source_target_pairs={{0,1},{1,0},{2,3},{3,2},{4,5},{5,4},{6,7},{7,6},{8,9},{9,8},{10,11... | collective-permute-start | bytes 995336 | tf_op jit(solution)/shard_map/ppermute | solution.py:530
  432.9 22.3 %collective-permute-start.34 = (f32[1,1,1,1,96,384]{5,4,3,2,1,0:T(8,128)S(1)}, f32[1,1,1,1,96,384]{5,4,3,2,1,0:T(8,128)S(1)}, u32[]{:S(2)}, u32[]{:S(2)}) collective-permute-start(f32[1,1,1,1,96,384]{5,4,3,2,1,0:T(8,128)S(1)} %dynamic-slice_add_fusion.13), channel_id=1, source_target_pairs={{0,16},{2,18},{4,20},{6,22},{8,24},{10,26},{12,28},{14,30},{16,0},... | collective-permute-start | bytes 442376 | tf_op jit(solution)/shard_map/ppermute | solution.py:530
  433.3 21.9 %collective-permute-start.33 = (f32[1,1,1,1,24,3456]{5,4,3,2,1,0:T(8,128)S(1)}, f32[1,1,1,1,24,3456]{5,4,3,2,1,0:T(8,128)S(1)}, u32[]{:S(2)}, u32[]{:S(2)}) collective-permute-start(f32[1,1,1,1,24,3456]{5,4,3,2,1,0:T(8,128)S(1)} %dynamic-slice_add_fusion.8), channel_id=1, source_target_pairs={{0,16},{2,18},{4,20},{6,22},{8,24},{10,26},{12,28},{14,30},{16,0},... | collective-permute-start | bytes 995336 | tf_op jit(solution)/shard_map/ppermute | solution.py:530
  521.0 21.1 %collective-permute-start.43 = (f32[1,1,1,1,96,384]{5,4,3,2,1,0:T(8,128)}, f32[1,1,1,1,96,384]{5,4,3,2,1,0:T(8,128)}, u32[]{:S(2)}, u32[]{:S(2)}) collective-permute-start(f32[1,1,1,1,96,384]{5,4,3,2,1,0:T(8,128)} %get-tuple-element.488), channel_id=1, source_target_pairs={{0,8},{2,10},{4,12},{6,14},{8,0},{10,2},{12,4},{14,6},{16,24},{18,... | collective-permute-start | bytes 442376 | tf_op jit(solution)/shard_map/ppermute | solution.py:530
  522.1 20.5 %collective-permute-start.42 = (f32[1,1,1,1,24,3456]{5,4,2,3,1,0:T(8,128)S(1)}, f32[1,1,1,1,24,3456]{5,4,2,3,1,0:T(8,128)S(1)}, u32[]{:S(2)}, u32[]{:S(2)}) collective-permute-start(f32[1,1,1,1,24,3456]{5,4,2,3,1,0:T(8,128)S(1)} %get-tuple-element.498), channel_id=1, source_target_pairs={{0,4},{2,6},{4,0},{6,2},{8,12},{10,14},{12,8},{14,10},{16,20},{18,... | collective-permute-start | bytes 995336 | tf_op jit(solution)/shard_map/ppermute | solution.py:530
  532.0 17.6 %collective-permute-start.38 = (f32[1,14720]{1,0:T(1,128)S(1)}, f32[1,14720]{1,0:T(1,128)S(1)}, u32[]{:S(2)}, u32[]{:S(2)}) collective-permute-start(f32[1,14720]{1,0:T(1,128)S(1)} %reshape.2751), channel_id=1, source_target_pairs={{0,2},{2,0},{4,6},{6,4},{8,10},{10,8},{12,14},{14,12},{16,18},{18,... | collective-permute-start | bytes 176648 | tf_op jit(solution)/shard_map/ppermute | solution.py:530
  533.6 12.9 %collective-permute-start.37 = (bf16[2,320,384]{2,1,0:T(8,128)(2,1)S(1)}, bf16[2,320,384]{2,1,0:T(8,128)(2,1)S(1)}, u32[]{:S(2)}, u32[]{:S(2)}) collective-permute-start(bf16[2,320,384]{2,1,0:T(8,128)(2,1)S(1)} %pad_maximum_fusion.2), channel_id=1, source_target_pairs={{0,2},{2,0},{4,6},{6,4},{8,10},{10,8},{12,14},{14,12},{16,18},{18,... | collective-permute-start | bytes 1474568 | tf_op jit(solution)/shard_map/ppermute | solution.py:530
  536.6 20.6 %collective-permute-start.41 = (f32[2,1,2,2,48,384]{5,4,3,2,1,0:T(8,128)}, f32[2,1,2,2,48,384]{5,4,3,2,1,0:T(8,128)}, u32[]{:S(2)}, u32[]{:S(2)}) collective-permute-start(f32[2,1,2,2,48,384]{5,4,3,2,1,0:T(8,128)} %constant_dynamic-slice_fusion.6), channel_id=1, source_target_pairs={{0,2},{2,0},{4,6},{6,4},{8,10},{10,8},{12,14},{14,12},{16,18},{18,... | collective-permute-start | bytes 1769480 | tf_op jit(solution)/shard_map/ppermute | solution.py:530
  548.6 16.9 %collective-permute-start.44 = (f32[1,1,2,1,24,3456]{5,4,2,3,1,0:T(8,128)}, f32[1,1,2,1,24,3456]{5,4,2,3,1,0:T(8,128)}, u32[]{:S(2)}, u32[]{:S(2)}) collective-permute-start(f32[1,1,2,1,24,3456]{5,4,2,3,1,0:T(8,128)} %maximum_select_fusion.21), channel_id=1, source_target_pairs={{0,8},{2,10},{4,12},{6,14},{8,0},{10,2},{12,4},{14,6},{16,24},{18,... | collective-permute-start | bytes 1990664 | tf_op jit(solution)/shard_map/ppermute | solution.py:530
  549.7 15.9 %collective-permute-start.39 = (f32[1,14720]{1,0:T(1,128)S(1)}, f32[1,14720]{1,0:T(1,128)S(1)}, u32[]{:S(2)}, u32[]{:S(2)}) collective-permute-start(f32[1,14720]{1,0:T(1,128)S(1)} %maximum_select_fusion.45), channel_id=1, source_target_pairs={{0,4},{2,6},{4,0},{6,2},{8,12},{10,14},{12,8},{14,10},{16,20},{18,... | collective-permute-start | bytes 176648 | tf_op jit(solution)/shard_map/ppermute | solution.py:530
  568.4 17.6 %collective-permute-start.49 = (f32[1,1,2,2,24,3456]{5,4,2,3,1,0:T(8,128)S(1)}, f32[1,1,2,2,24,3456]{5,4,2,3,1,0:T(8,128)}, u32[]{:S(2)}, u32[]{:S(2)}) collective-permute-start(f32[1,1,2,2,24,3456]{5,4,2,3,1,0:T(8,128)S(1)} %maximum_select_fusion.9), channel_id=1, source_target_pairs={{0,2},{2,0},{4,6},{6,4},{8,10},{10,8},{12,14},{14,12},{16,18},{18,... | collective-permute-start | bytes 3981320 | tf_op jit(solution)/shard_map/ppermute | solution.py:530
  586.1 17.5 %collective-permute-start.53 = (f32[1,14720]{1,0:T(1,128)S(1)}, f32[1,14720]{1,0:T(1,128)S(1)}, u32[]{:S(2)}, u32[]{:S(2)}) collective-permute-start(f32[1,14720]{1,0:T(1,128)S(1)} %maximum_select_fusion.43), channel_id=1, source_target_pairs={{0,24},{2,26},{4,28},{6,30},{8,16},{10,18},{12,20},{14,22},{16,8},... | collective-permute-start | bytes 176648 | tf_op jit(solution)/shard_map/ppermute | solution.py:530
  587.0 16.6 %collective-permute-start.52 = (f32[1,14720]{1,0:T(1,128)S(1)}, f32[1,14720]{1,0:T(1,128)S(1)}, u32[]{:S(2)}, u32[]{:S(2)}) collective-permute-start(f32[1,14720]{1,0:T(1,128)S(1)} %maximum_select_fusion.43), channel_id=1, source_target_pairs={{0,16},{2,18},{4,20},{6,22},{8,24},{10,26},{12,28},{14,30},{16,0},... | collective-permute-start | bytes 176648 | tf_op jit(solution)/shard_map/ppermute | solution.py:530
  588.7 14.9 %collective-permute-start.51 = (f32[1,14720]{1,0:T(1,128)S(1)}, f32[1,14720]{1,0:T(1,128)S(1)}, u32[]{:S(2)}, u32[]{:S(2)}) collective-permute-start(f32[1,14720]{1,0:T(1,128)S(1)} %maximum_select_fusion.43), channel_id=1, source_target_pairs={{0,8},{2,10},{4,12},{6,14},{8,0},{10,2},{12,4},{14,6},{16,24},{18,... | collective-permute-start | bytes 176648 | tf_op jit(solution)/shard_map/ppermute | solution.py:530
  609.3 40.9 %collective-permute-start.58 = (f16[1,2,2,576,384]{4,3,2,1,0:T(8,128)(2,1)}, f16[1,2,2,576,384]{4,3,2,1,0:T(8,128)(2,1)S(1)}, u32[]{:S(2)}, u32[]{:S(2)}) collective-permute-start(f16[1,2,2,576,384]{4,3,2,1,0:T(8,128)(2,1)} %multiply_convert_fusion), channel_id=1, source_target_pairs={{0,1},{1,0},{2,3},{3,2},{4,5},{5,4},{6,7},{7,6},{8,9},{9,8},{10,11... | collective-permute-start | bytes 5308424 | tf_op jit(solution)/shard_map/ppermute | solution.py:530
  614.4 35.8 %collective-permute-start.56 = (f16[2,1,2,96,1536]{4,3,2,1,0:T(8,128)(2,1)}, f16[2,1,2,96,1536]{4,3,2,1,0:T(8,128)(2,1)}, u32[]{:S(2)}, u32[]{:S(2)}) collective-permute-start(f16[2,1,2,96,1536]{4,3,2,1,0:T(8,128)(2,1)} %multiply_convert_fusion.2), channel_id=1, source_target_pairs={{0,4},{2,6},{4,0},{6,2},{8,12},{10,14},{12,8},{14,10},{16,20},{18,... | collective-permute-start | bytes 3538952 | tf_op jit(solution)/shard_map/ppermute | solution.py:530
  616.9 33.4 %collective-permute-start.57 = (f16[2,2,1,96,1536]{4,3,2,1,0:T(8,128)(2,1)}, f16[2,2,1,96,1536]{4,3,2,1,0:T(8,128)(2,1)}, u32[]{:S(2)}, u32[]{:S(2)}) collective-permute-start(f16[2,2,1,96,1536]{4,3,2,1,0:T(8,128)(2,1)} %multiply_convert_fusion.1), channel_id=1, source_target_pairs={{0,8},{2,10},{4,12},{6,14},{8,0},{10,2},{12,4},{14,6},{16,24},{18,... | collective-permute-start | bytes 3538952 | tf_op jit(solution)/shard_map/ppermute | solution.py:530
  618.8 31.5 %collective-permute-start.59 = (f32[1,1,1,1,24,1152]{5,4,3,2,1,0:T(8,128)S(1)}, f32[1,1,1,1,24,1152]{5,4,3,2,1,0:T(8,128)S(1)}, u32[]{:S(2)}, u32[]{:S(2)}) collective-permute-start(f32[1,1,1,1,24,1152]{5,4,3,2,1,0:T(8,128)S(1)} %constant_dynamic-slice_fusion.1), channel_id=1, source_target_pairs={{0,1},{1,0},{2,3},{3,2},{4,5},{5,4},{6,7},{7,6},{8,9},{9,8},{10,11... | collective-permute-start | bytes 331784 | tf_op jit(solution)/shard_map/ppermute | solution.py:530
  620.0 21.6 %collective-permute-start.60 = (f32[1,1,1,1,48,384]{5,4,3,2,1,0:T(8,128)}, f32[1,1,1,1,48,384]{5,4,3,2,1,0:T(8,128)S(1)}, u32[]{:S(2)}, u32[]{:S(2)}) collective-permute-start(f32[1,1,1,1,48,384]{5,4,3,2,1,0:T(8,128)} %constant_dynamic-slice_fusion), channel_id=1, source_target_pairs={{0,4},{2,6},{4,0},{6,2},{8,12},{10,14},{12,8},{14,10},{16,20},{18,... | collective-permute-start | bytes 221192 | tf_op jit(solution)/shard_map/ppermute | solution.py:530
  653.6 22.4 %collective-permute-start.62 = (f16[1,2,1,96,1536]{4,3,2,1,0:T(8,128)(2,1)S(1)}, f16[1,2,1,96,1536]{4,3,2,1,0:T(8,128)(2,1)S(1)}, u32[]{:S(2)}, u32[]{:S(2)}) collective-permute-start(f16[1,2,1,96,1536]{4,3,2,1,0:T(8,128)(2,1)S(1)} %multiply_convert_fusion.4), channel_id=1, source_target_pairs={{0,1},{1,0},{2,3},{3,2},{4,5},{5,4},{6,7},{7,6},{8,9},{9,8},{10,11... | collective-permute-start | bytes 1769480 | tf_op jit(solution)/shard_map/ppermute | solution.py:530
  658.4 18.6 %collective-permute-start.63 = (f16[1,1,2,576,384]{4,3,2,1,0:T(8,128)(2,1)S(1)}, f16[1,1,2,576,384]{4,3,2,1,0:T(8,128)(2,1)S(1)}, u32[]{:S(2)}, u32[]{:S(2)}) collective-permute-start(f16[1,1,2,576,384]{4,3,2,1,0:T(8,128)(2,1)S(1)} %multiply_convert_fusion.3), channel_id=1, source_target_pairs={{0,4},{2,6},{4,0},{6,2},{8,12},{10,14},{12,8},{14,10},{16,20},{18,... | collective-permute-start | bytes 2654216 | tf_op jit(solution)/shard_map/ppermute | solution.py:530
  661.3 15.6 %collective-permute-start.61 = (f16[2,1,1,96,1536]{4,3,2,1,0:T(8,128)(2,1)S(1)}, f16[2,1,1,96,1536]{4,3,2,1,0:T(8,128)(2,1)S(1)}, u32[]{:S(2)}, u32[]{:S(2)}) collective-permute-start(f16[2,1,1,96,1536]{4,3,2,1,0:T(8,128)(2,1)S(1)} %multiply_convert_fusion.5), channel_id=1, source_target_pairs={{0,8},{2,10},{4,12},{6,14},{8,0},{10,2},{12,4},{14,6},{16,24},{18,... | collective-permute-start | bytes 1769480 | tf_op jit(solution)/shard_map/ppermute | solution.py:530
  663.1 12.9 %collective-permute-start.64 = (f32[1,1,1,1,24,1152]{5,4,3,2,1,0:T(8,128)S(1)}, f32[1,1,1,1,24,1152]{5,4,3,2,1,0:T(8,128)S(1)}, u32[]{:S(2)}, u32[]{:S(2)}) collective-permute-start(f32[1,1,1,1,24,1152]{5,4,3,2,1,0:T(8,128)S(1)} %dynamic-slice_add_fusion.14), channel_id=1, source_target_pairs={{0,16},{2,18},{4,20},{6,22},{8,24},{10,26},{12,28},{14,30},{16,0},... | collective-permute-start | bytes 331784 | tf_op jit(solution)/shard_map/ppermute | solution.py:530
  678.4 15.8 %collective-permute-start.69 = (f32[1,1,1,1,24,1152]{5,4,2,3,1,0:T(8,128)S(1)}, f32[1,1,1,1,24,1152]{5,4,2,3,1,0:T(8,128)S(1)}, u32[]{:S(2)}, u32[]{:S(2)}) collective-permute-start(f32[1,1,1,1,24,1152]{5,4,2,3,1,0:T(8,128)S(1)} %get-tuple-element.512), channel_id=1, source_target_pairs={{0,4},{2,6},{4,0},{6,2},{8,12},{10,14},{12,8},{14,10},{16,20},{18,... | collective-permute-start | bytes 331784 | tf_op jit(solution)/shard_map/ppermute | solution.py:530
  681.4 12.9 %collective-permute-start.67 = (f16[1,1,1,96,1536]{4,3,2,1,0:T(8,128)(2,1)}, f16[1,1,1,96,1536]{4,3,2,1,0:T(8,128)(2,1)}, u32[]{:S(2)}, u32[]{:S(2)}) collective-permute-start(f16[1,1,1,96,1536]{4,3,2,1,0:T(8,128)(2,1)} %multiply_convert_fusion.13), channel_id=1, source_target_pairs={{0,4},{2,6},{4,0},{6,2},{8,12},{10,14},{12,8},{14,10},{16,20},{18,... | collective-permute-start | bytes 884744 | tf_op jit(solution)/shard_map/ppermute | solution.py:530
  699.8 42.8 %collective-permute-start.73 = (f16[1,1,1,576,384]{4,3,2,1,0:T(8,128)(2,1)S(1)}, f16[1,1,1,576,384]{4,3,2,1,0:T(8,128)(2,1)S(1)}, u32[]{:S(2)}, u32[]{:S(2)}) collective-permute-start(f16[1,1,1,576,384]{4,3,2,1,0:T(8,128)(2,1)S(1)} %multiply_convert_fusion.7), channel_id=1, source_target_pairs={{0,16},{2,18},{4,20},{6,22},{8,24},{10,26},{12,28},{14,30},{16,0},... | collective-permute-start | bytes 1327112 | tf_op jit(solution)/shard_map/ppermute | solution.py:530
  704.8 32.6 %collective-permute-start.72 = (f16[1,1,1,96,1536]{4,3,2,1,0:T(8,128)(2,1)S(1)}, f16[1,1,1,96,1536]{4,3,2,1,0:T(8,128)(2,1)S(1)}, u32[]{:S(2)}, u32[]{:S(2)}) collective-permute-start(f16[1,1,1,96,1536]{4,3,2,1,0:T(8,128)(2,1)S(1)} %multiply_convert_fusion.11), channel_id=1, source_target_pairs={{0,16},{2,18},{4,20},{6,22},{8,24},{10,26},{12,28},{14,30},{16,0},... | collective-permute-start | bytes 884744 | tf_op jit(solution)/shard_map/ppermute | solution.py:530
  705.7 36.9 %collective-permute-start.71 = (f16[1,1,1,96,1536]{4,3,2,1,0:T(8,128)(2,1)S(1)}, f16[1,1,1,96,1536]{4,3,2,1,0:T(8,128)(2,1)S(1)}, u32[]{:S(2)}, u32[]{:S(2)}) collective-permute-start(f16[1,1,1,96,1536]{4,3,2,1,0:T(8,128)(2,1)S(1)} %multiply_convert_fusion.12), channel_id=1, source_target_pairs={{0,16},{2,18},{4,20},{6,22},{8,24},{10,26},{12,28},{14,30},{16,0},... | collective-permute-start | bytes 884744 | tf_op jit(solution)/shard_map/ppermute | solution.py:530
  753.4 26.8 %collective-permute-start.85 = (f32[1,1,2,2,48,384]{5,4,3,2,1,0:T(8,128)S(1)}, f32[1,1,2,2,48,384]{5,4,3,2,1,0:T(8,128)S(1)}, u32[]{:S(2)}, u32[]{:S(2)}) collective-permute-start(f32[1,1,2,2,48,384]{5,4,3,2,1,0:T(8,128)S(1)} %maximum_select_fusion.35), channel_id=1, source_target_pairs={{0,2},{2,0},{4,6},{6,4},{8,10},{10,8},{12,14},{14,12},{16,18},{18,... | collective-permute-start | bytes 884744 | tf_op jit(solution)/shard_map/ppermute | solution.py:530
  755.7 13.6 %collective-permute-start.78 = (f16[1,1,1,96,1536]{4,3,2,1,0:T(8,128)(2,1)S(1)}, f16[1,1,1,96,1536]{4,3,2,1,0:T(8,128)(2,1)S(1)}, u32[]{:S(2)}, u32[]{:S(2)}) collective-permute-start(f16[1,1,1,96,1536]{4,3,2,1,0:T(8,128)(2,1)S(1)} %get-tuple-element.502), channel_id=1, source_target_pairs={{0,4},{2,6},{4,0},{6,2},{8,12},{10,14},{12,8},{14,10},{16,20},{18,... | collective-permute-start | bytes 884744 | tf_op jit(solution)/shard_map/ppermute | solution.py:530
  756.0 24.2 %collective-permute-start.84 = (f32[1,1,2,2,24,1152]{5,4,2,3,1,0:T(8,128)S(1)}, f32[1,1,2,2,24,1152]{5,4,2,3,1,0:T(8,128)S(1)}, u32[]{:S(2)}, u32[]{:S(2)}) collective-permute-start(f32[1,1,2,2,24,1152]{5,4,2,3,1,0:T(8,128)S(1)} %maximum_select_fusion.31), channel_id=1, source_target_pairs={{0,2},{2,0},{4,6},{6,4},{8,10},{10,8},{12,14},{14,12},{16,18},{18,... | collective-permute-start | bytes 1327112 | tf_op jit(solution)/shard_map/ppermute | solution.py:530
  772.8 13.8 %collective-permute-start.83 = (f32[1]{0:T(128)}, f32[1]{0:T(128)}, u32[]{:S(2)}, u32[]{:S(2)}) collective-permute-start(f32[1]{0:T(128)} %add.769), channel_id=1, source_target_pairs={{0,12},{2,14},{4,8},{6,10},{8,4},{10,6},{12,0},{14,2},{16,28},{18,... | collective-permute-start | bytes 20 | tf_op jit(solution)/shard_map/ppermute | solution.py:530
  784.6 19.5 %collective-permute-start.87 = (f16[1,2,1,96,1536]{4,3,2,1,0:T(8,128)(2,1)}, f16[1,2,1,96,1536]{4,3,2,1,0:T(8,128)(2,1)}, u32[]{:S(2)}, u32[]{:S(2)}) collective-permute-start(f16[1,2,1,96,1536]{4,3,2,1,0:T(8,128)(2,1)} %maximum_select_fusion.26), channel_id=1, source_target_pairs={{0,8},{2,10},{4,12},{6,14},{8,0},{10,2},{12,4},{14,6},{16,24},{18,... | collective-permute-start | bytes 1769480 | tf_op jit(solution)/shard_map/ppermute | solution.py:530
  784.9 24.2 %collective-permute-start.86 = (f16[1,2,1,96,1536]{4,3,2,1,0:T(8,128)(2,1)}, f16[1,2,1,96,1536]{4,3,2,1,0:T(8,128)(2,1)}, u32[]{:S(2)}, u32[]{:S(2)}) collective-permute-start(f16[1,2,1,96,1536]{4,3,2,1,0:T(8,128)(2,1)} %maximum_select_fusion.25), channel_id=1, source_target_pairs={{0,8},{2,10},{4,12},{6,14},{8,0},{10,2},{12,4},{14,6},{16,24},{18,... | collective-permute-start | bytes 1769480 | tf_op jit(solution)/shard_map/ppermute | solution.py:530
  786.6 22.4 %collective-permute-start.88 = (f16[1,1,2,576,384]{4,3,2,1,0:T(8,128)(2,1)}, f16[1,1,2,576,384]{4,3,2,1,0:T(8,128)(2,1)}, u32[]{:S(2)}, u32[]{:S(2)}) collective-permute-start(f16[1,1,2,576,384]{4,3,2,1,0:T(8,128)(2,1)} %maximum_select_fusion.20), channel_id=1, source_target_pairs={{0,4},{2,6},{4,0},{6,2},{8,12},{10,14},{12,8},{14,10},{16,20},{18,... | collective-permute-start | bytes 2654216 | tf_op jit(solution)/shard_map/ppermute | solution.py:530
  818.1 21.2 %collective-permute-start.90 = (f16[384,1536]{1,0:T(8,128)(2,1)S(1)}, f16[384,1536]{1,0:T(8,128)(2,1)S(1)}, u32[]{:S(2)}, u32[]{:S(2)}) collective-permute-start(f16[384,1536]{1,0:T(8,128)(2,1)S(1)} %bitcast.153), channel_id=1, source_target_pairs={{0,2},{2,0},{4,6},{6,4},{8,10},{10,8},{12,14},{14,12},{16,18},{18,... | collective-permute-start | bytes 3538952 | tf_op jit(solution)/shard_map/ppermute | solution.py:530
  820.7 18.5 %collective-permute-start.91 = (f16[384,1536]{1,0:T(8,128)(2,1)S(1)}, f16[384,1536]{1,0:T(8,128)(2,1)S(1)}, u32[]{:S(2)}, u32[]{:S(2)}) collective-permute-start(f16[384,1536]{1,0:T(8,128)(2,1)S(1)} %bitcast.150), channel_id=1, source_target_pairs={{0,2},{2,0},{4,6},{6,4},{8,10},{10,8},{12,14},{14,12},{16,18},{18,... | collective-permute-start | bytes 3538952 | tf_op jit(solution)/shard_map/ppermute | solution.py:530
  (113 other events, 948.7 us)

commit v4 on v3

--- a/solution.py
+++ b/solution.py
@@ -836,7 +836,7 @@
     far_rights = right_swap.result
     wide_cols, tall_rows = 2 * D, PATCH + FF
     zero = lambda i, j: (0, 0, i)
-    hops = [vector_flight, late, dec_flight]
+    hops = [vector_flight, late]
     sum_up = pair_product(
         (normed_two[None], far_lefts[2][None]), (rights[0], far_rights[0]), D, wide_cols, D, D // 2,
         zero, lambda i, j: (0, 0, j), "grad_up",

time: 879 us -> 876 us (level)
  transfers between devices with their start and end apart: 92 -> 92, of which waited for: 18 -> 19; matrix products, arithmetic and copies ran while one was open for 19% -> 19% of each run, Pallas kernels for 30% -> 30%
where the time goes in v4:
time: 876 us; the launch traced here: 868 us
  Pallas kernels  382 us (44%)
  other arithmetic  187 us (21%)
  waiting for transfers between devices  128 us (15%)
  starting transfers between devices  92.9 us (11%)
  local copies, waits for them, and re-layouts  54.9 us (6%)
  between operations  22.5 us (3%)
    ppermute x87, waiting for transfers between devices, swap(): return lax.ppermute(value, name, [(i, i ^ hop) for i in range(size)])  128 us
    pallas_call x6, Pallas kernels, attn_bwd(): pl.pallas_call(functools.partial(bwd_body, 64 ** (-0.5), nb, 0), grid=(1,...  116 us
    ppermute x87, starting transfers between devices, swap(): return lax.ppermute(value, name, [(i, i ^ hop) for i in range(size)])  86.3 us
    pallas_call x1, Pallas kernels, dec_post(): pl.pallas_call(functools.partial(post_body, nb, R, keys), grid=(clips, nb...  64.1 us
    pallas_call x1, Pallas kernels, attn_fwd(): pl.pallas_call(body, grid=(clips, pairs, nb), in_specs=[pl.BlockSpec((1,...  63.8 us
    convert_element_type x5, other arithmetic, update(): return (*updated, updated[0].astype(jnp.bfloat16))  54.1 us
    pallas_call x4, Pallas kernels, pick_rows(): pl.pallas_call(pick_body, grid=(m // R,), in_specs=[pl.BlockSpec((1, R, 1...  33.4 us
    select_n x29, other arithmetic, join(): jnp.where(bit == 0, jnp.concatenate([mine, other], axis=dim), jnp.concate...  33.4 us
  transfers between devices with their start and end apart: 92, of which 19 were waited for; matrix products, arithmetic and copies ran while one was open for 19% of the time, Pallas kernels for 30%

profile of v4, /device:TPU:0, one launch (start us, length us, event | category | flops | bytes accessed | tf_op | source)
XLA Modules:
  0.0 868.3 jit_solution(3479617231454931480)
XLA Ops:
  4.9 2.6 collective-permute-start.4
  18.6 4.3 pick_seen_0.1.refs_0_
  22.9 4.3 pick_seen_1.1
  27.3 3.5 negate_select_fusion.4
  32.2 3.5 convert_element_type.197
  35.7 5.3 convert_element_type.196.refs_3_
  41.1 2.8 convert_element_type.195.refs_0_
  45.5 2.9 collective-permute-start.1
  56.3 12.5 %pick_hidden_0.1.refs_0_ = bf16[2,1440,1536]{2,1,0:T(8,128)(2,1)} custom-call(s32[2,1440,1]{2,1,0:T(8,128)} %copy.80.idx_ref, bf16[2,1568,1536]{2,1,0:T(8,128)(2,1)} %x_ref.7), custom_call_target="tpu_custom_call" | custom-call | flops 11314285568 | tf_op jit(solution)/shard_map/pick_hidden_0/pallas_call | solution.py:299
  78.1 12.2 %pick_hidden_1.1.t_ref = bf16[2,1440,1536]{2,1,0:T(8,128)(2,1)} custom-call(s32[2,1440,1]{2,1,0:T(8,128)} %copy.81.idx_ref, bf16[2,1568,1536]{2,1,0:T(8,128)(2,1)} %x_ref.7, bf16[2,1440,1536]{2,1,0:T(8,128)(2,1)} %pick_hidden_0.1.refs_0_), custom_call_target="tpu_custom_call", output_to_operand_aliasing={{}: (2, {})} | custom-call | flops 11314285568 | tf_op jit(solution)/shard_map/pick_hidden_1/pallas_call | solution.py:299
  93.2 10.1 %collective-permute-done.7 = bf16[1,1,2,1,48,6528]{5,4,3,2,1,0:T(8,128)(2,1)S(1)} collective-permute-done((bf16[1,1,2,1,48,6528]{5,4,3,2,1,0:T(8,128)(2,1)}, bf16[1,1,2,1,48,6528]{5,4,3,2,1,0:T(8,128)(2,1)S(1)}, u32[]{:S(2)}, u32[]{:S(2)}) %collective-permute-start.7) | collective-permute-done | bytes 1253408 | tf_op jit(solution)/shard_map/ppermute | solution.py:530
  109.4 7.5 fusion.7
  117.9 2.5 pad_maximum_fusion
  124.4 20.5 %enc_forward.1 = (f32[320,768]{1,0:T(8,128)}, bf16[320,2304]{1,0:T(8,128)(2,1)}, f32[320,768]{1,0:T(8,128)}, f32[320,3072]{1,0:T(8,128)}, f32[320,768]{1,0:T(8,1...) custom-call(s32[3]{0:T(128)} %pad_add_fusion.at_ref, ...), custom_call_target="tpu_custom_call" | custom-call | flops 20899999744 | tf_op jit(solution)/shard_map/enc_forward/pallas_call | solution.py:404
  158.7 9.4 %dec_qkv.1.q_ref.k_ref.v_ref = bf16[2,1568,1152]{2,1,0:T(8,128)(2,1)} custom-call(f32[2,1568,384]{2,1,0:T(8,128)} %scatter-add.4.h_ref, bf16[384,1152]{1,0:T(8,128)(2,1)} %slice.204.w_ref, f32[1,14592]{1,0:T(1,128)} %bitcast.186), custom_call_target="tpu_custom_call" | custom-call | flops 9900000256 | tf_op jit(solution)/shard_map/dec_qkv/pallas_call | solution.py:249
  168.8 4.0 collective-permute-start.21
  172.8 63.8 %dec_attend_forward.1 = (bf16[2,1440,384]{2,1,0:T(8,128)(2,1)}, f32[6,2,2,720]{3,2,1,0:T(2,128)}) custom-call(bf16[2,1568,1152]{2,1,0:T(8,128)(2,1)} %dec_qkv.1.q_ref.k_ref.v_ref, bf16[2,1568,1152]{2,1,0:T(8,128)(2,1)} %dec_qkv.1.q_ref.k_ref.v_ref, bf16[2,1568,1152]{2,1,0:T(8,128)(2,1)} %dec_qkv.1.q_ref.k_ref.v_ref), custom_call_target="tpu_custom_call" | custom-call | flops 71499997184 | tf_op jit(solution)/shard_map/dec_attend_forward/pallas_call | solution.py:67
  241.6 64.1 %dec_post.1 = (f32[2,1568,384]{2,1,0:T(8,128)}, bf16[2,1440,384]{2,1,0:T(8,128)(2,1)}, f32[384,3456]{1,0:T(8,128)}, f32[1536,384]{1,0:T(8,128)}, f32[8,384]{1,0:...) custom-call(s32[2]{0:T(128)} %cnt_ref.1, f32[1]{0:T(128)} %bitcast.32.inv_ref, f32[2,1568,384]{2,1,0:T(8,128)} %scatter-add.4.h_ref, ...), custom_call_target="tpu_custom_call" | custom-call | flops 73699999744 | tf_op jit(solution)/shard_map/dec_post/pallas_call | solution.py:233
  308.9 2.4 constant_dynamic-slice_fusion.18
  313.8 19.0 %dec_attend_backward_0_0.1 = (bf16[1,1568,128]{2,1,0:T(8,128)(2,1)}, bf16[1,1568,128]{2,1,0:T(8,128)(2,1)}, bf16[1,1568,128]{2,1,0:T(8,128)(2,1)}) custom-call(bf16[2,1568,1152]{2,1,0:T(8,128)(2,1)} %dec_qkv.1.q_ref.k_ref.v_ref, bf16[2,1568,1152]{2,1,0:T(8,128)(2,1)} %dec_qkv.1.q_ref.k_ref.v_ref, bf16[2,1568,1152]{2,1,0:T(8,128)(2,1)} %dec_qkv.1.q_ref.k_ref.v_ref, ...), custom_call_target="tpu_custom_call" | custom-call | flops 18699999232 | tf_op jit(solution)/shard_map/dec_attend_backward_0_0/pallas_call | solution.py:132
  334.7 2.8 dynamic-slice_add_fusion
  342.0 19.3 %dec_attend_backward_0_1.1 = (bf16[1,1568,128]{2,1,0:T(8,128)(2,1)}, bf16[1,1568,128]{2,1,0:T(8,128)(2,1)}, bf16[1,1568,128]{2,1,0:T(8,128)(2,1)}) custom-call(bf16[2,1568,1152]{2,1,0:T(8,128)(2,1)} %dec_qkv.1.q_ref.k_ref.v_ref, bf16[2,1568,1152]{2,1,0:T(8,128)(2,1)} %dec_qkv.1.q_ref.k_ref.v_ref, bf16[2,1568,1152]{2,1,0:T(8,128)(2,1)} %dec_qkv.1.q_ref.k_ref.v_ref, ...), custom_call_target="tpu_custom_call" | custom-call | flops 18699999232 | tf_op jit(solution)/shard_map/dec_attend_backward_0_1/pallas_call | solution.py:132
  361.3 10.4 %collective-permute-done.27 = f32[2,1,1,2,24,3456]{5,4,3,2,1,0:T(8,128)} collective-permute-done((f32[2,1,1,2,24,3456]{5,4,3,2,1,0:T(8,128)}, f32[2,1,1,2,24,3456]{5,4,3,2,1,0:T(8,128)}, u32[]{:S(2)}, u32[]{:S(2)}) %collective-permute-start.27) | collective-permute-done | bytes 1327136 | tf_op jit(solution)/shard_map/ppermute | solution.py:530
  377.2 19.4 %dec_attend_backward_0_2.1 = (bf16[1,1568,128]{2,1,0:T(8,128)(2,1)}, bf16[1,1568,128]{2,1,0:T(8,128)(2,1)}, bf16[1,1568,128]{2,1,0:T(8,128)(2,1)}) custom-call(bf16[2,1568,1152]{2,1,0:T(8,128)(2,1)} %dec_qkv.1.q_ref.k_ref.v_ref, bf16[2,1568,1152]{2,1,0:T(8,128)(2,1)} %dec_qkv.1.q_ref.k_ref.v_ref, bf16[2,1568,1152]{2,1,0:T(8,128)(2,1)} %dec_qkv.1.q_ref.k_ref.v_ref, ...), custom_call_target="tpu_custom_call" | custom-call | flops 18699999232 | tf_op jit(solution)/shard_map/dec_attend_backward_0_2/pallas_call | solution.py:132
  398.6 11.7 %dec_qkv_back_0.1 = (bf16[1,1568,384]{2,1,0:T(8,128)(2,1)}, f32[384,1152]{1,0:T(8,128)}, f32[8,384]{1,0:T(8,128)}) custom-call(f32[2,1568,384]{2,1,0:T(8,128)} %scatter-add.4.h_ref, f32[2,1568,384]{2,1,0:T(8,128)} %get-tuple-element.293.dmid_ref, bf16[384,1152]{1,0:T(8,128)(2,1)} %slice.204.w_ref, f32[1,14592]{1,0:T(1,128)} %bitcast.188, ...), custom_call_target="tpu_custom_call" | custom-call | flops 11000000512 | tf_op jit(solution)/shard_map/dec_qkv_back_0/pallas_call | solution.py:284
  413.7 19.2 %dec_attend_backward_1_0.1 = (bf16[1,1568,128]{2,1,0:T(8,128)(2,1)}, bf16[1,1568,128]{2,1,0:T(8,128)(2,1)}, bf16[1,1568,128]{2,1,0:T(8,128)(2,1)}) custom-call(bf16[2,1568,1152]{2,1,0:T(8,128)(2,1)} %dec_qkv.1.q_ref.k_ref.v_ref, bf16[2,1568,1152]{2,1,0:T(8,128)(2,1)} %dec_qkv.1.q_ref.k_ref.v_ref, bf16[2,1568,1152]{2,1,0:T(8,128)(2,1)} %dec_qkv.1.q_ref.k_ref.v_ref, ...), custom_call_target="tpu_custom_call" | custom-call | flops 18699999232 | tf_op jit(solution)/shard_map/dec_attend_backward_1_0/pallas_call | solution.py:132
  433.5 2.6 collective-permute-start.33
  436.0 19.3 %dec_attend_backward_1_1.1 = (bf16[1,1568,128]{2,1,0:T(8,128)(2,1)}, bf16[1,1568,128]{2,1,0:T(8,128)(2,1)}, bf16[1,1568,128]{2,1,0:T(8,128)(2,1)}) custom-call(bf16[2,1568,1152]{2,1,0:T(8,128)(2,1)} %dec_qkv.1.q_ref.k_ref.v_ref, bf16[2,1568,1152]{2,1,0:T(8,128)(2,1)} %dec_qkv.1.q_ref.k_ref.v_ref, bf16[2,1568,1152]{2,1,0:T(8,128)(2,1)} %dec_qkv.1.q_ref.k_ref.v_ref, ...), custom_call_target="tpu_custom_call" | custom-call | flops 18699999232 | tf_op jit(solution)/shard_map/dec_attend_backward_1_1/pallas_call | solution.py:132
  455.4 19.5 %dec_attend_backward_1_2.1 = (bf16[1,1568,128]{2,1,0:T(8,128)(2,1)}, bf16[1,1568,128]{2,1,0:T(8,128)(2,1)}, bf16[1,1568,128]{2,1,0:T(8,128)(2,1)}) custom-call(bf16[2,1568,1152]{2,1,0:T(8,128)(2,1)} %dec_qkv.1.q_ref.k_ref.v_ref, bf16[2,1568,1152]{2,1,0:T(8,128)(2,1)} %dec_qkv.1.q_ref.k_ref.v_ref, bf16[2,1568,1152]{2,1,0:T(8,128)(2,1)} %dec_qkv.1.q_ref.k_ref.v_ref, ...), custom_call_target="tpu_custom_call" | custom-call | flops 18699999232 | tf_op jit(solution)/shard_map/dec_attend_backward_1_2/pallas_call | solution.py:132
  474.9 11.8 %dec_qkv_back_1.1 = (bf16[1,1568,384]{2,1,0:T(8,128)(2,1)}, f32[384,1152]{1,0:T(8,128)}, f32[8,384]{1,0:T(8,128)}) custom-call(f32[2,1568,384]{2,1,0:T(8,128)} %scatter-add.4.h_ref, f32[2,1568,384]{2,1,0:T(8,128)} %get-tuple-element.293.dmid_ref, bf16[384,1152]{1,0:T(8,128)(2,1)} %slice.204.w_ref, f32[1,14592]{1,0:T(1,128)} %bitcast.189, ...), custom_call_target="tpu_custom_call" | custom-call | flops 11000000512 | tf_op jit(solution)/shard_map/dec_qkv_back_1/pallas_call | solution.py:284
  488.4 28.1 %enc_backward.1 = (bf16[320,768]{1,0:T(8,128)(2,1)}, bf16[320,3072]{1,0:T(8,128)(2,1)}, bf16[320,3072]{1,0:T(8,128)(2,1)}, bf16[320,768]{1,0:T(8,128)(2,1)}, f32...) custom-call(s32[3]{0:T(128)} %pad_add_fusion.at_ref, bf16[320,384]{1,0:T(8,128)(2,1)} %bitcast.172, ...), custom_call_target="tpu_custom_call" | custom-call | flops 29699999744 | tf_op jit(solution)/shard_map/enc_backward/pallas_call | solution.py:471
  541.8 6.9 grad_up.1
  553.8 7.0 grad_wide.1
  561.0 3.9 collective-permute-done.43
  570.6 10.0 %grad_tall.1 = f32[4608,384]{1,0:T(8,128)} custom-call(bf16[1,320,4608]{2,1,0:T(8,128)(2,1)} %bitcast.192, bf16[1,320,4608]{2,1,0:T(8,128)(2,1)} %bitcast.58.bl_ref, bf16[2,320,384]{2,1,0:T(8,128)(2,1)} %pad_maximum_fusion.1.ar_ref, bf16[2,320,384]{2,1,0:T(8,128)(2,1)} %copy-done.95), custom_call_target="tpu_custom_call" | custom-call | flops 8800000000 | tf_op jit(solution)/shard_map/grad_tall/pallas_call | solution.py:486
  584.6 3.6 multiply_convert_fusion.2
  589.6 3.0 multiply_convert_fusion
  594.1 3.7 multiply_convert_fusion.1
  605.1 10.0 %collective-permute-done.54 = f32[1,1,1,1,48,384]{5,4,3,2,1,0:T(8,128)} collective-permute-done((f32[1,1,1,1,48,384]{5,4,3,2,1,0:T(8,128)}, f32[1,1,1,1,48,384]{5,4,3,2,1,0:T(8,128)}, u32[]{:S(2)}, u32[]{:S(2)}) %collective-permute-start.54) | collective-permute-done | bytes 73760 | tf_op jit(solution)/shard_map/ppermute | solution.py:530
  615.2 17.3 %collective-permute-done.53 = f32[1,1,1,1,24,1152]{5,4,3,2,1,0:T(8,128)} collective-permute-done((f32[1,1,1,1,24,1152]{5,4,3,2,1,0:T(8,128)}, f32[1,1,1,1,24,1152]{5,4,3,2,1,0:T(8,128)}, u32[]{:S(2)}, u32[]{:S(2)}) %collective-permute-start.53) | collective-permute-done | bytes 110624 | tf_op jit(solution)/shard_map/ppermute | solution.py:530
  634.9 2.7 collective-permute-start.62
  637.6 2.4 multiply_add_fusion.5
  642.8 2.9 multiply_add_fusion.4
  648.4 2.5 maximum_select_fusion.9
  658.2 14.2 %collective-permute-done.59 = f16[2,1,1,96,1536]{4,3,2,1,0:T(8,128)(2,1)} collective-permute-done((f16[2,1,1,96,1536]{4,3,2,1,0:T(8,128)(2,1)}, f16[2,1,1,96,1536]{4,3,2,1,0:T(8,128)(2,1)}, u32[]{:S(2)}, u32[]{:S(2)}) %collective-permute-start.59) | collective-permute-done | bytes 589856 | tf_op jit(solution)/shard_map/ppermute | solution.py:530
  686.7 3.1 collective-permute-done.69
  689.9 3.2 collective-permute-done.68
  698.4 2.6 collective-permute-start.72
  701.8 10.1 %collective-permute-done.74 = f32[1,1,2,1,24,1152]{5,4,2,3,1,0:T(8,128)S(1)} collective-permute-done((f32[1,1,2,1,24,1152]{5,4,2,3,1,0:T(8,128)S(1)}, f32[1,1,2,1,24,1152]{5,4,2,3,1,0:T(8,128)S(1)}, u32[]{:S(2)}, u32[]{:S(2)}) %collective-permute-start.74) | collective-permute-done | bytes 221216 | tf_op jit(solution)/shard_map/ppermute | solution.py:530
  711.9 24.1 %collective-permute-done.72 = f16[1,1,1,96,1536]{4,3,2,1,0:T(8,128)(2,1)S(1)} collective-permute-done((f16[1,1,1,96,1536]{4,3,2,1,0:T(8,128)(2,1)S(1)}, f16[1,1,1,96,1536]{4,3,2,1,0:T(8,128)(2,1)S(1)}, u32[]{:S(2)}, u32[]{:S(2)}) %collective-permute-start.72) | collective-permute-done | bytes 294944 | tf_op jit(solution)/shard_map/ppermute | solution.py:530
  736.0 5.1 collective-permute-done.71
  754.2 2.4 collective-permute-start.77
  758.0 3.0 maximum_select_fusion.2
  762.7 4.2 collective-permute-done.78
  766.8 2.8 collective-permute-done.80
  772.1 3.0 collective-permute-start.82
  775.1 2.5 collective-permute-start.81
  787.5 8.3 fusion.87
  798.5 2.6 fusion.84
  801.1 5.2 collective-permute-done.86
  806.3 2.9 maximum_select_fusion.7
  818.2 18.4 %fusion.80 = (bf16[2304,768]{1,0:T(8,128)(2,1)}, f32[2304,768]{1,0:T(8,128)}, f32[2304,768]{1,0:T(8,128)}, f32[2304,768]{1,0:T(8,128)}) fusion(f32[2304,768]{1,0:T(8,128)} %param.26, f32[]{:T(128)S(6)} %min.3, f32[]{:T(128)S(6)} %div.277, f16[2304,384]{1,0:T(8,128)(2,1)S(1)} %bitcast.138, f16[2304,384]{1,0:T(8,128)(2,1)S(1)} %collective-permute-done.89, ...), kind=kLoop, calls=%fused_computation.314 | loop fusion | flops 38928384 | bytes 49545224 | tf_op jit(solution)/shard_map/convert_element_type | solution.py:887
  839.0 2.7 convert_multiply_fusion
  841.7 24.1 %fusion.78 = (bf16[384,6528]{1,0:T(8,128)(2,1)}, f32[384,6528]{1,0:T(8,128)}, f32[384,6528]{1,0:T(8,128)}, f32[384,6528]{1,0:T(8,128)}) fusion(f32[384,6528]{1,0:T(8,128)} %param.25, f32[]{:T(128)S(6)} %min.3, f32[384,384]{1,0:T(8,128)} %bitcast.163, f32[384,3072]{1,0:T(8,128)} %convert_multiply_fusion, f32[384,768]{1,0:T(8,128)} %convert_multiply_fusion.2, ...), kind=kLoop, calls=%fused_computation.313 | loop fusion | flops 50135040 | bytes 75202560 | tf_op jit(solution)/shard_map/convert_element_type | solution.py:887
  (525 shorter events, 204.3 us)
Async XLA Ops:
  2.7 42.2 %collective-permute-start = (f32[1]{0:T(128)}, f32[1]{0:T(128)}, u32[]{:S(2)}, u32[]{:S(2)}) collective-permute-start(f32[1]{0:T(128)} %bitcast.4), channel_id=1, source_target_pairs={{0,2},{2,0},{4,6},{6,4},{8,10},{10,8},{12,14},{14,12},{16,18},{18,... | collective-permute-start | bytes 20 | tf_op jit(solution)/shard_map/ppermute | solution.py:530
  4.9 44.2 %collective-permute-start.4 = (bf16[1,7296]{1,0:T(2,128)(2,1)S(1)}, bf16[1,7296]{1,0:T(2,128)(2,1)}, u32[]{:S(2)}, u32[]{:S(2)}) collective-permute-start(bf16[1,7296]{1,0:T(2,128)(2,1)S(1)} %reshape.2737), channel_id=1, source_target_pairs={{0,1},{1,0},{2,3},{3,2},{4,5},{5,4},{6,7},{7,6},{8,9},{9,8},{10,11... | collective-permute-start | bytes 43784 | tf_op jit(solution)/shard_map/ppermute | solution.py:694
  9.4 39.7 %collective-permute-start.3 = (bf16[1,1,1,1,288,768]{5,4,3,2,1,0:T(8,128)(2,1)}, bf16[1,1,1,1,288,768]{5,4,3,2,1,0:T(8,128)(2,1)}, u32[]{:S(2)}, u32[]{:S(2)}) collective-permute-start(bf16[1,1,1,1,288,768]{5,4,3,2,1,0:T(8,128)(2,1)} %dynamic-slice_convert_fusion.1), channel_id=1, source_target_pairs={{0,1},{1,0},{2,3},{3,2},{4,5},{5,4},{6,7},{7,6},{8,9},{9,8},{10,11... | collective-permute-start | bytes 1327112 | tf_op jit(solution)/shard_map/ppermute | solution.py:694
  11.7 37.4 %collective-permute-start.2 = (bf16[1,1,1,1,48,6528]{5,4,3,2,1,0:T(8,128)(2,1)}, bf16[1,1,1,1,48,6528]{5,4,3,2,1,0:T(8,128)(2,1)S(1)}, u32[]{:S(2)}, u32[]{:S(2)}) collective-permute-start(bf16[1,1,1,1,48,6528]{5,4,3,2,1,0:T(8,128)(2,1)} %dynamic-slice_convert_fusion), channel_id=1, source_target_pairs={{0,1},{1,0},{2,3},{3,2},{4,5},{5,4},{6,7},{7,6},{8,9},{9,8},{10,11... | collective-permute-start | bytes 1880072 | tf_op jit(solution)/shard_map/ppermute | solution.py:694
  49.7 96.3 %collective-permute-start.15 = (f32[1]{0:T(128)}, f32[1]{0:T(128)}, u32[]{:S(2)}, u32[]{:S(2)}) collective-permute-start(f32[1]{0:T(128)} %add.707), channel_id=1, source_target_pairs={{0,1},{1,0},{2,3},{3,2},{4,5},{5,4},{6,7},{7,6},{8,9},{9,8},{10,11... | collective-permute-start | bytes 20 | tf_op jit(solution)/shard_map/ppermute | solution.py:530
  51.2 19.2 %collective-permute-start.6 = (bf16[1,1,1,1,288,768]{5,4,3,2,1,0:T(8,128)(2,1)}, bf16[1,1,1,1,288,768]{5,4,3,2,1,0:T(8,128)(2,1)S(1)}, u32[]{:S(2)}, u32[]{:S(2)}) collective-permute-start(bf16[1,1,1,1,288,768]{5,4,3,2,1,0:T(8,128)(2,1)} %collective-permute-done.3), channel_id=1, source_target_pairs={{0,8},{2,10},{4,12},{6,14},{8,0},{10,2},{12,4},{14,6},{16,24},{18,... | collective-permute-start | bytes 1327112 | tf_op jit(solution)/shard_map/ppermute | solution.py:530
  53.2 17.3 %collective-permute-start.5 = (bf16[1,1,1,1,48,6528]{5,4,3,2,1,0:T(8,128)(2,1)S(1)}, bf16[1,1,1,1,48,6528]{5,4,3,2,1,0:T(8,128)(2,1)S(1)}, u32[]{:S(2)}, u32[]{:S(2)}) collective-permute-start(bf16[1,1,1,1,48,6528]{5,4,3,2,1,0:T(8,128)(2,1)S(1)} %collective-permute-done.2), channel_id=1, source_target_pairs={{0,4},{2,6},{4,0},{6,2},{8,12},{10,14},{12,8},{14,10},{16,20},{18,... | collective-permute-start | bytes 1880072 | tf_op jit(solution)/shard_map/ppermute | solution.py:530
  70.4 21.4 %collective-permute-start.10 = (bf16[1,1,1,1,96,384]{5,4,3,2,1,0:T(8,128)(2,1)S(1)}, bf16[1,1,1,1,96,384]{5,4,3,2,1,0:T(8,128)(2,1)}, u32[]{:S(2)}, u32[]{:S(2)}) collective-permute-start(bf16[1,1,1,1,96,384]{5,4,3,2,1,0:T(8,128)(2,1)S(1)} %dynamic-slice_convert_fusion.3), channel_id=1, source_target_pairs={{0,1},{1,0},{2,3},{3,2},{4,5},{5,4},{6,7},{7,6},{8,9},{9,8},{10,11... | collective-permute-start | bytes 221192 | tf_op jit(solution)/shard_map/ppermute | solution.py:694
  72.0 19.9 %collective-permute-start.9 = (bf16[1,1,1,1,24,4608]{5,4,3,2,1,0:T(8,128)(2,1)S(1)}, bf16[1,1,1,1,24,4608]{5,4,3,2,1,0:T(8,128)(2,1)}, u32[]{:S(2)}, u32[]{:S(2)}) collective-permute-start(bf16[1,1,1,1,24,4608]{5,4,3,2,1,0:T(8,128)(2,1)S(1)} %copy-done.62), channel_id=1, source_target_pairs={{0,1},{1,0},{2,3},{3,2},{4,5},{5,4},{6,7},{7,6},{8,9},{9,8},{10,11... | collective-permute-start | bytes 663560 | tf_op jit(solution)/shard_map/ppermute | solution.py:694
  74.7 18.6 %collective-permute-start.8 = (bf16[1,1,1,2,288,768]{5,4,3,2,1,0:T(8,128)(2,1)}, bf16[1,1,1,2,288,768]{5,4,3,2,1,0:T(8,128)(2,1)}, u32[]{:S(2)}, u32[]{:S(2)}) collective-permute-start(bf16[1,1,1,2,288,768]{5,4,3,2,1,0:T(8,128)(2,1)} %maximum_select_fusion.16), channel_id=1, source_target_pairs={{0,4},{2,6},{4,0},{6,2},{8,12},{10,14},{12,8},{14,10},{16,20},{18,... | collective-permute-start | bytes 2654216 | tf_op jit(solution)/shard_map/ppermute | solution.py:530
  76.4 26.9 %collective-permute-start.7 = (bf16[1,1,2,1,48,6528]{5,4,3,2,1,0:T(8,128)(2,1)}, bf16[1,1,2,1,48,6528]{5,4,3,2,1,0:T(8,128)(2,1)S(1)}, u32[]{:S(2)}, u32[]{:S(2)}) collective-permute-start(bf16[1,1,2,1,48,6528]{5,4,3,2,1,0:T(8,128)(2,1)} %maximum_select_fusion.10), channel_id=1, source_target_pairs={{0,8},{2,10},{4,12},{6,14},{8,0},{10,2},{12,4},{14,6},{16,24},{18,... | collective-permute-start | bytes 3760136 | tf_op jit(solution)/shard_map/ppermute | solution.py:530
  103.3 17.1 %collective-permute-start.14 = (bf16[1,1,1,1,96,384]{5,4,3,2,1,0:T(8,128)(2,1)}, bf16[1,1,1,1,96,384]{5,4,3,2,1,0:T(8,128)(2,1)S(1)}, u32[]{:S(2)}, u32[]{:S(2)}) collective-permute-start(bf16[1,1,1,1,96,384]{5,4,3,2,1,0:T(8,128)(2,1)} %collective-permute-done.10), channel_id=1, source_target_pairs={{0,8},{2,10},{4,12},{6,14},{8,0},{10,2},{12,4},{14,6},{16,24},{18,... | collective-permute-start | bytes 221192 | tf_op jit(solution)/shard_map/ppermute | solution.py:530
  104.3 16.1 %collective-permute-start.13 = (bf16[1,1,1,1,24,4608]{5,4,3,2,1,0:T(8,128)(2,1)}, bf16[1,1,1,1,24,4608]{5,4,3,2,1,0:T(8,128)(2,1)S(1)}, u32[]{:S(2)}, u32[]{:S(2)}) collective-permute-start(bf16[1,1,1,1,24,4608]{5,4,3,2,1,0:T(8,128)(2,1)} %collective-permute-done.9), channel_id=1, source_target_pairs={{0,4},{2,6},{4,0},{6,2},{8,12},{10,14},{12,8},{14,10},{16,20},{18,... | collective-permute-start | bytes 663560 | tf_op jit(solution)/shard_map/ppermute | solution.py:530
  121.6 24.5 %collective-permute-start.17 = (bf16[1,1,1,2,96,384]{5,4,3,2,1,0:T(8,128)(2,1)S(1)}, bf16[1,1,1,2,96,384]{5,4,3,2,1,0:T(8,128)(2,1)S(1)}, u32[]{:S(2)}, u32[]{:S(2)}) collective-permute-start(bf16[1,1,1,2,96,384]{5,4,3,2,1,0:T(8,128)(2,1)S(1)} %maximum_select_fusion.38), channel_id=1, source_target_pairs={{0,4},{2,6},{4,0},{6,2},{8,12},{10,14},{12,8},{14,10},{16,20},{18,... | collective-permute-start | bytes 442376 | tf_op jit(solution)/shard_map/ppermute | solution.py:530
  123.3 22.8 %collective-permute-start.16 = (bf16[1,1,2,1,24,4608]{5,4,3,2,1,0:T(8,128)(2,1)S(1)}, bf16[1,1,2,1,24,4608]{5,4,3,2,1,0:T(8,128)(2,1)S(1)}, u32[]{:S(2)}, u32[]{:S(2)}) collective-permute-start(bf16[1,1,2,1,24,4608]{5,4,3,2,1,0:T(8,128)(2,1)S(1)} %maximum_select_fusion.29), channel_id=1, source_target_pairs={{0,8},{2,10},{4,12},{6,14},{8,0},{10,2},{12,4},{14,6},{16,24},{18,... | collective-permute-start | bytes 1327112 | tf_op jit(solution)/shard_map/ppermute | solution.py:530
  147.9 92.9 %collective-permute-start.24 = (bf16[320,768]{1,0:T(8,128)(2,1)}, bf16[320,768]{1,0:T(8,128)(2,1)}, u32[]{:S(2)}, u32[]{:S(2)}) collective-permute-start(bf16[320,768]{1,0:T(8,128)(2,1)} %get-tuple-element.287), channel_id=1, source_target_pairs={{0,2},{2,0},{4,6},{6,4},{8,10},{10,8},{12,14},{14,12},{16,18},{18,... | collective-permute-start | bytes 1474568 | tf_op jit(solution)/shard_map/ppermute | solution.py:530
  148.0 92.8 %collective-permute-start.23 = (bf16[2,320,768]{2,1,0:T(8,128)(2,1)}, bf16[2,320,768]{2,1,0:T(8,128)(2,1)}, u32[]{:S(2)}, u32[]{:S(2)}) collective-permute-start(bf16[2,320,768]{2,1,0:T(8,128)(2,1)} %get-tuple-element.286.al_ref), channel_id=1, source_target_pairs={{0,2},{2,0},{4,6},{6,4},{8,10},{10,8},{12,14},{14,12},{16,18},{18,... | collective-permute-start | bytes 2949128 | tf_op jit(solution)/shard_map/ppermute | solution.py:530
  149.1 19.0 %collective-permute-start.20 = (f32[1]{0:T(128)}, f32[1]{0:T(128)}, u32[]{:S(2)}, u32[]{:S(2)}) collective-permute-start(f32[1]{0:T(128)} %add.709), channel_id=1, source_target_pairs={{0,8},{2,10},{4,12},{6,14},{8,0},{10,2},{12,4},{14,6},{16,24},{18,... | collective-permute-start | bytes 20 | tf_op jit(solution)/shard_map/ppermute | solution.py:530
  154.5 86.4 %collective-permute-start.22 = (bf16[320,4608]{1,0:T(8,128)(2,1)}, bf16[320,4608]{1,0:T(8,128)(2,1)}, u32[]{:S(2)}, u32[]{:S(2)}) collective-permute-start(bf16[320,4608]{1,0:T(8,128)(2,1)} %get-tuple-element.285), channel_id=1, source_target_pairs={{0,2},{2,0},{4,6},{6,4},{8,10},{10,8},{12,14},{14,12},{16,18},{18,... | collective-permute-start | bytes 8847368 | tf_op jit(solution)/shard_map/ppermute | solution.py:530
  168.8 72.0 %collective-permute-start.21 = (f32[1]{0:T(128)}, f32[1]{0:T(128)}, u32[]{:S(2)}, u32[]{:S(2)}) collective-permute-start(f32[1]{0:T(128)} %add.710), channel_id=1, source_target_pairs={{0,16},{2,18},{4,20},{6,22},{8,24},{10,26},{12,28},{14,30},{16,0},... | collective-permute-start | bytes 20 | tf_op jit(solution)/shard_map/ppermute | solution.py:530
  307.7 25.2 %collective-permute-start.25 = (f32[2,1,2,2,24,3456]{5,4,3,2,1,0:T(8,128)S(1)}, f32[2,1,2,2,24,3456]{5,4,3,2,1,0:T(8,128)}, u32[]{:S(2)}, u32[]{:S(2)}) collective-permute-start(f32[2,1,2,2,24,3456]{5,4,3,2,1,0:T(8,128)S(1)} %constant_dynamic-slice_fusion.19), channel_id=1, source_target_pairs={{0,2},{2,0},{4,6},{6,4},{8,10},{10,8},{12,14},{14,12},{16,18},{18,... | collective-permute-start | bytes 7962632 | tf_op jit(solution)/shard_map/ppermute | solution.py:530
  311.3 21.6 %collective-permute-start.26 = (f32[2,1,2,2,96,384]{5,4,3,2,1,0:T(8,128)}, f32[2,1,2,2,96,384]{5,4,3,2,1,0:T(8,128)}, u32[]{:S(2)}, u32[]{:S(2)}) collective-permute-start(f32[2,1,2,2,96,384]{5,4,3,2,1,0:T(8,128)} %constant_dynamic-slice_fusion.18), channel_id=1, source_target_pairs={{0,2},{2,0},{4,6},{6,4},{8,10},{10,8},{12,14},{14,12},{16,18},{18,... | collective-permute-start | bytes 3538952 | tf_op jit(solution)/shard_map/ppermute | solution.py:530
  338.3 23.0 %collective-permute-start.28 = (f32[2,1,2,1,96,384]{5,4,3,2,1,0:T(8,128)}, f32[2,1,2,1,96,384]{5,4,3,2,1,0:T(8,128)}, u32[]{:S(2)}, u32[]{:S(2)}) collective-permute-start(f32[2,1,2,1,96,384]{5,4,3,2,1,0:T(8,128)} %constant_dynamic-slice_fusion.16), channel_id=1, source_target_pairs={{0,8},{2,10},{4,12},{6,14},{8,0},{10,2},{12,4},{14,6},{16,24},{18,... | collective-permute-start | bytes 1769480 | tf_op jit(solution)/shard_map/ppermute | solution.py:530
  340.6 31.1 %collective-permute-start.27 = (f32[2,1,1,2,24,3456]{5,4,3,2,1,0:T(8,128)}, f32[2,1,1,2,24,3456]{5,4,3,2,1,0:T(8,128)}, u32[]{:S(2)}, u32[]{:S(2)}) collective-permute-start(f32[2,1,1,2,24,3456]{5,4,3,2,1,0:T(8,128)} %constant_dynamic-slice_fusion.17), channel_id=1, source_target_pairs={{0,4},{2,6},{4,0},{6,2},{8,12},{10,14},{12,8},{14,10},{16,20},{18,... | collective-permute-start | bytes 3981320 | tf_op jit(solution)/shard_map/ppermute | solution.py:530
  374.6 36.8 %collective-permute-start.30 = (f32[1,1,2,1,96,384]{5,4,3,2,1,0:T(8,128)S(1)}, f32[1,1,2,1,96,384]{5,4,3,2,1,0:T(8,128)S(1)}, u32[]{:S(2)}, u32[]{:S(2)}) collective-permute-start(f32[1,1,2,1,96,384]{5,4,3,2,1,0:T(8,128)S(1)} %constant_dynamic-slice_fusion.14), channel_id=1, source_target_pairs={{0,1},{1,0},{2,3},{3,2},{4,5},{5,4},{6,7},{7,6},{8,9},{9,8},{10,11... | collective-permute-start | bytes 884744 | tf_op jit(solution)/shard_map/ppermute | solution.py:530
  376.2 35.2 %collective-permute-start.29 = (f32[2,1,1,1,24,3456]{5,4,3,2,1,0:T(8,128)S(1)}, f32[2,1,1,1,24,3456]{5,4,3,2,1,0:T(8,128)S(1)}, u32[]{:S(2)}, u32[]{:S(2)}) collective-permute-start(f32[2,1,1,1,24,3456]{5,4,3,2,1,0:T(8,128)S(1)} %constant_dynamic-slice_fusion.15), channel_id=1, source_target_pairs={{0,8},{2,10},{4,12},{6,14},{8,0},{10,2},{12,4},{14,6},{16,24},{18,... | collective-permute-start | bytes 1990664 | tf_op jit(solution)/shard_map/ppermute | solution.py:530
  411.5 21.4 %collective-permute-start.32 = (f32[1,1,1,1,96,384]{5,4,3,2,1,0:T(8,128)S(1)}, f32[1,1,1,1,96,384]{5,4,3,2,1,0:T(8,128)S(1)}, u32[]{:S(2)}, u32[]{:S(2)}) collective-permute-start(f32[1,1,1,1,96,384]{5,4,3,2,1,0:T(8,128)S(1)} %constant_dynamic-slice_fusion.12), channel_id=1, source_target_pairs={{0,4},{2,6},{4,0},{6,2},{8,12},{10,14},{12,8},{14,10},{16,20},{18,... | collective-permute-start | bytes 442376 | tf_op jit(solution)/shard_map/ppermute | solution.py:530
  413.1 19.8 %collective-permute-start.31 = (f32[1,1,1,1,24,3456]{5,4,3,2,1,0:T(8,128)S(1)}, f32[1,1,1,1,24,3456]{5,4,3,2,1,0:T(8,128)S(1)}, u32[]{:S(2)}, u32[]{:S(2)}) collective-permute-start(f32[1,1,1,1,24,3456]{5,4,3,2,1,0:T(8,128)S(1)} %constant_dynamic-slice_fusion.13), channel_id=1, source_target_pairs={{0,1},{1,0},{2,3},{3,2},{4,5},{5,4},{6,7},{7,6},{8,9},{9,8},{10,11... | collective-permute-start | bytes 995336 | tf_op jit(solution)/shard_map/ppermute | solution.py:530
  433.0 22.3 %collective-permute-start.34 = (f32[1,1,1,1,96,384]{5,4,3,2,1,0:T(8,128)S(1)}, f32[1,1,1,1,96,384]{5,4,3,2,1,0:T(8,128)S(1)}, u32[]{:S(2)}, u32[]{:S(2)}) collective-permute-start(f32[1,1,1,1,96,384]{5,4,3,2,1,0:T(8,128)S(1)} %dynamic-slice_add_fusion.13), channel_id=1, source_target_pairs={{0,16},{2,18},{4,20},{6,22},{8,24},{10,26},{12,28},{14,30},{16,0},... | collective-permute-start | bytes 442376 | tf_op jit(solution)/shard_map/ppermute | solution.py:530
  433.5 21.9 %collective-permute-start.33 = (f32[1,1,1,1,24,3456]{5,4,3,2,1,0:T(8,128)S(1)}, f32[1,1,1,1,24,3456]{5,4,3,2,1,0:T(8,128)S(1)}, u32[]{:S(2)}, u32[]{:S(2)}) collective-permute-start(f32[1,1,1,1,24,3456]{5,4,3,2,1,0:T(8,128)S(1)} %dynamic-slice_add_fusion.8), channel_id=1, source_target_pairs={{0,16},{2,18},{4,20},{6,22},{8,24},{10,26},{12,28},{14,30},{16,0},... | collective-permute-start | bytes 995336 | tf_op jit(solution)/shard_map/ppermute | solution.py:530
  521.1 15.9 %collective-permute-start.56 = (f32[1,1,1,1,96,384]{5,4,3,2,1,0:T(8,128)S(1)}, f32[1,1,1,1,96,384]{5,4,3,2,1,0:T(8,128)S(1)}, u32[]{:S(2)}, u32[]{:S(2)}) collective-permute-start(f32[1,1,1,1,96,384]{5,4,3,2,1,0:T(8,128)S(1)} %get-tuple-element.488), channel_id=1, source_target_pairs={{0,8},{2,10},{4,12},{6,14},{8,0},{10,2},{12,4},{14,6},{16,24},{18,... | collective-permute-start | bytes 442376 | tf_op jit(solution)/shard_map/ppermute | solution.py:530
  522.2 14.9 %collective-permute-start.55 = (f32[1,1,1,1,24,3456]{5,4,2,3,1,0:T(8,128)S(1)}, f32[1,1,1,1,24,3456]{5,4,2,3,1,0:T(8,128)S(1)}, u32[]{:S(2)}, u32[]{:S(2)}) collective-permute-start(f32[1,1,1,1,24,3456]{5,4,2,3,1,0:T(8,128)S(1)} %get-tuple-element.498), channel_id=1, source_target_pairs={{0,4},{2,6},{4,0},{6,2},{8,12},{10,14},{12,8},{14,10},{16,20},{18,... | collective-permute-start | bytes 995336 | tf_op jit(solution)/shard_map/ppermute | solution.py:530
  565.0 15.6 %collective-permute-start.47 = (f32[1,14720]{1,0:T(1,128)S(1)}, f32[1,14720]{1,0:T(1,128)S(1)}, u32[]{:S(2)}, u32[]{:S(2)}) collective-permute-start(f32[1,14720]{1,0:T(1,128)S(1)} %maximum_select_fusion.43), channel_id=1, source_target_pairs={{0,24},{2,26},{4,28},{6,30},{8,16},{10,18},{12,20},{14,22},{16,8},... | collective-permute-start | bytes 176648 | tf_op jit(solution)/shard_map/ppermute | solution.py:530
  565.9 15.4 %collective-permute-start.46 = (f32[1,14720]{1,0:T(1,128)S(1)}, f32[1,14720]{1,0:T(1,128)S(1)}, u32[]{:S(2)}, u32[]{:S(2)}) collective-permute-start(f32[1,14720]{1,0:T(1,128)S(1)} %maximum_select_fusion.43), channel_id=1, source_target_pairs={{0,16},{2,18},{4,20},{6,22},{8,24},{10,26},{12,28},{14,30},{16,0},... | collective-permute-start | bytes 176648 | tf_op jit(solution)/shard_map/ppermute | solution.py:530
  567.6 15.6 %collective-permute-start.45 = (f32[1,14720]{1,0:T(1,128)S(1)}, f32[1,14720]{1,0:T(1,128)S(1)}, u32[]{:S(2)}, u32[]{:S(2)}) collective-permute-start(f32[1,14720]{1,0:T(1,128)S(1)} %maximum_select_fusion.43), channel_id=1, source_target_pairs={{0,8},{2,10},{4,12},{6,14},{8,0},{10,2},{12,4},{14,6},{16,24},{18,... | collective-permute-start | bytes 176648 | tf_op jit(solution)/shard_map/ppermute | solution.py:530
  569.6 13.6 %collective-permute-start.49 = (f32[1,1,2,1,48,384]{5,4,3,2,1,0:T(8,128)S(1)}, f32[1,1,2,1,48,384]{5,4,3,2,1,0:T(8,128)S(1)}, u32[]{:S(2)}, u32[]{:S(2)}) collective-permute-start(f32[1,1,2,1,48,384]{5,4,3,2,1,0:T(8,128)S(1)} %constant_dynamic-slice_fusion.2), channel_id=1, source_target_pairs={{0,1},{1,0},{2,3},{3,2},{4,5},{5,4},{6,7},{7,6},{8,9},{9,8},{10,11... | collective-permute-start | bytes 442376 | tf_op jit(solution)/shard_map/ppermute | solution.py:530
  570.4 12.8 %collective-permute-start.48 = (f32[2,1,1,1,24,1152]{5,4,3,2,1,0:T(8,128)S(1)}, f32[2,1,1,1,24,1152]{5,4,3,2,1,0:T(8,128)S(1)}, u32[]{:S(2)}, u32[]{:S(2)}) collective-permute-start(f32[2,1,1,1,24,1152]{5,4,3,2,1,0:T(8,128)S(1)} %constant_dynamic-slice_fusion.3), channel_id=1, source_target_pairs={{0,8},{2,10},{4,12},{6,14},{8,0},{10,2},{12,4},{14,6},{16,24},{18,... | collective-permute-start | bytes 663560 | tf_op jit(solution)/shard_map/ppermute | solution.py:530
  580.6 19.7 %collective-permute-start.58 = (f32[1,1,1,2,96,384]{5,4,3,2,1,0:T(8,128)}, f32[1,1,1,2,96,384]{5,4,3,2,1,0:T(8,128)S(1)}, u32[]{:S(2)}, u32[]{:S(2)}) collective-permute-start(f32[1,1,1,2,96,384]{5,4,3,2,1,0:T(8,128)} %maximum_select_fusion.33), channel_id=1, source_target_pairs={{0,4},{2,6},{4,0},{6,2},{8,12},{10,14},{12,8},{14,10},{16,20},{18,... | collective-permute-start | bytes 884744 | tf_op jit(solution)/shard_map/ppermute | solution.py:530
  581.3 20.3 %collective-permute-start.57 = (f32[1,1,2,1,24,3456]{5,4,2,3,1,0:T(8,128)}, f32[1,1,2,1,24,3456]{5,4,2,3,1,0:T(8,128)}, u32[]{:S(2)}, u32[]{:S(2)}) collective-permute-start(f32[1,1,2,1,24,3456]{5,4,2,3,1,0:T(8,128)} %maximum_select_fusion.21), channel_id=1, source_target_pairs={{0,8},{2,10},{4,12},{6,14},{8,0},{10,2},{12,4},{14,6},{16,24},{18,... | collective-permute-start | bytes 1990664 | tf_op jit(solution)/shard_map/ppermute | solution.py:530
  588.2 44.2 %collective-permute-start.50 = (f16[2,1,2,96,1536]{4,3,2,1,0:T(8,128)(2,1)}, f16[2,1,2,96,1536]{4,3,2,1,0:T(8,128)(2,1)}, u32[]{:S(2)}, u32[]{:S(2)}) collective-permute-start(f16[2,1,2,96,1536]{4,3,2,1,0:T(8,128)(2,1)} %multiply_convert_fusion.2), channel_id=1, source_target_pairs={{0,4},{2,6},{4,0},{6,2},{8,12},{10,14},{12,8},{14,10},{16,20},{18,... | collective-permute-start | bytes 3538952 | tf_op jit(solution)/shard_map/ppermute | solution.py:530
  592.6 39.8 %collective-permute-start.52 = (f16[1,2,2,576,384]{4,3,2,1,0:T(8,128)(2,1)S(1)}, f16[1,2,2,576,384]{4,3,2,1,0:T(8,128)(2,1)S(1)}, u32[]{:S(2)}, u32[]{:S(2)}) collective-permute-start(f16[1,2,2,576,384]{4,3,2,1,0:T(8,128)(2,1)S(1)} %multiply_convert_fusion), channel_id=1, source_target_pairs={{0,1},{1,0},{2,3},{3,2},{4,5},{5,4},{6,7},{7,6},{8,9},{9,8},{10,11... | collective-permute-start | bytes 5308424 | tf_op jit(solution)/shard_map/ppermute | solution.py:530
  597.7 34.7 %collective-permute-start.51 = (f16[2,2,1,96,1536]{4,3,2,1,0:T(8,128)(2,1)}, f16[2,2,1,96,1536]{4,3,2,1,0:T(8,128)(2,1)}, u32[]{:S(2)}, u32[]{:S(2)}) collective-permute-start(f16[2,2,1,96,1536]{4,3,2,1,0:T(8,128)(2,1)} %multiply_convert_fusion.1), channel_id=1, source_target_pairs={{0,8},{2,10},{4,12},{6,14},{8,0},{10,2},{12,4},{14,6},{16,24},{18,... | collective-permute-start | bytes 3538952 | tf_op jit(solution)/shard_map/ppermute | solution.py:530
  601.0 14.2 %collective-permute-start.54 = (f32[1,1,1,1,48,384]{5,4,3,2,1,0:T(8,128)}, f32[1,1,1,1,48,384]{5,4,3,2,1,0:T(8,128)}, u32[]{:S(2)}, u32[]{:S(2)}) collective-permute-start(f32[1,1,1,1,48,384]{5,4,3,2,1,0:T(8,128)} %constant_dynamic-slice_fusion), channel_id=1, source_target_pairs={{0,4},{2,6},{4,0},{6,2},{8,12},{10,14},{12,8},{14,10},{16,20},{18,... | collective-permute-start | bytes 221192 | tf_op jit(solution)/shard_map/ppermute | solution.py:530
  601.6 30.8 %collective-permute-start.53 = (f32[1,1,1,1,24,1152]{5,4,3,2,1,0:T(8,128)}, f32[1,1,1,1,24,1152]{5,4,3,2,1,0:T(8,128)}, u32[]{:S(2)}, u32[]{:S(2)}) collective-permute-start(f32[1,1,1,1,24,1152]{5,4,3,2,1,0:T(8,128)} %constant_dynamic-slice_fusion.1), channel_id=1, source_target_pairs={{0,1},{1,0},{2,3},{3,2},{4,5},{5,4},{6,7},{7,6},{8,9},{9,8},{10,11... | collective-permute-start | bytes 331784 | tf_op jit(solution)/shard_map/ppermute | solution.py:530
  634.6 21.8 %collective-permute-start.63 = (f32[1,1,1,1,48,384]{5,4,3,2,1,0:T(8,128)S(1)}, f32[1,1,1,1,48,384]{5,4,3,2,1,0:T(8,128)S(1)}, u32[]{:S(2)}, u32[]{:S(2)}) collective-permute-start(f32[1,1,1,1,48,384]{5,4,3,2,1,0:T(8,128)S(1)} %dynamic-slice_add_fusion.15), channel_id=1, source_target_pairs={{0,16},{2,18},{4,20},{6,22},{8,24},{10,26},{12,28},{14,30},{16,0},... | collective-permute-start | bytes 221192 | tf_op jit(solution)/shard_map/ppermute | solution.py:530
  634.9 21.8 %collective-permute-start.62 = (f32[1,1,1,1,24,1152]{5,4,3,2,1,0:T(8,128)S(1)}, f32[1,1,1,1,24,1152]{5,4,3,2,1,0:T(8,128)S(1)}, u32[]{:S(2)}, u32[]{:S(2)}) collective-permute-start(f32[1,1,1,1,24,1152]{5,4,3,2,1,0:T(8,128)S(1)} %dynamic-slice_add_fusion.14), channel_id=1, source_target_pairs={{0,16},{2,18},{4,20},{6,22},{8,24},{10,26},{12,28},{14,30},{16,0},... | collective-permute-start | bytes 331784 | tf_op jit(solution)/shard_map/ppermute | solution.py:530
  641.8 16.4 %collective-permute-start.60 = (f16[1,2,1,96,1536]{4,3,2,1,0:T(8,128)(2,1)}, f16[1,2,1,96,1536]{4,3,2,1,0:T(8,128)(2,1)}, u32[]{:S(2)}, u32[]{:S(2)}) collective-permute-start(f16[1,2,1,96,1536]{4,3,2,1,0:T(8,128)(2,1)} %multiply_convert_fusion.4), channel_id=1, source_target_pairs={{0,1},{1,0},{2,3},{3,2},{4,5},{5,4},{6,7},{7,6},{8,9},{9,8},{10,11... | collective-permute-start | bytes 1769480 | tf_op jit(solution)/shard_map/ppermute | solution.py:530
  647.5 24.9 %collective-permute-start.61 = (f16[1,1,2,576,384]{4,3,2,1,0:T(8,128)(2,1)}, f16[1,1,2,576,384]{4,3,2,1,0:T(8,128)(2,1)}, u32[]{:S(2)}, u32[]{:S(2)}) collective-permute-start(f16[1,1,2,576,384]{4,3,2,1,0:T(8,128)(2,1)} %multiply_convert_fusion.3), channel_id=1, source_target_pairs={{0,4},{2,6},{4,0},{6,2},{8,12},{10,14},{12,8},{14,10},{16,20},{18,... | collective-permute-start | bytes 2654216 | tf_op jit(solution)/shard_map/ppermute | solution.py:530
  650.9 21.5 %collective-permute-start.64 = (f32[1,1,2,2,24,3456]{5,4,2,3,1,0:T(8,128)}, f32[1,1,2,2,24,3456]{5,4,2,3,1,0:T(8,128)}, u32[]{:S(2)}, u32[]{:S(2)}) collective-permute-start(f32[1,1,2,2,24,3456]{5,4,2,3,1,0:T(8,128)} %maximum_select_fusion.9), channel_id=1, source_target_pairs={{0,2},{2,0},{4,6},{6,4},{8,10},{10,8},{12,14},{14,12},{16,18},{18,... | collective-permute-start | bytes 3981320 | tf_op jit(solution)/shard_map/ppermute | solution.py:530
  656.4 16.0 %collective-permute-start.59 = (f16[2,1,1,96,1536]{4,3,2,1,0:T(8,128)(2,1)}, f16[2,1,1,96,1536]{4,3,2,1,0:T(8,128)(2,1)}, u32[]{:S(2)}, u32[]{:S(2)}) collective-permute-start(f16[2,1,1,96,1536]{4,3,2,1,0:T(8,128)(2,1)} %multiply_convert_fusion.5), channel_id=1, source_target_pairs={{0,8},{2,10},{4,12},{6,14},{8,0},{10,2},{12,4},{14,6},{16,24},{18,... | collective-permute-start | bytes 1769480 | tf_op jit(solution)/shard_map/ppermute | solution.py:530
  657.7 14.7 %collective-permute-start.65 = (f32[1,1,2,2,96,384]{5,4,3,2,1,0:T(8,128)}, f32[1,1,2,2,96,384]{5,4,3,2,1,0:T(8,128)}, u32[]{:S(2)}, u32[]{:S(2)}) collective-permute-start(f32[1,1,2,2,96,384]{5,4,3,2,1,0:T(8,128)} %maximum_select_fusion.24), channel_id=1, source_target_pairs={{0,2},{2,0},{4,6},{6,4},{8,10},{10,8},{12,14},{14,12},{16,18},{18,... | collective-permute-start | bytes 1769480 | tf_op jit(solution)/shard_map/ppermute | solution.py:530
  695.5 45.7 %collective-permute-start.73 = (f16[1,1,1,576,384]{4,3,2,1,0:T(8,128)(2,1)S(1)}, f16[1,1,1,576,384]{4,3,2,1,0:T(8,128)(2,1)S(1)}, u32[]{:S(2)}, u32[]{:S(2)}) collective-permute-start(f16[1,1,1,576,384]{4,3,2,1,0:T(8,128)(2,1)S(1)} %multiply_convert_fusion.7), channel_id=1, source_target_pairs={{0,16},{2,18},{4,20},{6,22},{8,24},{10,26},{12,28},{14,30},{16,0},... | collective-permute-start | bytes 1327112 | tf_op jit(solution)/shard_map/ppermute | solution.py:530
  697.5 14.4 %collective-permute-start.74 = (f32[1,1,2,1,24,1152]{5,4,2,3,1,0:T(8,128)S(1)}, f32[1,1,2,1,24,1152]{5,4,2,3,1,0:T(8,128)S(1)}, u32[]{:S(2)}, u32[]{:S(2)}) collective-permute-start(f32[1,1,2,1,24,1152]{5,4,2,3,1,0:T(8,128)S(1)} %maximum_select_fusion.36), channel_id=1, source_target_pairs={{0,8},{2,10},{4,12},{6,14},{8,0},{10,2},{12,4},{14,6},{16,24},{18,... | collective-permute-start | bytes 663560 | tf_op jit(solution)/shard_map/ppermute | solution.py:530
  698.4 37.6 %collective-permute-start.72 = (f16[1,1,1,96,1536]{4,3,2,1,0:T(8,128)(2,1)S(1)}, f16[1,1,1,96,1536]{4,3,2,1,0:T(8,128)(2,1)S(1)}, u32[]{:S(2)}, u32[]{:S(2)}) collective-permute-start(f16[1,1,1,96,1536]{4,3,2,1,0:T(8,128)(2,1)S(1)} %multiply_convert_fusion.11), channel_id=1, source_target_pairs={{0,16},{2,18},{4,20},{6,22},{8,24},{10,26},{12,28},{14,30},{16,0},... | collective-permute-start | bytes 884744 | tf_op jit(solution)/shard_map/ppermute | solution.py:530
  701.1 40.0 %collective-permute-start.71 = (f16[1,1,1,96,1536]{4,3,2,1,0:T(8,128)(2,1)S(1)}, f16[1,1,1,96,1536]{4,3,2,1,0:T(8,128)(2,1)S(1)}, u32[]{:S(2)}, u32[]{:S(2)}) collective-permute-start(f16[1,1,1,96,1536]{4,3,2,1,0:T(8,128)(2,1)S(1)} %multiply_convert_fusion.12), channel_id=1, source_target_pairs={{0,16},{2,18},{4,20},{6,22},{8,24},{10,26},{12,28},{14,30},{16,0},... | collective-permute-start | bytes 884744 | tf_op jit(solution)/shard_map/ppermute | solution.py:530
  750.9 26.7 %collective-permute-start.85 = (f32[1,1,2,2,48,384]{5,4,3,2,1,0:T(8,128)S(1)}, f32[1,1,2,2,48,384]{5,4,3,2,1,0:T(8,128)S(1)}, u32[]{:S(2)}, u32[]{:S(2)}) collective-permute-start(f32[1,1,2,2,48,384]{5,4,3,2,1,0:T(8,128)S(1)} %maximum_select_fusion.35), channel_id=1, source_target_pairs={{0,2},{2,0},{4,6},{6,4},{8,10},{10,8},{12,14},{14,12},{16,18},{18,... | collective-permute-start | bytes 884744 | tf_op jit(solution)/shard_map/ppermute | solution.py:530
  752.3 14.5 %collective-permute-start.78 = (f16[1,1,1,96,1536]{4,3,2,1,0:T(8,128)(2,1)S(1)}, f16[1,1,1,96,1536]{4,3,2,1,0:T(8,128)(2,1)S(1)}, u32[]{:S(2)}, u32[]{:S(2)}) collective-permute-start(f16[1,1,1,96,1536]{4,3,2,1,0:T(8,128)(2,1)S(1)} %get-tuple-element.502), channel_id=1, source_target_pairs={{0,4},{2,6},{4,0},{6,2},{8,12},{10,14},{12,8},{14,10},{16,20},{18,... | collective-permute-start | bytes 884744 | tf_op jit(solution)/shard_map/ppermute | solution.py:530
  753.6 24.1 %collective-permute-start.84 = (f32[1,1,2,2,24,1152]{5,4,2,3,1,0:T(8,128)S(1)}, f32[1,1,2,2,24,1152]{5,4,2,3,1,0:T(8,128)S(1)}, u32[]{:S(2)}, u32[]{:S(2)}) collective-permute-start(f32[1,1,2,2,24,1152]{5,4,2,3,1,0:T(8,128)S(1)} %maximum_select_fusion.31), channel_id=1, source_target_pairs={{0,2},{2,0},{4,6},{6,4},{8,10},{10,8},{12,14},{14,12},{16,18},{18,... | collective-permute-start | bytes 1327112 | tf_op jit(solution)/shard_map/ppermute | solution.py:530
  770.2 13.8 %collective-permute-start.83 = (f32[1]{0:T(128)}, f32[1]{0:T(128)}, u32[]{:S(2)}, u32[]{:S(2)}) collective-permute-start(f32[1]{0:T(128)} %add.769), channel_id=1, source_target_pairs={{0,12},{2,14},{4,8},{6,10},{8,4},{10,6},{12,0},{14,2},{16,28},{18,... | collective-permute-start | bytes 20 | tf_op jit(solution)/shard_map/ppermute | solution.py:530
  782.0 19.1 %collective-permute-start.87 = (f16[1,2,1,96,1536]{4,3,2,1,0:T(8,128)(2,1)}, f16[1,2,1,96,1536]{4,3,2,1,0:T(8,128)(2,1)}, u32[]{:S(2)}, u32[]{:S(2)}) collective-permute-start(f16[1,2,1,96,1536]{4,3,2,1,0:T(8,128)(2,1)} %maximum_select_fusion.26), channel_id=1, source_target_pairs={{0,8},{2,10},{4,12},{6,14},{8,0},{10,2},{12,4},{14,6},{16,24},{18,... | collective-permute-start | bytes 1769480 | tf_op jit(solution)/shard_map/ppermute | solution.py:530
  782.3 24.0 %collective-permute-start.86 = (f16[1,2,1,96,1536]{4,3,2,1,0:T(8,128)(2,1)}, f16[1,2,1,96,1536]{4,3,2,1,0:T(8,128)(2,1)}, u32[]{:S(2)}, u32[]{:S(2)}) collective-permute-start(f16[1,2,1,96,1536]{4,3,2,1,0:T(8,128)(2,1)} %maximum_select_fusion.25), channel_id=1, source_target_pairs={{0,8},{2,10},{4,12},{6,14},{8,0},{10,2},{12,4},{14,6},{16,24},{18,... | collective-permute-start | bytes 1769480 | tf_op jit(solution)/shard_map/ppermute | solution.py:530
  784.0 22.3 %collective-permute-start.88 = (f16[1,1,2,576,384]{4,3,2,1,0:T(8,128)(2,1)}, f16[1,1,2,576,384]{4,3,2,1,0:T(8,128)(2,1)}, u32[]{:S(2)}, u32[]{:S(2)}) collective-permute-start(f16[1,1,2,576,384]{4,3,2,1,0:T(8,128)(2,1)} %maximum_select_fusion.20), channel_id=1, source_target_pairs={{0,4},{2,6},{4,0},{6,2},{8,12},{10,14},{12,8},{14,10},{16,20},{18,... | collective-permute-start | bytes 2654216 | tf_op jit(solution)/shard_map/ppermute | solution.py:530
  815.4 21.2 %collective-permute-start.90 = (f16[384,1536]{1,0:T(8,128)(2,1)S(1)}, f16[384,1536]{1,0:T(8,128)(2,1)S(1)}, u32[]{:S(2)}, u32[]{:S(2)}) collective-permute-start(f16[384,1536]{1,0:T(8,128)(2,1)S(1)} %bitcast.151), channel_id=1, source_target_pairs={{0,2},{2,0},{4,6},{6,4},{8,10},{10,8},{12,14},{14,12},{16,18},{18,... | collective-permute-start | bytes 3538952 | tf_op jit(solution)/shard_map/ppermute | solution.py:530
  818.1 18.5 %collective-permute-start.91 = (f16[384,1536]{1,0:T(8,128)(2,1)S(1)}, f16[384,1536]{1,0:T(8,128)(2,1)S(1)}, u32[]{:S(2)}, u32[]{:S(2)}) collective-permute-start(f16[384,1536]{1,0:T(8,128)(2,1)S(1)} %bitcast.148), channel_id=1, source_target_pairs={{0,2},{2,0},{4,6},{6,4},{8,10},{10,8},{12,14},{14,12},{16,18},{18,... | collective-permute-start | bytes 3538952 | tf_op jit(solution)/shard_map/ppermute | solution.py:530
  (129 other events, 922.2 us)
